TPU v7x, 32 devices: a whole 2x2x4 slice. The times are simulated.
32 devices in a mesh: wide: 8 (over z, x), head: 4 (over y, core).
Axes of the slice: x: 2, y: 2, z: 4, core: 2. Of those that a mesh axis runs over, the one named last changes fastest.
Arguments:
- hidden_in: bfloat16 [2048, 2048], P('wide'), may hold values from -6 to 6
- out_cotangent: bfloat16 [2048, 2048], P('wide'), may hold values from -6 to 6
- doc_lengths: int32 [8], replicated, may hold values from 1 to 1024, 2048 in all
- query_weight: bfloat16 [2048, 2048], P('wide', 'head'), may hold values from -0.125 to 0.125
- key_matrix: bfloat16 [2048, 1024], P('wide', 'head'), may hold values from -0.125 to 0.125
- value_matrix: bfloat16 [2048, 1024], P('wide', 'head'), may hold values from -0.125 to 0.125
- gate_weight: bfloat16 [2048, 2048], P('wide', 'head'), may hold values from -0.125 to 0.125
- out_weight: bfloat16 [2048, 2048], P('wide', 'head'), may hold values from -6 to 6
- ffn_gate_weight: bfloat16 [2048, 6144], P('wide', 'head'), may hold values from -0.125 to 0.125
- ffn_up_weight: bfloat16 [2048, 6144], P('wide', 'head'), may hold values from -0.125 to 0.125
- ffn_down_weight: bfloat16 [2048, 6144], P('wide', 'head'), may hold values from -0.078125 to 0.078125
- attn_gain: float32 [2048], replicated, may hold values from 0.5 to 2
- ffn_gain: float32 [2048], replicated, may hold values from 0.5 to 2
- query_gain: float32 [128], replicated, may hold values from 0.5 to 2
- key_gain: float32 [128], replicated, may hold values from 0.5 to 2
Outputs:
- layer_out: bfloat16 [2048, 2048], P('wide')
- input_grad: bfloat16 [2048, 2048], P('wide')
- query_weight_grad: float32 [2048, 2048], P('wide', 'head')
- key_weight_grad: float32 [2048, 1024], P('wide', 'head')
- value_weight_grad: float32 [2048, 1024], P('wide', 'head')
- gate_weight_grad: float32 [2048, 2048], P('wide', 'head')
- out_weight_grad: float32 [2048, 2048], P('wide', 'head')
- ffn_gate_weight_grad: float32 [2048, 6144], P('wide', 'head')
- ffn_up_weight_grad: float32 [2048, 6144], P('wide', 'head')
- ffn_down_weight_grad: float32 [2048, 6144], P('wide', 'head')
- attn_gain_grad: float32 [2048], replicated
- ffn_gain_grad: float32 [2048], replicated
- query_gain_grad: float32 [128], replicated
- key_gain_grad: float32 [128], replicated
Inputs may be any that keep to these rules, and one draw needn't show every extreme that they name: `doc_lengths`: 8 documents packed in order fill the row of 2048 tokens; their lengths sum to 2048 and the longest has exactly 1024 tokens.
All inputs are finite; a program needn't handle non-finite values.
Results may differ from a plain program's by a relative error of at most 0.03.
Values may be sent and summed in bfloat16 or wider, within the bound.
No kernel may reach another device: no remote copies, remote signals or barrier semaphores. Data moves between devices by JAX's collectives and lax.ppermute only.
A program may use at most 128 MiB of HBM per device.

v0:
```python
import jax
import jax.numpy as jnp
from jax import lax
from jax.sharding import PartitionSpec as P

HEAD_WIDTH = 128


epsilon = 1e-06
rope_base = 1000000.0
masked_score = -1e30


def segment_of(lengths, token_ids):
    doc_ends = jnp.cumsum(lengths)
    return jnp.sum((token_ids[:, None] >= doc_ends[None, :]).astype(jnp.int32), axis=1)


def doc_tables(lengths, token_ids):
    doc_ends = jnp.cumsum(lengths)
    starts = doc_ends - lengths
    segment = segment_of(lengths, token_ids)
    labels = jnp.arange(lengths.shape[0], dtype=jnp.int32)
    doc_begin = jnp.sum(jnp.where(segment[:, None] == labels[None, :], starts[None, :], 0), axis=1)
    return (segment, token_ids - doc_begin)


def rope_tables(positions, head_size):
    half_size = head_size // 2
    frequency = rope_base ** (-2.0 * jnp.arange(half_size, dtype=jnp.float32) / head_size)
    angles = positions.astype(jnp.float32)[:, None] * frequency[None, :]
    cosine = jnp.cos(angles)
    sine_table = jnp.sin(angles)
    return (
        jnp.concatenate([cosine, cosine], axis=1),
        jnp.concatenate([sine_table, sine_table], axis=1),
    )


def rotate_half(values):
    half_size = values.shape[-1] // 2
    return jnp.concatenate([-values[..., half_size:], values[..., :half_size]], axis=-1)


def rotate_back(values):
    half_size = values.shape[-1] // 2
    return jnp.concatenate([values[..., half_size:], -values[..., :half_size]], axis=-1)


def apply_rope(values, cos_table, sin_table):
    return values * cos_table[:, None, :] + rotate_half(values) * sin_table[:, None, :]


def rope_back(grads, cos_table, sin_table):
    return grads * cos_table[:, None, :] + rotate_back(grads * sin_table[:, None, :])


def contract_last(left, right):
    return lax.dot_general(
        left, right, (((1,), (1,)), ((), ())), preferred_element_type=jnp.float32
    )


def contract_first(left, right):
    return lax.dot_general(
        left, right, (((0,), (0,)), ((), ())), preferred_element_type=jnp.float32
    )


def norm_back(grad_out, inputs, inv_root, gain):
    scaled = grad_out * gain
    return inv_root * scaled - inputs * inv_root**3 * jnp.mean(
        scaled * inputs, axis=-1, keepdims=True
    )


def on_device(
    hidden_in,
    out_cotangent,
    doc_lengths,
    query_weight,
    key_matrix,
    value_matrix,
    gate_weight,
    out_weight,
    ffn_gate_weight,
    ffn_up_weight,
    ffn_down_weight,
    attn_gain,
    ffn_gain,
    query_gain,
    key_gain,
):
    tok_rows = hidden_in.shape[0]
    row_length = tok_rows * lax.axis_size("wide")
    first_row = lax.axis_index("wide") * tok_rows
    token_ids = first_row + jnp.arange(tok_rows, dtype=jnp.int32)
    segment, positions = doc_tables(doc_lengths, token_ids)
    shard_begin = first_row - positions[0]
    shard_last = first_row + tok_rows - 1
    cos_table, sin_table = rope_tables(positions, HEAD_WIDTH)
    local_heads = query_weight.shape[1] // HEAD_WIDTH
    kv_heads = key_matrix.shape[1] // HEAD_WIDTH
    group_width = local_heads // kv_heads
    query_rows = group_width * tok_rows
    score_scale = HEAD_WIDTH ** (-0.5)
    (
        full_query,
        full_key,
        full_value,
        full_gate,
        full_out,
        full_ffn_gate,
        full_ffn_up,
        full_ffn_down,
    ) = (
        lax.all_gather(query_weight, "wide", axis=0, tiled=True),
        lax.all_gather(key_matrix, "wide", axis=0, tiled=True),
        lax.all_gather(value_matrix, "wide", axis=0, tiled=True),
        lax.all_gather(gate_weight, "wide", axis=0, tiled=True),
        lax.all_gather(out_weight, "wide", axis=0, tiled=True),
        lax.all_gather(ffn_gate_weight, "wide", axis=0, tiled=True),
        lax.all_gather(ffn_up_weight, "wide", axis=0, tiled=True),
        lax.all_gather(ffn_down_weight, "wide", axis=0, tiled=True),
    )
    hidden32 = hidden_in.astype(jnp.float32)
    inv_one = lax.rsqrt(jnp.mean(hidden32 * hidden32, axis=1, keepdims=True) + epsilon)
    normed_input = (hidden32 * inv_one * attn_gain).astype(jnp.bfloat16)
    query_pre = jnp.dot(normed_input, full_query, preferred_element_type=jnp.float32).reshape(
        tok_rows, local_heads, HEAD_WIDTH
    )
    key_before_norm = jnp.dot(normed_input, full_key, preferred_element_type=jnp.float32).reshape(
        tok_rows, kv_heads, HEAD_WIDTH
    )
    value_rows = jnp.dot(normed_input, full_value, preferred_element_type=jnp.float32).astype(
        jnp.bfloat16
    )
    gate_pre = jnp.dot(normed_input, full_gate, preferred_element_type=jnp.float32)
    inv_query = lax.rsqrt(jnp.mean(query_pre * query_pre, axis=-1, keepdims=True) + epsilon)
    inv_key = lax.rsqrt(
        jnp.mean(key_before_norm * key_before_norm, axis=-1, keepdims=True) + epsilon
    )
    query_unit = query_pre * inv_query
    key_unit = key_before_norm * inv_key
    query_rot = apply_rope(query_unit * query_gain, cos_table, sin_table).astype(jnp.bfloat16)
    key_rows = (
        apply_rope(key_unit * key_gain, cos_table, sin_table)
        .astype(jnp.bfloat16)
        .reshape(tok_rows, kv_heads * HEAD_WIDTH)
    )
    query_heads = (
        query_rot.reshape(tok_rows, kv_heads, group_width, HEAD_WIDTH)
        .transpose(1, 2, 0, 3)
        .reshape(kv_heads, query_rows, HEAD_WIDTH)
    )
    query_seg = jnp.tile(segment, group_width)
    query_ids = jnp.tile(token_ids, group_width)
    start_state = (
        jnp.full((kv_heads, query_rows), masked_score, jnp.float32),
        jnp.zeros((kv_heads, query_rows), jnp.float32),
        jnp.zeros((kv_heads, query_rows, HEAD_WIDTH), jnp.float32),
    )
    key_piece = lax.all_gather(key_rows, "wide", axis=0, tiled=True)
    value_piece = lax.all_gather(value_rows, "wide", axis=0, tiled=True)
    count = key_piece.shape[0]
    step_rows = 512
    steps_count = count // step_rows
    key_ids = jnp.arange(count, dtype=jnp.int32)
    key_seg = segment_of(doc_lengths, key_ids)
    key_blocks = key_piece.reshape(steps_count, step_rows, kv_heads, HEAD_WIDTH).transpose(
        0, 2, 1, 3
    )
    value_blocks = value_piece.reshape(steps_count, step_rows, kv_heads, HEAD_WIDTH).transpose(
        0, 2, 1, 3
    )

    def inner(state, block):
        key_block, value_block, block_seg, block_ids = block

        def inner_work(state_in):
            scores = (
                jnp.einsum(
                    "hqd,hkd->hqk", query_heads, key_block, preferred_element_type=jnp.float32
                )
                * score_scale
            )
            allowed = (
                (query_seg[:, None] == block_seg[None, :])
                & (block_ids[None, :] <= query_ids[:, None])
            )[None]
            scores = jnp.where(allowed, scores, masked_score)
            running, total, accum = state_in
            newest = jnp.maximum(running, jnp.max(scores, axis=-1))
            factor = jnp.exp(running - newest)
            weights = jnp.where(allowed, jnp.exp(scores - newest[..., None]), 0.0)
            total = total * factor + jnp.sum(weights, axis=-1)
            accum = accum * factor[..., None] + jnp.einsum(
                "hqk,hkd->hqd",
                weights.astype(jnp.bfloat16),
                value_block,
                preferred_element_type=jnp.float32,
            )
            return (newest, total, accum)

        useful = (block_ids[0] <= shard_last) & (block_ids[step_rows - 1] >= shard_begin)
        return (lax.cond(useful, inner_work, lambda state_in: state_in, state), None)

    state, unused = lax.scan(
        inner,
        start_state,
        (
            key_blocks,
            value_blocks,
            key_seg.reshape(steps_count, step_rows),
            key_ids.reshape(steps_count, step_rows),
        ),
    )
    running, total, accum = state
    attended_heads = accum / total[..., None]
    log_total = running + jnp.log(total)
    attended = (
        attended_heads.reshape(kv_heads, group_width, tok_rows, HEAD_WIDTH)
        .transpose(2, 0, 1, 3)
        .reshape(tok_rows, local_heads * HEAD_WIDTH)
    )
    gate_sig = jax.nn.sigmoid(gate_pre)
    gated = (attended * gate_sig).astype(jnp.bfloat16)
    branch = lax.psum(contract_last(gated, full_out).astype(jnp.bfloat16), "head").astype(
        jnp.float32
    )
    middle = hidden32 + branch
    inv_two = lax.rsqrt(jnp.mean(middle * middle, axis=1, keepdims=True) + epsilon)
    normed_two = (middle * inv_two * ffn_gain).astype(jnp.bfloat16)
    ffn_gate_pre = jnp.dot(normed_two, full_ffn_gate, preferred_element_type=jnp.float32)
    ffn_up_pre = jnp.dot(normed_two, full_ffn_up, preferred_element_type=jnp.float32)
    gate_act = jax.nn.sigmoid(ffn_gate_pre)
    silu_gate = ffn_gate_pre * gate_act
    hidden_act = (silu_gate * ffn_up_pre).astype(jnp.bfloat16)
    ffn_out = lax.psum(
        contract_last(hidden_act, full_ffn_down).astype(jnp.bfloat16), "head"
    ).astype(jnp.float32)
    layer_out = (middle + ffn_out).astype(jnp.bfloat16)
    (
        back_query,
        back_key,
        back_value,
        back_gate,
        back_out,
        back_ffn_gate,
        back_ffn_up,
        back_ffn_down,
    ) = (
        lax.all_gather(query_weight, "wide", axis=0, tiled=True),
        lax.all_gather(key_matrix, "wide", axis=0, tiled=True),
        lax.all_gather(value_matrix, "wide", axis=0, tiled=True),
        lax.all_gather(gate_weight, "wide", axis=0, tiled=True),
        lax.all_gather(out_weight, "wide", axis=0, tiled=True),
        lax.all_gather(ffn_gate_weight, "wide", axis=0, tiled=True),
        lax.all_gather(ffn_up_weight, "wide", axis=0, tiled=True),
        lax.all_gather(ffn_down_weight, "wide", axis=0, tiled=True),
    )
    grad32 = out_cotangent.astype(jnp.float32)
    grad_hidden = jnp.dot(out_cotangent, back_ffn_down, preferred_element_type=jnp.float32)
    grad_ffn_gate = (
        grad_hidden * ffn_up_pre * gate_act * (1.0 + ffn_gate_pre * (1.0 - gate_act))
    ).astype(jnp.bfloat16)
    grad_ffn_up = (grad_hidden * silu_gate).astype(jnp.bfloat16)
    grad_normed_two = lax.psum(
        (
            contract_last(grad_ffn_gate, back_ffn_gate) + contract_last(grad_ffn_up, back_ffn_up)
        ).astype(jnp.bfloat16),
        "head",
    ).astype(jnp.float32)
    grad_middle = grad32 + norm_back(grad_normed_two, middle, inv_two, ffn_gain)
    grad_branch = grad_middle.astype(jnp.bfloat16)
    grad_gated = jnp.dot(grad_branch, back_out, preferred_element_type=jnp.float32)
    grad_attended = (grad_gated * gate_sig).astype(jnp.bfloat16)
    grad_gate_pre = (grad_gated * attended * gate_sig * (1.0 - gate_sig)).astype(jnp.bfloat16)
    grad_heads = (
        grad_attended.reshape(tok_rows, kv_heads, group_width, HEAD_WIDTH)
        .transpose(1, 2, 0, 3)
        .reshape(kv_heads, query_rows, HEAD_WIDTH)
    )
    delta = jnp.sum(grad_heads.astype(jnp.float32) * attended_heads, axis=-1)
    all_keys, all_values = (
        lax.all_gather(key_rows, "wide", axis=0, tiled=True),
        lax.all_gather(value_rows, "wide", axis=0, tiled=True),
    )
    key_step = 512
    key_count = row_length // key_step
    all_ids = jnp.arange(row_length, dtype=jnp.int32)
    all_seg = segment_of(doc_lengths, all_ids)
    key_blocks = all_keys.reshape(key_count, key_step, kv_heads, HEAD_WIDTH).transpose(0, 2, 1, 3)
    value_blocks = all_values.reshape(key_count, key_step, kv_heads, HEAD_WIDTH).transpose(
        0, 2, 1, 3
    )
    key_scan_items = (
        key_blocks,
        value_blocks,
        all_seg.reshape(key_count, key_step),
        all_ids.reshape(key_count, key_step),
    )
    zero_query = jnp.zeros((kv_heads, query_rows, HEAD_WIDTH), jnp.float32)

    def block_terms(key_block, value_block, block_seg, block_ids):
        scores = (
            jnp.einsum("hqd,hkd->hqk", query_heads, key_block, preferred_element_type=jnp.float32)
            * score_scale
        )
        allowed = (
            (query_seg[:, None] == block_seg[None, :]) & (block_ids[None, :] <= query_ids[:, None])
        )[None]
        weights = jnp.where(
            allowed, jnp.exp(jnp.where(allowed, scores, masked_score) - log_total[..., None]), 0.0
        )
        grad_weights = jnp.einsum(
            "hqd,hkd->hqk", grad_heads, value_block, preferred_element_type=jnp.float32
        )
        grad_scores = (weights * (grad_weights - delta[..., None])).astype(jnp.bfloat16)
        return (weights, grad_scores)

    def block_useful(block_ids):
        return (block_ids[0] <= shard_last) & (block_ids[key_step - 1] >= shard_begin)

    def back_block(grad_query, block):
        key_block, value_block, block_seg, block_ids = block

        def back_work(grad_in):
            weights, grad_scores = block_terms(key_block, value_block, block_seg, block_ids)
            grad_out = (
                grad_in
                + jnp.einsum(
                    "hqk,hkd->hqd", grad_scores, key_block, preferred_element_type=jnp.float32
                )
                * score_scale
            )
            grad_key = (
                jnp.einsum(
                    "hqk,hqd->hkd", grad_scores, query_heads, preferred_element_type=jnp.float32
                )
                * score_scale
            )
            grad_value = jnp.einsum(
                "hqk,hqd->hkd",
                weights.astype(jnp.bfloat16),
                grad_heads,
                preferred_element_type=jnp.float32,
            )
            return (grad_out, (grad_key, grad_value))

        def skip(grad_in):
            nothing = jnp.zeros((kv_heads, key_step, HEAD_WIDTH), jnp.float32)
            return (grad_in, (nothing, nothing))

        return lax.cond(block_useful(block_ids), back_work, skip, grad_query)

    grad_query, (key_parts, value_parts) = lax.scan(back_block, zero_query, key_scan_items)
    key_grad_rows = key_parts.transpose(0, 2, 1, 3).reshape(row_length, kv_heads * HEAD_WIDTH)
    value_grad_rows = value_parts.transpose(0, 2, 1, 3).reshape(row_length, kv_heads * HEAD_WIDTH)
    key_total, value_total = (
        lax.psum_scatter(
            key_grad_rows.astype(jnp.bfloat16), "wide", scatter_dimension=0, tiled=True
        ).astype(jnp.float32),
        lax.psum_scatter(
            value_grad_rows.astype(jnp.bfloat16), "wide", scatter_dimension=0, tiled=True
        ).astype(jnp.float32),
    )
    grad_values = value_total.astype(jnp.bfloat16)
    grad_key_rot = (
        key_total.astype(jnp.bfloat16).astype(jnp.float32).reshape(tok_rows, kv_heads, HEAD_WIDTH)
    )
    grad_query_rot = (
        grad_query.astype(jnp.bfloat16)
        .astype(jnp.float32)
        .reshape(kv_heads, group_width, tok_rows, HEAD_WIDTH)
        .transpose(2, 0, 1, 3)
        .reshape(tok_rows, local_heads, HEAD_WIDTH)
    )
    grad_query_unit = rope_back(grad_query_rot, cos_table, sin_table)
    grad_key_unit = rope_back(grad_key_rot, cos_table, sin_table)
    query_gain_part = jnp.sum(grad_query_unit * query_unit, axis=(0, 1))
    key_gain_part = jnp.sum(grad_key_unit * key_unit, axis=(0, 1))
    grad_query_pre = (
        norm_back(grad_query_unit, query_pre, inv_query, query_gain)
        .reshape(tok_rows, local_heads * HEAD_WIDTH)
        .astype(jnp.bfloat16)
    )
    grad_key_pre = (
        norm_back(grad_key_unit, key_before_norm, inv_key, key_gain)
        .reshape(tok_rows, kv_heads * HEAD_WIDTH)
        .astype(jnp.bfloat16)
    )
    grad_normed_part = (
        contract_last(grad_query_pre, back_query)
        + contract_last(grad_key_pre, back_key)
        + contract_last(grad_values, back_value)
        + contract_last(grad_gate_pre, back_gate)
    )
    grad_normed = lax.psum(grad_normed_part.astype(jnp.bfloat16), "head").astype(jnp.float32)
    input_grad = (grad_middle + norm_back(grad_normed, hidden32, inv_one, attn_gain)).astype(
        jnp.bfloat16
    )
    attn_gain_part = jnp.sum(grad_normed * hidden32 * inv_one, axis=0)
    ffn_gain_part = jnp.sum(grad_normed_two * middle * inv_two, axis=0)
    weight_grads = lax.psum_scatter(
        jnp.concatenate(
            [
                contract_first(normed_input, grad_query_pre),
                contract_first(normed_input, grad_key_pre),
                contract_first(normed_input, grad_values),
                contract_first(normed_input, grad_gate_pre),
                contract_first(grad_branch, gated),
                contract_first(normed_two, grad_ffn_gate),
                contract_first(normed_two, grad_ffn_up),
                contract_first(out_cotangent, hidden_act),
            ],
            axis=1,
        ).astype(jnp.bfloat16),
        "wide",
        scatter_dimension=0,
        tiled=True,
    ).astype(jnp.float32)
    col_widths = [
        query_weight.shape[1],
        key_matrix.shape[1],
        value_matrix.shape[1],
        gate_weight.shape[1],
        out_weight.shape[1],
        ffn_gate_weight.shape[1],
        ffn_up_weight.shape[1],
        ffn_down_weight.shape[1],
    ]
    pieces = []
    offset = 0
    for width in col_widths:
        pieces.append(weight_grads[:, offset : offset + width])
        offset = offset + width
    head_first = (lax.axis_index("head") == 0).astype(jnp.float32)
    attn_gain_grad, ffn_gain_grad, query_gain_grad, key_gain_grad = lax.psum(
        (attn_gain_part * head_first, ffn_gain_part * head_first, query_gain_part, key_gain_part),
        ("wide", "head"),
    )
    return (
        layer_out,
        input_grad,
        pieces[0],
        pieces[1],
        pieces[2],
        pieces[3],
        pieces[4],
        pieces[5],
        pieces[6],
        pieces[7],
        attn_gain_grad,
        ffn_gain_grad,
        query_gain_grad,
        key_gain_grad,
    )


def solution(mesh):
    return jax.shard_map(
        on_device,
        mesh=mesh,
        in_specs=(
            P("wide", None),
            P("wide", None),
            P(),
            P("wide", "head"),
            P("wide", "head"),
            P("wide", "head"),
            P("wide", "head"),
            P("wide", "head"),
            P("wide", "head"),
            P("wide", "head"),
            P("wide", "head"),
            P(),
            P(),
            P(),
            P(),
        ),
        out_specs=(
            P("wide", None),
            P("wide", None),
            P("wide", "head"),
            P("wide", "head"),
            P("wide", "head"),
            P("wide", "head"),
            P("wide", "head"),
            P("wide", "head"),
            P("wide", "head"),
            P("wide", "head"),
            P(),
            P(),
            P(),
            P(),
        ),
        check_vma=False,
    )
```

profile of v0, /device:TPU:0, one launch (start us, length us, event | category | flops | bytes accessed | tf_op | source)
XLA Modules:
  0.0 1408.4 jit_solution(11112789473760182477)
XLA Ops:
  13.2 39.8 %all-gather.17.cloned.1.call-done = bf16[2048,256]{1,0:T(8,128)(2,1)} async-done(((bf16[256,256]{1,0:T(8,128)(2,1)}), bf16[2048,256]{1,0:T(8,128)(2,1)}) %all-gather.17.cloned.1.call-update) | async-done | bytes 1048592 | tf_op jit(solution)/shard_map/all_gather | solution.py:119
  56.9 37.2 %all-gather.11.cloned.1.call-done = bf16[2048,256]{1,0:T(8,128)(2,1)} async-done(((bf16[256,256]{1,0:T(8,128)(2,1)}), bf16[2048,256]{1,0:T(8,128)(2,1)}) %all-gather.11.cloned.1.call-update) | async-done | bytes 1048592 | tf_op jit(solution)/shard_map/all_gather | solution.py:118
  101.2 43.1 %all-gather.15.cloned.1.call-done = bf16[2048,512]{1,0:T(8,128)(2,1)} async-done(((bf16[256,512]{1,0:T(8,128)(2,1)}), bf16[2048,512]{1,0:T(8,128)(2,1)}) %all-gather.15.cloned.1.call-update) | async-done | bytes 2097168 | tf_op jit(solution)/shard_map/all_gather | solution.py:117
  149.1 36.5 %all-gather.19.cloned.1.call-done = bf16[2048,256]{1,0:T(8,128)(2,1)} async-done(((bf16[256,256]{1,0:T(8,128)(2,1)}), bf16[2048,256]{1,0:T(8,128)(2,1)}) %all-gather.19.cloned.1.call-update) | async-done | bytes 1048592 | tf_op jit(solution)/shard_map/all_gather | solution.py:164
  190.0 36.3 %all-gather.13.cloned.1.call-done = bf16[2048,256]{0,1:T(8,128)(2,1)} async-done(((bf16[256,256]{0,1:T(8,128)(2,1)}), bf16[2048,256]{0,1:T(8,128)(2,1)}) %all-gather.13.cloned.1.call-update) | async-done | bytes 1048592 | tf_op jit(solution)/shard_map/all_gather | solution.py:163
  234.2 12.7 while.33
  248.8 27.7 %all-gather.21.cloned.1.call-done = bf16[2048,512]{1,0:T(8,128)(2,1)} async-done(((bf16[256,512]{1,0:T(8,128)(2,1)}), bf16[2048,512]{1,0:T(8,128)(2,1)}) %all-gather.21.cloned.1.call-update) | async-done | bytes 2097168 | tf_op jit(solution)/shard_map/all_gather | solution.py:120
  279.8 46.6 %all-gather.23.cloned.1.call-done = bf16[2048,512]{1,0:T(8,128)(2,1)} async-done(((bf16[256,512]{1,0:T(8,128)(2,1)}), bf16[2048,512]{1,0:T(8,128)(2,1)}) %all-gather.23.cloned.1.call-update) | async-done | bytes 2097168 | tf_op jit(solution)/shard_map/all_gather | solution.py:121
  332.2 32.3 %all-reduce.6.cloned.1.call-done = bf16[256,2048]{1,0:T(8,128)(2,1)} async-done(((bf16[256,2048]{1,0:T(8,128)(2,1)}), bf16[256,2048]{1,0:T(8,128)(2,1)}) %all-reduce.6.cloned.1.call-update) | async-done | bytes 1048592 | tf_op jit(solution)/shard_map/psum | solution.py:228
  368.3 98.1 %all-gather.27.cloned.1.call-done = bf16[2048,1536]{1,0:T(8,128)(2,1)} async-done(((bf16[256,1536]{1,0:T(8,128)(2,1)}), bf16[2048,1536]{1,0:T(8,128)(2,1)}) %all-gather.27.cloned.1.call-update) | async-done | bytes 6291472 | tf_op jit(solution)/shard_map/all_gather | solution.py:123
  466.4 6.0 fusion.116
  472.4 93.5 %all-gather.25.cloned.1.call-done = bf16[2048,1536]{1,0:T(8,128)(2,1)} async-done(((bf16[256,1536]{1,0:T(8,128)(2,1)}), bf16[2048,1536]{1,0:T(8,128)(2,1)}) %all-gather.25.cloned.1.call-update) | async-done | bytes 6291472 | tf_op jit(solution)/shard_map/all_gather | solution.py:122
  565.9 6.1 fusion.115
  571.9 93.6 %all-gather.29.cloned.1.call-done = bf16[2048,1536]{1,0:T(8,128)(2,1)} async-done(((bf16[256,1536]{1,0:T(8,128)(2,1)}), bf16[2048,1536]{1,0:T(8,128)(2,1)}) %all-gather.29.cloned.1.call-update) | async-done | bytes 6291472 | tf_op jit(solution)/shard_map/all_gather | solution.py:124
  665.5 7.2 multiply_convert_fusion.1
  681.5 33.2 %all-reduce.8.cloned.1.call-done = bf16[256,2048]{1,0:T(8,128)(2,1)} async-done(((bf16[256,2048]{1,0:T(8,128)(2,1)}), bf16[256,2048]{1,0:T(8,128)(2,1)}) %all-reduce.8.cloned.1.call-update) | async-done | bytes 1048592 | tf_op jit(solution)/shard_map/psum | solution.py:268
  721.6 18.3 %while.34 = (s32[]{:T(128)}, f32[2,512,128]{2,1,0:T(8,128)S(1)}, bf16[4,2,512,128]{3,2,1,0:T(8,128)(2,1)}, bf16[4,2,512,128]{3,2,1,0:T(8,128)(2,1)}, s32[4,512]{...) while((s32[]{:T(128)}, f32[2,512,128]{2,1,0:T(8,128)S(1)}, ...), condition=%wide.region_22.23_spmd.clone, body=%wide.region_19.22_spmd.clone.sunk | while | flops 676593664 | bytes 15524267 | solution.py:357
  723.5 7.4 conditional.7
  745.3 5.9 convolution_convert_fusion.9
  768.8 46.9 %reduce-scatter.4.cloned.1.call-done = bf16[256,256]{0,1:T(8,128)(2,1)} async-done(((bf16[2048,256]{0,1:T(8,128)(2,1)}), bf16[256,256]{0,1:T(8,128)(2,1)}) %reduce-scatter.4.cloned.1.call-update) | async-done | bytes 131088 | tf_op jit(solution)/shard_map/reduce_scatter | solution.py:361
  820.2 62.3 %reduce-scatter.6.cloned.1.call-done = bf16[256,256]{1,0:T(8,128)(2,1)} async-done(((bf16[2048,256]{1,0:T(8,128)(2,1)}), bf16[256,256]{1,0:T(8,128)(2,1)}) %reduce-scatter.6.cloned.1.call-update) | async-done | bytes 131088 | tf_op jit(solution)/shard_map/reduce_scatter | solution.py:364
  917.4 26.7 %all-reduce.10.cloned.1.call-done = (bf16[256,2048]{1,0:T(8,128)(2,1)}, bf16[256,2048]{1,0:T(8,128)(2,1)}) async-done(((bf16[256,2048]{1,0:T(8,128)(2,1)}, bf16[256,2048]{1,0:T(8,128)(2,1)}), (bf16[256,2048]{1,0:T(8,128)(2,1)}, bf16[256,2048]{1,0:T(8,128)(2,1)})) %all-reduce.10.cloned.1.call-update) | async-done | bytes 2097168 | tf_op jit(solution)/shard_map/psum | solution.py:239
  946.1 43.8 %all-reduce = (f32[2048]{0:T(1024)}, f32[2048]{0:T(1024)}, f32[128]{0:T(128)}, f32[128]{0:T(128)}) all-reduce(f32[2048]{0:T(1024)S(1)} %get-tuple-element.661, f32[2048]{0:T(1024)S(1)} %get-tuple-element.660, f32[128]{0:T(128)S(1)} %copy-done.74, f32[128]{0:T(128)S(1)} %bitcast_reduce_fusion), channel_id=1, replica_groups=mesh['wide'=8,'head'=4] {'wide','head'}, use_global_device_ids=true, to_apply=%region_31.32 | all-reduce | flops 4352 | bytes 34816 | tf_op jit(solution)/shard_map/psum | solution.py:439
  994.3 389.0 %reduce-scatter.8.cloned.1.call-done = bf16[256,6656]{0,1:T(8,128)(2,1)} async-done(((bf16[2048,6656]{0,1:T(8,128)(2,1)}), bf16[256,6656]{0,1:T(8,128)(2,1)}) %reduce-scatter.8.cloned.1.call-update) | async-done | bytes 3407888 | tf_op jit(solution)/shard_map/reduce_scatter | solution.py:405
  (369 shorter events, 175.7 us)
Async XLA Ops:
  7.2 45.8 %all-gather.17.cloned.1.call-start = ((), (), s32[]{:S(2)}) async-start(), calls=%async_computation.6 | async-start | bytes 1179648 | tf_op jit(solution)/shard_map/all_gather | solution.py:119
  7.9 86.2 %all-gather.11.cloned.1.call-start = ((), (), s32[]{:S(2)}) async-start(), calls=%async_computation.3 | async-start | bytes 1179648 | tf_op jit(solution)/shard_map/all_gather | solution.py:118
  8.7 135.6 %all-gather.15.cloned.1.call-start = ((), (), s32[]{:S(2)}) async-start(), calls=%async_computation.5 | async-start | bytes 2359296 | tf_op jit(solution)/shard_map/all_gather | solution.py:117
  9.4 176.1 %all-gather.19.cloned.1.call-start = ((), (), s32[]{:S(2)}) async-start(), calls=%async_computation.7 | async-start | bytes 1179648 | tf_op jit(solution)/shard_map/all_gather | solution.py:164
  13.2 131.1 %copy-start.59 = (f32[256]{0:T(256)}, f32[256]{0:T(256)S(1)}, u32[]{:S(2)}) copy-start(f32[256]{0:T(256)S(1)} %get-tuple-element.653) | copy-start | bytes 3076
  55.9 170.5 %all-gather.13.cloned.1.call-start = ((), (), s32[]{:S(2)}) async-start(), calls=%async_computation.4 | async-start | bytes 1179648 | tf_op jit(solution)/shard_map/all_gather | solution.py:163
  97.6 178.9 %all-gather.21.cloned.1.call-start = ((), (), s32[]{:S(2)}) async-start(), calls=%async_computation.8 | async-start | bytes 2359296 | tf_op jit(solution)/shard_map/all_gather | solution.py:120
  98.2 228.2 %all-gather.23.cloned.1.call-start = ((), (), s32[]{:S(2)}) async-start(), calls=%async_computation.9 | async-start | bytes 2359296 | tf_op jit(solution)/shard_map/all_gather | solution.py:121
  99.0 265.6 %all-reduce.6.cloned.1.call-start = ((), (), s32[]{:S(2)}) async-start(), calls=%async_computation.10 | async-start | bytes 2097152 | tf_op jit(solution)/shard_map/psum | solution.py:228
  146.8 84.2 %copy-start.5 = (f32[256,4,128]{2,1,0:T(4,128)}, f32[256,4,128]{2,1,0:T(4,128)S(1)}, u32[]{:S(2)}) copy-start(f32[256,4,128]{2,1,0:T(4,128)S(1)} %reshape.425) | copy-start | bytes 1572868
  149.0 83.7 %copy-start.9 = (f32[256,2,2,128]{3,2,1,0:T(2,128)}, f32[256,2,2,128]{3,2,1,0:T(2,128)S(1)}, u32[]{:S(2)}) copy-start(f32[256,2,2,128]{3,2,1,0:T(2,128)S(1)} %reshape.424) | copy-start | bytes 1572868
  329.8 136.6 %all-gather.27.cloned.1.call-start = ((), (), s32[]{:S(2)}) async-start(), calls=%async_computation.12 | async-start | bytes 7077888 | tf_op jit(solution)/shard_map/all_gather | solution.py:123
  330.5 235.3 %all-gather.25.cloned.1.call-start = ((), (), s32[]{:S(2)}) async-start(), calls=%async_computation.11 | async-start | bytes 7077888 | tf_op jit(solution)/shard_map/all_gather | solution.py:122
  331.1 334.4 %all-gather.29.cloned.1.call-start = ((), (), s32[]{:S(2)}) async-start(), calls=%async_computation.13 | async-start | bytes 7077888 | tf_op jit(solution)/shard_map/all_gather | solution.py:124
  331.9 382.8 %all-reduce.8.cloned.1.call-start = ((), (), s32[]{:S(2)}) async-start(), calls=%async_computation.14 | async-start | bytes 2097152 | tf_op jit(solution)/shard_map/psum | solution.py:268
  366.8 347.9 %copy-start.55 = (f32[256]{0:T(256)}, f32[256]{0:T(256)S(1)}, u32[]{:S(2)}) copy-start(f32[256]{0:T(256)S(1)} %get-tuple-element.655) | copy-start | bytes 3076
  680.2 135.5 %reduce-scatter.4.cloned.1.call-start = ((), (), s32[]{:S(2)}) async-start(), calls=%async_computation.15 | async-start | bytes 1179648 | tf_op jit(solution)/shard_map/reduce_scatter | solution.py:361
  745.1 137.4 %reduce-scatter.6.cloned.1.call-start = ((), (), s32[]{:S(2)}) async-start(), calls=%async_computation.16 | async-start | bytes 1179648 | tf_op jit(solution)/shard_map/reduce_scatter | solution.py:364
  756.1 188.0 %all-reduce.10.cloned.1.call-start = ((), (), s32[]{:S(2)}) async-start(), calls=%async_computation.18 | async-start | bytes 4194304 | tf_op jit(solution)/shard_map/psum | solution.py:239
  893.4 490.0 %reduce-scatter.8.cloned.1.call-start = ((), (), s32[]{:S(2)}) async-start(), calls=%async_computation.17 | async-start | bytes 30670848 | tf_op jit(solution)/shard_map/reduce_scatter | solution.py:405
  916.7 73.2 %copy-start.61 = (f32[256]{0:T(256)S(1)}, f32[256]{0:T(256)}, u32[]{:S(2)}) copy-start(f32[256]{0:T(256)} %copy-done.59) | copy-start | bytes 3076
  916.7 73.2 %copy-start.67 = (f32[256]{0:T(256)S(1)}, f32[256]{0:T(256)}, u32[]{:S(2)}) copy-start(f32[256]{0:T(256)} %get-tuple-element.652) | copy-start | bytes 3076
  916.7 73.2 %copy-start.69 = (f32[256]{0:T(256)S(1)}, f32[256]{0:T(256)}, u32[]{:S(2)}) copy-start(f32[256]{0:T(256)} %get-tuple-element.654) | copy-start | bytes 3076
  916.7 73.2 %copy-start.72 = (f32[256]{0:T(256)S(1)}, f32[256]{0:T(256)}, u32[]{:S(2)}) copy-start(f32[256]{0:T(256)} %copy-done.70) | copy-start | bytes 3076
  (73 other events, 1280.9 us)
Sparse Core Ops, SparseCore 0:
  10.1 42.8 all-gather.16
  55.1 38.8 all-gather.10
  96.2 48.0 all-gather.14
  146.8 38.6 all-gather.18
  188.0 38.2 all-gather.12
  228.3 48.1 all-gather.20
  278.6 47.7 all-gather.22
  329.9 34.5 all-reduce.5
  366.9 99.3 all-gather.26
  468.6 97.1 all-gather.24
  568.3 97.1 all-gather.28
  680.4 34.2 all-reduce.7
  745.2 70.4 reduce-scatter.3
  820.0 62.4 reduce-scatter.5
  893.5 50.5 all-reduce.9
  948.3 435.0 reduce-scatter.7
where the time goes:
time: 1410 us
  waiting for transfers between devices  1150 us (82%)
  matrix products  87.3 us (6%)
  local copies, waits for them, and re-layouts  61.6 us (4%)
  blocking collectives  43.8 us (3%)
  other arithmetic  39.1 us (3%)
  between operations  15.8 us (1%)
    reduce_scatter x1, waiting for transfers between devices, on_device(): lax.psum_scatter(jnp.concatenate([contract_first(normed_input, grad_query...  389 us
    all_gather x1, waiting for transfers between devices, on_device(): lax.all_gather(ffn_up_weight, 'wide', axis=0, tiled=True)  98.1 us
    all_gather x1, waiting for transfers between devices, on_device(): lax.all_gather(ffn_down_weight, 'wide', axis=0, tiled=True)  93.6 us
    all_gather x1, waiting for transfers between devices, on_device(): lax.all_gather(ffn_gate_weight, 'wide', axis=0, tiled=True)  93.5 us
    reduce_scatter x1, waiting for transfers between devices, on_device(): lax.psum_scatter(value_grad_rows.astype(jnp.bfloat16), 'wide', scatter_di...  62.3 us
    reduce_scatter x1, waiting for transfers between devices, on_device(): lax.psum_scatter(key_grad_rows.astype(jnp.bfloat16), 'wide', scatter_dime...  46.9 us
    all_gather x1, waiting for transfers between devices, on_device(): lax.all_gather(out_weight, 'wide', axis=0, tiled=True)  46.6 us
    psum x1, blocking collectives, on_device(): lax.psum((attn_gain_part * head_first, ffn_gain_part * head_first, query_...  43.8 us
  transfers between devices with their start and end apart: 16, of which 16 were waited for; matrix products, arithmetic and copies ran while one was open for 8% of the time, Pallas kernels for 0%

commit v1 on v0

--- a/solution.py
+++ b/solution.py
@@ -1,6 +1,7 @@
 import jax
 import jax.numpy as jnp
 from jax import lax
+from jax.sharding import Mesh
 from jax.sharding import PartitionSpec as P
 
 HEAD_WIDTH = 128
@@ -240,40 +241,21 @@
         contract_last(hidden_act, full_ffn_down).astype(jnp.bfloat16), "head"
     ).astype(jnp.float32)
     layer_out = (middle + ffn_out).astype(jnp.bfloat16)
-    (
-        back_query,
-        back_key,
-        back_value,
-        back_gate,
-        back_out,
-        back_ffn_gate,
-        back_ffn_up,
-        back_ffn_down,
-    ) = (
-        lax.all_gather(query_weight, "wide", axis=0, tiled=True),
-        lax.all_gather(key_matrix, "wide", axis=0, tiled=True),
-        lax.all_gather(value_matrix, "wide", axis=0, tiled=True),
-        lax.all_gather(gate_weight, "wide", axis=0, tiled=True),
-        lax.all_gather(out_weight, "wide", axis=0, tiled=True),
-        lax.all_gather(ffn_gate_weight, "wide", axis=0, tiled=True),
-        lax.all_gather(ffn_up_weight, "wide", axis=0, tiled=True),
-        lax.all_gather(ffn_down_weight, "wide", axis=0, tiled=True),
-    )
     grad32 = out_cotangent.astype(jnp.float32)
-    grad_hidden = jnp.dot(out_cotangent, back_ffn_down, preferred_element_type=jnp.float32)
+    grad_hidden = jnp.dot(out_cotangent, full_ffn_down, preferred_element_type=jnp.float32)
     grad_ffn_gate = (
         grad_hidden * ffn_up_pre * gate_act * (1.0 + ffn_gate_pre * (1.0 - gate_act))
     ).astype(jnp.bfloat16)
     grad_ffn_up = (grad_hidden * silu_gate).astype(jnp.bfloat16)
     grad_normed_two = lax.psum(
         (
-            contract_last(grad_ffn_gate, back_ffn_gate) + contract_last(grad_ffn_up, back_ffn_up)
+            contract_last(grad_ffn_gate, full_ffn_gate) + contract_last(grad_ffn_up, full_ffn_up)
         ).astype(jnp.bfloat16),
         "head",
     ).astype(jnp.float32)
     grad_middle = grad32 + norm_back(grad_normed_two, middle, inv_two, ffn_gain)
     grad_branch = grad_middle.astype(jnp.bfloat16)
-    grad_gated = jnp.dot(grad_branch, back_out, preferred_element_type=jnp.float32)
+    grad_gated = jnp.dot(grad_branch, full_out, preferred_element_type=jnp.float32)
     grad_attended = (grad_gated * gate_sig).astype(jnp.bfloat16)
     grad_gate_pre = (grad_gated * attended * gate_sig * (1.0 - gate_sig)).astype(jnp.bfloat16)
     grad_heads = (
@@ -282,10 +264,7 @@
         .reshape(kv_heads, query_rows, HEAD_WIDTH)
     )
     delta = jnp.sum(grad_heads.astype(jnp.float32) * attended_heads, axis=-1)
-    all_keys, all_values = (
-        lax.all_gather(key_rows, "wide", axis=0, tiled=True),
-        lax.all_gather(value_rows, "wide", axis=0, tiled=True),
-    )
+    all_keys, all_values = key_piece, value_piece
     key_step = 512
     key_count = row_length // key_step
     all_ids = jnp.arange(row_length, dtype=jnp.int32)
@@ -391,10 +370,10 @@
         .astype(jnp.bfloat16)
     )
     grad_normed_part = (
-        contract_last(grad_query_pre, back_query)
-        + contract_last(grad_key_pre, back_key)
-        + contract_last(grad_values, back_value)
-        + contract_last(grad_gate_pre, back_gate)
+        contract_last(grad_query_pre, full_query)
+        + contract_last(grad_key_pre, full_key)
+        + contract_last(grad_values, full_value)
+        + contract_last(grad_gate_pre, full_gate)
     )
     grad_normed = lax.psum(grad_normed_part.astype(jnp.bfloat16), "head").astype(jnp.float32)
     input_grad = (grad_middle + norm_back(grad_normed, hidden32, inv_one, attn_gain)).astype(
@@ -458,42 +437,415 @@
     )
 
 
+PLANES = 4
+
+
+def pair_swap(values, axis):
+    return lax.ppermute(values, axis, [(0, 1), (1, 0)])
+
+
+def plane_swap(values, step):
+    return lax.ppermute(values, "z", [(i, i ^ step) for i in range(PLANES)])
+
+
+def gather_chunks(chunk):
+    columns = [chunk] + [plane_swap(chunk, step) for step in range(1, PLANES)]
+    return jnp.concatenate(columns + [pair_swap(piece, "y") for piece in columns], axis=0)
+
+
+def sum_chunks(parts):
+    rows = parts.shape[0] // (2 * PLANES)
+    total = None
+    for step in (2, 3, 1, 0):
+        other = PLANES + step
+        got = pair_swap(parts[other * rows : (other + 1) * rows], "y")
+        both = parts[step * rows : (step + 1) * rows].astype(jnp.float32) + got.astype(jnp.float32)
+        if step:
+            both = plane_swap(both.astype(jnp.bfloat16), step).astype(jnp.float32)
+        total = both if total is None else total + both
+    return total
+
+
+def flip_if(values, axis, flag):
+    return jnp.where(flag, jnp.flip(values, axis), values)
+
+
+def to_own_first(values, flag):
+    lead = values.shape[:-1]
+    width = values.shape[-1]
+    split = values.reshape(lead + (PLANES, 2, width // (2 * PLANES)))
+    zero = split[..., 0, :].reshape(lead + (width // 2,))
+    one = split[..., 1, :].reshape(lead + (width // 2,))
+    return jnp.concatenate([jnp.where(flag, one, zero), jnp.where(flag, zero, one)], axis=-1)
+
+
+def from_own_first(values, flag):
+    lead = values.shape[:-1]
+    width = values.shape[-1]
+    block = width // (2 * PLANES)
+    own = values[..., : width // 2].reshape(lead + (PLANES, block))
+    other = values[..., width // 2 :].reshape(lead + (PLANES, block))
+    pair = jnp.stack([jnp.where(flag, other, own), jnp.where(flag, own, other)], axis=-2)
+    return pair.reshape(lead + (width,))
+
+
+def spread_weight(local):
+    rows, planes, width = local.shape
+    mine = lax.all_to_all(
+        local.reshape(rows, planes * width), "z", split_axis=1, concat_axis=0, tiled=True
+    )
+    mine = jnp.concatenate([mine, pair_swap(mine, "x")], axis=0)
+    return mine, pair_swap(mine, "c")
+
+
+def collect_grad(mine, other):
+    half = mine.shape[0] // 2
+    both = mine.astype(jnp.float32) + pair_swap(other, "c").astype(jnp.float32)
+    both = both.astype(jnp.bfloat16)
+    rows = both[:half].astype(jnp.float32) + pair_swap(both[half:], "x").astype(jnp.float32)
+    back = lax.all_to_all(
+        rows.astype(jnp.bfloat16), "z", split_axis=0, concat_axis=1, tiled=True
+    )
+    return back.reshape(half // PLANES, PLANES, mine.shape[1])
+
+
+def head_norm(pre, gain):
+    inverse = lax.rsqrt(jnp.mean(pre * pre, axis=-1, keepdims=True) + epsilon)
+    unit = pre * inverse
+    return inverse, unit, unit * gain
+
+
+def on_slice_device(
+    hidden_in,
+    out_cotangent,
+    doc_lengths,
+    query_weight,
+    key_matrix,
+    value_matrix,
+    gate_weight,
+    out_weight,
+    ffn_gate_weight,
+    ffn_up_weight,
+    ffn_down_weight,
+    attn_gain,
+    ffn_gain,
+    query_gain,
+    key_gain,
+):
+    bf16, f32 = jnp.bfloat16, jnp.float32
+    block_rows, width = hidden_in.shape
+    chunk_rows = block_rows // 4
+    z, x, y, c = (lax.axis_index(name) for name in ("z", "x", "y", "c"))
+    odd_x, odd_c = x == 1, c == 1
+    score_scale = HEAD_WIDTH ** (-0.5)
+
+    def by_head(weight, inner):
+        return weight.reshape(block_rows, 2, inner, HEAD_WIDTH)
+
+    queries, gates = by_head(query_weight, 2), by_head(gate_weight, 2)
+    keys, vals = by_head(key_matrix, 1), by_head(value_matrix, 1)
+    half_zero = jnp.concatenate([queries[:, :, 0], gates[:, :, 0], keys[:, :, 0]], axis=-1)
+    half_one = jnp.concatenate([queries[:, :, 1], gates[:, :, 1], vals[:, :, 0]], axis=-1)
+    kept = jnp.where(odd_c, half_one, half_zero)
+    taken = pair_swap(jnp.where(odd_c, half_zero, half_one), "c")
+    attn_local = jnp.concatenate(
+        [jnp.where(odd_c, taken, kept), jnp.where(odd_c, kept, taken)], axis=1
+    )
+    attn_mine, attn_other = spread_weight(attn_local)
+
+    chunk_start = (y * 2 + c) * chunk_rows
+    own_hidden = lax.dynamic_slice_in_dim(hidden_in, chunk_start, chunk_rows, 0)
+    own_cotangent = lax.dynamic_slice_in_dim(out_cotangent, chunk_start, chunk_rows, 0)
+    hidden32 = to_own_first(own_hidden, odd_x).astype(f32)
+    cotangent = to_own_first(own_cotangent, odd_x)
+    gain_one = to_own_first(attn_gain, odd_x)
+    gain_two = to_own_first(ffn_gain, odd_x)
+    inv_one = lax.rsqrt(jnp.mean(hidden32 * hidden32, axis=1, keepdims=True) + epsilon)
+    normed_chunk = (hidden32 * inv_one * gain_one).astype(bf16)
+    normed = gather_chunks(normed_chunk)
+    tokens = normed.shape[0]
+
+    def ids_of(x_at, c_at):
+        step = jnp.arange(2 * PLANES, dtype=jnp.int32)
+        z_at, y_at = z ^ (step % PLANES), y ^ (step // PLANES)
+        start = (z_at * 2 + x_at) * block_rows + (y_at * 2 + c_at) * chunk_rows
+        return (start[:, None] + jnp.arange(chunk_rows, dtype=jnp.int32)[None, :]).reshape(-1)
+
+    query_ids = ids_of(x, c)
+    key_ids = jnp.concatenate([query_ids, ids_of(x ^ 1, c), ids_of(x, c ^ 1), ids_of(x ^ 1, c ^ 1)])
+    query_seg, positions = doc_tables(doc_lengths, query_ids)
+    key_seg = segment_of(doc_lengths, key_ids)
+    cos_table, sin_table = rope_tables(positions, HEAD_WIDTH)
+    cos_rows, sin_rows = cos_table, sin_table
+
+    def turn(values):
+        return values * cos_rows + rotate_half(values) * sin_rows
+
+    def turn_back(grads):
+        return grads * cos_rows + rotate_back(grads * sin_rows)
+
+    mine = jnp.dot(normed, attn_mine, preferred_element_type=f32)
+    other = jnp.dot(normed, attn_other, preferred_element_type=f32)
+    low, high = HEAD_WIDTH, 2 * HEAD_WIDTH
+    key_pre = jnp.where(odd_c, other[:, high:], mine[:, high:])
+    value_rows = jnp.where(odd_c, mine[:, high:], other[:, high:]).astype(bf16)
+    inv_key, key_unit, key_scaled = head_norm(key_pre, key_gain)
+    key_rows = turn(key_scaled).astype(bf16)
+    pair = jnp.concatenate([key_rows, value_rows], axis=1)
+    pair_x = pair_swap(pair, "x")
+    both_x = jnp.concatenate([pair, pair_x], axis=0)
+    all_pairs = jnp.concatenate([both_x, pair_swap(both_x, "c")], axis=0)
+    all_keys, all_values = all_pairs[:, :low], all_pairs[:, low:]
+
+    query_pre = jnp.stack([mine[:, :low], other[:, :low]])
+    gate_pre = jnp.stack([mine[:, low:high], other[:, low:high]])
+    inv_query, query_unit, query_scaled = head_norm(query_pre, query_gain)
+    query_rot = turn(query_scaled).astype(bf16)
+
+    allowed = (query_seg[:, None] == key_seg[None, :]) & (key_ids[None, :] <= query_ids[:, None])
+    scores = jnp.einsum("hqd,kd->hqk", query_rot, all_keys, preferred_element_type=f32) * score_scale
+    scores = jnp.where(allowed[None], scores, masked_score)
+    top = jnp.max(scores, axis=-1, keepdims=True)
+    raised = jnp.exp(scores - top)
+    total = jnp.sum(raised, axis=-1, keepdims=True)
+    attended = (
+        jnp.einsum("hqk,kd->hqd", raised.astype(bf16), all_values, preferred_element_type=f32)
+        / total
+    )
+    log_total = top + jnp.log(total)
+    gate_sig = jax.nn.sigmoid(gate_pre)
+    gated = (attended * gate_sig).astype(bf16)
+
+    out_rows = [out_weight] + [plane_swap(out_weight, step) for step in range(1, PLANES)]
+    out_plane = jnp.zeros((PLANES * block_rows, out_weight.shape[1]), bf16)
+    for step in range(PLANES):
+        out_plane = lax.dynamic_update_slice_in_dim(
+            out_plane, out_rows[step], (z ^ step) * block_rows, 0
+        )
+    out_here = jnp.concatenate([out_plane, pair_swap(out_plane, "x")], axis=0)
+    out_y = pair_swap(out_here, "y")
+    out_blocks = [[out_here, pair_swap(out_here, "c")], [out_y, pair_swap(out_y, "c")]]
+
+    flip_hi, flip_lo = (z // 2) != c, (z % 2) == 1
+
+    def to_blocks(pieces):
+        tiles = pieces.reshape(2, 2, 2, chunk_rows, 2, HEAD_WIDTH)
+        tiles = flip_if(flip_if(flip_if(tiles, 1, flip_hi), 2, flip_lo), 4, odd_c)
+        return tiles.transpose(0, 1, 3, 2, 4, 5).reshape(2, 2, chunk_rows, 4 * HEAD_WIDTH)
+
+    def from_blocks(blocks):
+        tiles = blocks.reshape(2, 2, chunk_rows, 2, 2, HEAD_WIDTH).transpose(0, 1, 3, 2, 4, 5)
+        tiles = flip_if(flip_if(flip_if(tiles, 1, flip_hi), 2, flip_lo), 4, odd_c)
+        return tiles.reshape(2, PLANES, chunk_rows, 2 * HEAD_WIDTH)
+
+    def to_owner(rows):
+        tiles = rows.reshape(2, PLANES, chunk_rows, 2 * HEAD_WIDTH)
+        tiles = jnp.stack(
+            [tiles[:, 0]] + [plane_swap(tiles[:, step], step) for step in range(1, PLANES)], axis=1
+        )
+        return jnp.stack([tiles[0], pair_swap(tiles[1], "y")])
+
+    def from_owner(tiles):
+        tiles = jnp.stack([tiles[0], pair_swap(tiles[1], "y")])
+        tiles = jnp.stack(
+            [tiles[:, 0]] + [plane_swap(tiles[:, step], step) for step in range(1, PLANES)], axis=1
+        )
+        return tiles.reshape(tokens, 2 * HEAD_WIDTH)
+
+    gated_rows = jnp.concatenate([gated[0], gated[1]], axis=1)
+    gated_blocks = to_blocks(to_owner(gated_rows))
+    branch = sum(
+        contract_last(gated_blocks[i, j], out_blocks[i][j]) for i in range(2) for j in range(2)
+    )
+    middle = hidden32 + branch
+    inv_two = lax.rsqrt(jnp.mean(middle * middle, axis=1, keepdims=True) + epsilon)
+    normed_two_chunk = (middle * inv_two * gain_two).astype(bf16)
+    normed_two = gather_chunks(normed_two_chunk)
+
+    def by_plane(weight):
+        return weight.reshape(block_rows, PLANES, weight.shape[1] // PLANES)
+
+    ffn_gate = spread_weight(by_plane(ffn_gate_weight))
+    ffn_up = spread_weight(by_plane(ffn_up_weight))
+    ffn_down = spread_weight(by_plane(ffn_down_weight))
+    all_cotangent = gather_chunks(cotangent)
+    hidden_acts, grads_gate, grads_up = [], [], []
+    for side in range(2):
+        ffn_gate_pre = jnp.dot(normed_two, ffn_gate[side], preferred_element_type=f32)
+        ffn_up_pre = jnp.dot(normed_two, ffn_up[side], preferred_element_type=f32)
+        grad_act = jnp.dot(all_cotangent, ffn_down[side], preferred_element_type=f32)
+        gate_act = jax.nn.sigmoid(ffn_gate_pre)
+        silu_gate = ffn_gate_pre * gate_act
+        hidden_acts.append((silu_gate * ffn_up_pre).astype(bf16))
+        grads_gate.append(
+            (grad_act * ffn_up_pre * gate_act * (1.0 + ffn_gate_pre * (1.0 - gate_act))).astype(bf16)
+        )
+        grads_up.append((grad_act * silu_gate).astype(bf16))
+    grad_normed_two = sum_chunks(
+        sum(
+            contract_last(grads_gate[side], ffn_gate[side])
+            + contract_last(grads_up[side], ffn_up[side])
+            for side in range(2)
+        ).astype(bf16)
+    )
+    ffn_out = sum_chunks(
+        sum(contract_last(hidden_acts[side], ffn_down[side]) for side in range(2)).astype(bf16)
+    )
+    layer_chunk = (middle + ffn_out).astype(bf16)
+
+    def whole_block(chunk):
+        chunk = from_own_first(chunk, odd_x)
+        by_core = jnp.stack([chunk, pair_swap(chunk, "c")])
+        by_core = flip_if(by_core, 0, odd_c)
+        by_y = jnp.stack([by_core, pair_swap(by_core, "y")])
+        return flip_if(by_y, 0, y == 1).reshape(block_rows, width)
+
+    layer_out = whole_block(layer_chunk)
+    down_grad = collect_grad(
+        *(contract_first(all_cotangent, act).astype(bf16) for act in hidden_acts)
+    )
+    gate_grad = collect_grad(*(contract_first(normed_two, g).astype(bf16) for g in grads_gate))
+    up_grad = collect_grad(*(contract_first(normed_two, g).astype(bf16) for g in grads_up))
+
+    grad_middle = cotangent.astype(f32) + norm_back(grad_normed_two, middle, inv_two, gain_two)
+    grad_branch = grad_middle.astype(bf16)
+    grad_blocks = jnp.stack(
+        [
+            jnp.stack(
+                [
+                    jnp.dot(grad_branch, out_blocks[i][j], preferred_element_type=f32).astype(bf16)
+                    for j in range(2)
+                ]
+            )
+            for i in range(2)
+        ]
+    )
+    grad_gated_rows = from_owner(from_blocks(grad_blocks)).astype(f32)
+    grad_gated = jnp.stack([grad_gated_rows[:, :low], grad_gated_rows[:, low:]])
+    grad_attended = (grad_gated * gate_sig).astype(bf16)
+    grad_gate_pre = (grad_gated * attended * gate_sig * (1.0 - gate_sig)).astype(bf16)
+    all_grad_branch = gather_chunks(grad_branch)
+    wo_gate_grad = collect_grad(
+        *(
+            jnp.concatenate(
+                [
+                    contract_first(all_grad_branch, gated[i]).astype(bf16),
+                    contract_first(normed, grad_gate_pre[i]).astype(bf16),
+                ],
+                axis=1,
+            )
+            for i in range(2)
+        )
+    )
+
+    delta = jnp.sum(grad_attended.astype(f32) * attended, axis=-1, keepdims=True)
+    weights = jnp.exp(scores - log_total)
+    grad_weights = jnp.einsum("hqd,kd->hqk", grad_attended, all_values, preferred_element_type=f32)
+    grad_scores = (weights * (grad_weights - delta)).astype(bf16)
+    grad_query_rot = (
+        jnp.einsum("hqk,kd->hqd", grad_scores, all_keys, preferred_element_type=f32) * score_scale
+    )
+    grad_keys = (
+        jnp.einsum("hqk,hqd->kd", grad_scores, query_rot, preferred_element_type=f32) * score_scale
+    )
+    grad_vals = jnp.einsum(
+        "hqk,hqd->kd", weights.astype(bf16), grad_attended, preferred_element_type=f32
+    )
+    grad_pairs = jnp.concatenate([grad_keys, grad_vals], axis=1).astype(bf16)
+    near = grad_pairs[: 2 * tokens].astype(f32) + pair_swap(grad_pairs[2 * tokens :], "c").astype(
+        f32
+    )
+    near = near.astype(bf16)
+    own_pair = near[:tokens].astype(f32) + pair_swap(near[tokens:], "x").astype(f32)
+    grad_key_unit = turn_back(own_pair[:, :low].astype(bf16).astype(f32))
+    grad_values = own_pair[:, low:].astype(bf16)
+    grad_query_unit = turn_back(grad_query_rot.astype(bf16).astype(f32))
+    query_gain_part = jnp.sum(grad_query_unit * query_unit, axis=(0, 1))
+    key_gain_part = jnp.sum(grad_key_unit * key_unit, axis=0)
+    grad_query_pre = norm_back(grad_query_unit, query_pre, inv_query, query_gain).astype(bf16)
+    grad_key_pre = norm_back(grad_key_unit, key_pre, inv_key, key_gain).astype(bf16)
+    key_or_value = [
+        jnp.where(odd_c, grad_values, grad_key_pre),
+        jnp.where(odd_c, grad_key_pre, grad_values),
+    ]
+    attn_sides = (attn_mine, attn_other)
+    grad_pre = [
+        jnp.concatenate([grad_query_pre[i], grad_gate_pre[i], key_or_value[i]], axis=1)
+        for i in range(2)
+    ]
+    grad_normed = sum_chunks(
+        sum(contract_last(grad_pre[i], attn_sides[i]) for i in range(2)).astype(bf16)
+    )
+    qk_grad = collect_grad(
+        *(
+            contract_first(
+                normed, jnp.concatenate([grad_query_pre[i], key_or_value[i]], axis=1)
+            ).astype(bf16)
+            for i in range(2)
+        )
+    )
+    input_chunk = (grad_middle + norm_back(grad_normed, hidden32, inv_one, gain_one)).astype(bf16)
+    input_grad = whole_block(input_chunk)
+
+    by_z = jnp.concatenate([wo_gate_grad, qk_grad], axis=-1)
+    kept = jnp.where(odd_c, by_z[:, 2:], by_z[:, :2])
+    taken = pair_swap(jnp.where(odd_c, by_z[:, :2], by_z[:, 2:]), "c")
+    heads = jnp.stack([jnp.where(odd_c, taken, kept), jnp.where(odd_c, kept, taken)], axis=2)
+    heads = heads.reshape(block_rows, 2, 2, 4, HEAD_WIDTH).astype(f32)
+
+    def head_columns(which):
+        return heads[:, :, :, which].reshape(block_rows, 4 * HEAD_WIDTH)
+
+    out_weight_grad, gate_weight_grad, query_weight_grad = (head_columns(i) for i in range(3))
+    key_weight_grad = heads[:, :, 0, 3].reshape(block_rows, 2 * HEAD_WIDTH)
+    value_weight_grad = heads[:, :, 1, 3].reshape(block_rows, 2 * HEAD_WIDTH)
+
+    gains = jnp.concatenate(
+        [
+            from_own_first(jnp.sum(grad_normed * hidden32 * inv_one, axis=0), odd_x),
+            from_own_first(jnp.sum(grad_normed_two * middle * inv_two, axis=0), odd_x),
+            query_gain_part,
+            key_gain_part,
+        ]
+    )
+    gains = (gains + plane_swap(gains, 1)) + (plane_swap(gains, 2) + plane_swap(gains, 3))
+    for axis in ("x", "y", "c"):
+        gains = gains + pair_swap(gains, axis)
+
+    def flat(grad):
+        return grad.reshape(block_rows, -1).astype(f32)
+
+    return (
+        layer_out,
+        input_grad,
+        query_weight_grad,
+        key_weight_grad,
+        value_weight_grad,
+        gate_weight_grad,
+        out_weight_grad,
+        flat(gate_grad),
+        flat(up_grad),
+        flat(down_grad),
+        gains[:width],
+        gains[width : 2 * width],
+        gains[2 * width : 2 * width + HEAD_WIDTH],
+        gains[2 * width + HEAD_WIDTH :],
+    )
+
+
 def solution(mesh):
+    wide, head = mesh.shape["wide"], mesh.shape["head"]
+    if wide == 2 * PLANES and head == 4:
+        devices = mesh.devices.reshape(PLANES, 2, 2, 2)
+        mesh = Mesh(devices, ("z", "x", "y", "c"))
+        program, rows, columns = on_slice_device, ("z", "x"), ("y", "c")
+    else:
+        program, rows, columns = on_device, "wide", "head"
+    tokens, weight = P(rows, None), P(rows, columns)
     return jax.shard_map(
-        on_device,
+        program,
         mesh=mesh,
-        in_specs=(
-            P("wide", None),
-            P("wide", None),
-            P(),
-            P("wide", "head"),
-            P("wide", "head"),
-            P("wide", "head"),
-            P("wide", "head"),
-            P("wide", "head"),
-            P("wide", "head"),
-            P("wide", "head"),
-            P("wide", "head"),
-            P(),
-            P(),
-            P(),
-            P(),
-        ),
-        out_specs=(
-            P("wide", None),
-            P("wide", None),
-            P("wide", "head"),
-            P("wide", "head"),
-            P("wide", "head"),
-            P("wide", "head"),
-            P("wide", "head"),
-            P("wide", "head"),
-            P("wide", "head"),
-            P("wide", "head"),
-            P(),
-            P(),
-            P(),
-            P(),
-        ),
+        in_specs=(tokens, tokens, P()) + (weight,) * 8 + (P(),) * 4,
+        out_specs=(tokens, tokens) + (weight,) * 8 + (P(),) * 4,
         check_vma=False,
     )

time: 1410 us -> 767 us (0.54)
  waiting for transfers between devices: 1150 us -> 346 us
  starting transfers between devices: 2.23 us -> 151 us
  blocking collectives: 43.8 us -> 0 us
  other arithmetic: 39.1 us -> 72.2 us
  local copies, waits for them, and re-layouts: 61.6 us -> 89.8 us
    all_gather x10 -> x0, waiting for transfers between devices: 552 us -> none  [the longest x1 98.1 us: on_device(): lax.all_gather(ffn_up_weight, 'wide', axis=0, tiled=True)]
    reduce_scatter x3 -> x0, waiting for transfers between devices: 498 us -> none  [the longest x1 389 us: on_device(): lax.psum_scatter(jnp.concatenate([contract_first(normed_input, grad_query...]
    ppermute x0 -> x98, waiting for transfers between devices: none -> 301 us  [the longest x65 185 us: pair_swap(): return lax.ppermute(values, axis, [(0, 1), (1, 0)])]
    ppermute x0 -> x98, starting transfers between devices: none -> 114 us  [the longest x33 65.3 us: plane_swap(): return lax.ppermute(values, 'z', [(i, i ^ step) for i in range(PLANES)])]
    psum x3 -> x0, waiting for transfers between devices: 92.1 us -> none  [the longest x1 33.2 us: on_device(): lax.psum((contract_last(grad_ffn_gate, back_ffn_gate) + contract_last(gra...]
    all_to_all x0 -> x9, waiting for transfers between devices: none -> 44.9 us  [the longest x5 28.1 us: collect_grad(): lax.all_to_all(rows.astype(jnp.bfloat16), 'z', split_axis=0, concat_axis=...]
    psum x1 -> x0, blocking collectives: 43.8 us -> none  [on_device(): lax.psum((attn_gain_part * head_first, ffn_gain_part * head_first, query_...]
    all_to_all x0 -> x9, starting transfers between devices: none -> 36.5 us  [the longest x5 19.5 us: collect_grad(): lax.all_to_all(rows.astype(jnp.bfloat16), 'z', split_axis=0, concat_axis=...]
  transfers between devices with their start and end apart: 16 -> 107, of which waited for: 16 -> 46; matrix products, arithmetic and copies ran while one was open for 8% -> 30% of each run, Pallas kernels for 0% -> 0%
where the time goes in v1:
time: 767 us; the launch traced here: 757 us
  waiting for transfers between devices  346 us (45%)
  starting transfers between devices  151 us (20%)
  matrix products  95.2 us (12%)
  local copies, waits for them, and re-layouts  89.8 us (12%)
  other arithmetic  72.2 us (9%)
    ppermute x65, waiting for transfers between devices, pair_swap(): return lax.ppermute(values, axis, [(0, 1), (1, 0)])  185 us
    ppermute x33, waiting for transfers between devices, plane_swap(): return lax.ppermute(values, 'z', [(i, i ^ step) for i in range(PLANES)])  115 us
    ppermute x33, starting transfers between devices, plane_swap(): return lax.ppermute(values, 'z', [(i, i ^ step) for i in range(PLANES)])  65.3 us
    ppermute x65, starting transfers between devices, pair_swap(): return lax.ppermute(values, axis, [(0, 1), (1, 0)])  49.1 us
    unnamed x235, local copies, waits for them, and re-layouts  34 us
    all_to_all x5, waiting for transfers between devices, collect_grad(): lax.all_to_all(rows.astype(jnp.bfloat16), 'z', split_axis=0, concat_axis=...  28.1 us
    dot_general x12, matrix products, contract_last(): lax.dot_general(left, right, (((1,), (1,)), ((), ())), preferred_element_...  27.2 us
    dot_general x12, matrix products, contract_first(): lax.dot_general(left, right, (((0,), (0,)), ((), ())), preferred_element_...  20.6 us
  transfers between devices with their start and end apart: 107, of which 46 were waited for; matrix products, arithmetic and copies ran while one was open for 30% of the time, Pallas kernels for 0%

profile of v1, /device:TPU:0, one launch (start us, length us, event | category | flops | bytes accessed | tf_op | source)
XLA Modules:
  0.0 756.9 jit_solution(9212522972233269744)
XLA Ops:
  36.4 16.7 %all-to-all-done.1 = bf16[256,4,384]{0,2,1:T(8,128)(2,1)S(1)} async-done(((bf16[256,4,384]{0,2,1:T(8,128)(2,1)}), bf16[256,4,384]{0,2,1:T(8,128)(2,1)S(1)}, u32[]{:S(2)}, u32[]{:S(2)}) %all-to-all-start.1) | async-done | bytes 786464 | tf_op jit(solution)/shard_map/all_to_all | solution.py:494
  72.6 6.3 collective-permute-done.47
  82.4 16.3 %collective-permute-start.1 = (bf16[64,2048]{1,0:T(8,128)(2,1)}, bf16[64,2048]{1,0:T(8,128)(2,1)}, u32[]{:S(2)}, u32[]{:S(2)}) collective-permute-start(bf16[64,2048]{1,0:T(8,128)(2,1)} %get-tuple-element.41), channel_id=1, source_target_pairs={{0,16},{8,24},{16,0},{24,8},{1,17},{9,25},{17,1},{25,9},{2,18},{10... | collective-permute-start | bytes 786440 | tf_op jit(solution)/shard_map/ppermute | solution.py:448
  115.2 9.4 %collective-permute-done.1 = bf16[64,2048]{1,0:T(8,128)(2,1)} collective-permute-done((bf16[64,2048]{1,0:T(8,128)(2,1)}, bf16[64,2048]{1,0:T(8,128)(2,1)}, u32[]{:S(2)}, u32[]{:S(2)}) %collective-permute-start.1) | collective-permute-done | bytes 262176 | tf_op jit(solution)/shard_map/ppermute | solution.py:448
  181.2 23.9 %collective-permute-done.31 = bf16[1024,384]{1,0:T(8,128)(2,1)S(1)} collective-permute-done((bf16[1024,384]{1,0:T(8,128)(2,1)}, bf16[1024,384]{1,0:T(8,128)(2,1)S(1)}, u32[]{:S(2)}, u32[]{:S(2)}) %collective-permute-start.31) | collective-permute-done | bytes 786464 | tf_op jit(solution)/shard_map/ppermute | solution.py:444
  208.6 17.7 %collective-permute-done.10 = bf16[512,256]{0,1:T(8,128)(2,1)S(1)} collective-permute-done((bf16[512,256]{0,1:T(8,128)(2,1)S(1)}, bf16[512,256]{0,1:T(8,128)(2,1)S(1)}, u32[]{:S(2)}, u32[]{:S(2)}) %collective-permute-start.10) | collective-permute-done | bytes 262176 | tf_op jit(solution)/shard_map/ppermute | solution.py:444
  288.4 6.3 collective-permute-done.25
  295.2 13.5 %collective-permute-done.24 = bf16[64,2048]{1,0:T(8,128)(2,1)S(1)} collective-permute-done((bf16[64,2048]{1,0:T(8,128)(2,1)S(1)}, bf16[64,2048]{1,0:T(8,128)(2,1)S(1)}, u32[]{:S(2)}, u32[]{:S(2)}) %collective-permute-start.24) | collective-permute-done | bytes 262176 | tf_op jit(solution)/shard_map/ppermute | solution.py:448
  310.8 11.1 %collective-permute-done.28 = bf16[64,2048]{1,0:T(8,128)(2,1)S(1)} collective-permute-done((bf16[64,2048]{1,0:T(8,128)(2,1)S(1)}, bf16[64,2048]{1,0:T(8,128)(2,1)S(1)}, u32[]{:S(2)}, u32[]{:S(2)}) %collective-permute-start.28) | collective-permute-done | bytes 262176 | tf_op jit(solution)/shard_map/ppermute | solution.py:444
  382.5 9.8 %collective-permute-done.56 = bf16[64,2048]{1,0:T(8,128)(2,1)S(1)} collective-permute-done((bf16[64,2048]{1,0:T(8,128)(2,1)S(1)}, bf16[64,2048]{1,0:T(8,128)(2,1)S(1)}, u32[]{:S(2)}, u32[]{:S(2)}) %collective-permute-start.56) | collective-permute-done | bytes 262176 | tf_op jit(solution)/shard_map/ppermute | solution.py:444
  407.3 19.4 %collective-permute-done.53 = bf16[64,2048]{1,0:T(8,128)(2,1)S(1)} collective-permute-done((bf16[64,2048]{1,0:T(8,128)(2,1)S(1)}, bf16[64,2048]{1,0:T(8,128)(2,1)S(1)}, u32[]{:S(2)}, u32[]{:S(2)}) %collective-permute-start.53) | collective-permute-done | bytes 262176 | tf_op jit(solution)/shard_map/ppermute | solution.py:448
  462.3 7.6 %collective-permute-done.61 = bf16[2,64,256]{2,1,0:T(8,128)(2,1)S(1)} collective-permute-done((bf16[2,64,256]{2,1,0:T(8,128)(2,1)S(1)}, bf16[2,64,256]{2,1,0:T(8,128)(2,1)S(1)}, u32[]{:S(2)}, u32[]{:S(2)}) %collective-permute-start.61) | collective-permute-done | bytes 65568 | tf_op jit(solution)/shard_map/ppermute | solution.py:448
  472.7 6.1 fusion.18
  492.1 6.9 collective-permute-done.74
  502.2 6.5 collective-permute-done.76
  510.9 7.1 collective-permute-done.78
  529.0 9.8 %collective-permute-done.44 = bf16[2,64,2048]{2,1,0:T(8,128)(2,1)S(1)} collective-permute-done((bf16[2,64,2048]{2,1,0:T(8,128)(2,1)S(1)}, bf16[2,64,2048]{2,1,0:T(8,128)(2,1)S(1)}, u32[]{:S(2)}, u32[]{:S(2)}) %collective-permute-start.44) | collective-permute-done | bytes 524320 | tf_op jit(solution)/shard_map/ppermute | solution.py:444
  583.1 9.7 %collective-permute-done.66 = bf16[64,2048]{1,0:T(8,128)(2,1)S(1)} collective-permute-done((bf16[64,2048]{1,0:T(8,128)(2,1)S(1)}, bf16[64,2048]{1,0:T(8,128)(2,1)S(1)}, u32[]{:S(2)}, u32[]{:S(2)}) %collective-permute-start.66) | collective-permute-done | bytes 262176 | tf_op jit(solution)/shard_map/ppermute | solution.py:448
  599.3 12.3 %collective-permute-done.82 = bf16[1024,256]{0,1:T(8,128)(2,1)S(1)} collective-permute-done((bf16[1024,256]{0,1:T(8,128)(2,1)S(1)}, bf16[1024,256]{0,1:T(8,128)(2,1)S(1)}, u32[]{:S(2)}, u32[]{:S(2)}) %collective-permute-start.82) | collective-permute-done | bytes 524320 | tf_op jit(solution)/shard_map/ppermute | solution.py:444
  621.3 10.5 %collective-permute-done.93 = f32[4352]{0:T(1024)S(1)} collective-permute-done((f32[4352]{0:T(1024)S(1)}, f32[4352]{0:T(1024)S(1)}, u32[]{:S(2)}, u32[]{:S(2)}) %collective-permute-start.93) | collective-permute-done | bytes 17440 | tf_op jit(solution)/shard_map/ppermute | solution.py:448
  642.6 24.9 %collective-permute-done.95 = f32[4352]{0:T(1024)S(1)} collective-permute-done((f32[4352]{0:T(1024)S(1)}, f32[4352]{0:T(1024)S(1)}, u32[]{:S(2)}, u32[]{:S(2)}) %collective-permute-start.95) | collective-permute-done | bytes 17440 | tf_op jit(solution)/shard_map/ppermute | solution.py:444
  689.8 9.7 %collective-permute-done.84 = bf16[1024,256]{1,0:T(8,128)(2,1)S(1)} collective-permute-done((bf16[1024,256]{1,0:T(8,128)(2,1)S(1)}, bf16[1024,256]{1,0:T(8,128)(2,1)S(1)}, u32[]{:S(2)}, u32[]{:S(2)}) %collective-permute-start.84) | collective-permute-done | bytes 524320 | tf_op jit(solution)/shard_map/ppermute | solution.py:444
  711.1 10.6 %all-to-all-done.5 = bf16[4,256,256]{1,2,0:T(8,128)(2,1)S(1)} async-done(((bf16[4,256,256]{1,2,0:T(8,128)(2,1)}), bf16[4,256,256]{1,2,0:T(8,128)(2,1)S(1)}, u32[]{:S(2)}, u32[]{:S(2)}) %all-to-all-start.5) | async-done | bytes 524320 | tf_op jit(solution)/shard_map/all_to_all | solution.py:506
  731.3 14.2 %all-to-all-done.8 = bf16[4,256,384]{2,1,0:T(8,128)(2,1)} async-done(((bf16[4,256,384]{2,1,0:T(8,128)(2,1)}), bf16[4,256,384]{2,1,0:T(8,128)(2,1)}, u32[]{:S(2)}, u32[]{:S(2)}) %all-to-all-start.8) | async-done | bytes 786464 | tf_op jit(solution)/shard_map/all_to_all | solution.py:506
  (673 shorter events, 467.3 us)
Async XLA Ops:
  0.7 80.5 %collective-permute-start.16 = (bf16[256,512]{1,0:T(8,128)(2,1)}, bf16[256,512]{1,0:T(8,128)(2,1)}, u32[]{:S(2)}, u32[]{:S(2)}) collective-permute-start(bf16[256,512]{1,0:T(8,128)(2,1)} %param.22), channel_id=1, source_target_pairs={{0,8},{8,0},{16,24},{24,16},{1,9},{9,1},{17,25},{25,17},{2,10},{10... | collective-permute-start | bytes 786440 | tf_op jit(solution)/shard_map/ppermute | solution.py:448
  3.7 95.9 %collective-permute-start.18 = (bf16[256,512]{1,0:T(8,128)(2,1)}, bf16[256,512]{1,0:T(8,128)(2,1)}, u32[]{:S(2)}, u32[]{:S(2)}) collective-permute-start(bf16[256,512]{1,0:T(8,128)(2,1)} %param.22), channel_id=1, source_target_pairs={{0,24},{8,16},{16,8},{24,0},{1,25},{9,17},{17,9},{25,1},{2,26},{10... | collective-permute-start | bytes 786440 | tf_op jit(solution)/shard_map/ppermute | solution.py:448
  6.2 76.1 %collective-permute-start.17 = (bf16[256,512]{1,0:T(8,128)(2,1)}, bf16[256,512]{1,0:T(8,128)(2,1)}, u32[]{:S(2)}, u32[]{:S(2)}) collective-permute-start(bf16[256,512]{1,0:T(8,128)(2,1)} %param.22), channel_id=1, source_target_pairs={{0,16},{8,24},{16,0},{24,8},{1,17},{9,25},{17,1},{25,9},{2,18},{10... | collective-permute-start | bytes 786440 | tf_op jit(solution)/shard_map/ppermute | solution.py:448
  21.7 47.7 %collective-permute-start.46 = (bf16[64,2048]{1,0:T(8,128)(2,1)}, bf16[64,2048]{1,0:T(8,128)(2,1)}, u32[]{:S(2)}, u32[]{:S(2)}) collective-permute-start(bf16[64,2048]{1,0:T(8,128)(2,1)} %get-tuple-element.119), channel_id=1, source_target_pairs={{0,16},{8,24},{16,0},{24,8},{1,17},{9,25},{17,1},{25,9},{2,18},{10... | collective-permute-start | bytes 786440 | tf_op jit(solution)/shard_map/ppermute | solution.py:448
  54.0 46.7 %all-to-all-start = ((bf16[256,4,384]{0,2,1:T(8,128)(2,1)}), bf16[256,4,384]{0,2,1:T(8,128)(2,1)}, u32[]{:S(2)}, u32[]{:S(2)}) async-start(bf16[256,4,384]{0,2,1:T(8,128)(2,1)} %pad_maximum_fusion.9), calls=%async_computation | async-start | bytes 1572864 | tf_op jit(solution)/shard_map/all_to_all | solution.py:494
  78.9 49.7 %collective-permute-start.3 = (bf16[64,2048]{1,0:T(8,128)(2,1)}, bf16[64,2048]{1,0:T(8,128)(2,1)}, u32[]{:S(2)}, u32[]{:S(2)}) collective-permute-start(bf16[64,2048]{1,0:T(8,128)(2,1)} %get-tuple-element.41), channel_id=1, source_target_pairs={{0,2},{2,0},{1,3},{3,1},{4,6},{6,4},{5,7},{7,5},{8,10},{10,8},{9,1... | collective-permute-start | bytes 786440 | tf_op jit(solution)/shard_map/ppermute | solution.py:444
  81.2 45.9 %collective-permute-start.2 = (bf16[64,2048]{1,0:T(8,128)(2,1)}, bf16[64,2048]{1,0:T(8,128)(2,1)}, u32[]{:S(2)}, u32[]{:S(2)}) collective-permute-start(bf16[64,2048]{1,0:T(8,128)(2,1)} %get-tuple-element.41), channel_id=1, source_target_pairs={{0,24},{8,16},{16,8},{24,0},{1,25},{9,17},{17,9},{25,1},{2,26},{10... | collective-permute-start | bytes 786440 | tf_op jit(solution)/shard_map/ppermute | solution.py:448
  82.4 42.3 %collective-permute-start.1 = (bf16[64,2048]{1,0:T(8,128)(2,1)}, bf16[64,2048]{1,0:T(8,128)(2,1)}, u32[]{:S(2)}, u32[]{:S(2)}) collective-permute-start(bf16[64,2048]{1,0:T(8,128)(2,1)} %get-tuple-element.41), channel_id=1, source_target_pairs={{0,16},{8,24},{16,0},{24,8},{1,17},{9,25},{17,1},{25,9},{2,18},{10... | collective-permute-start | bytes 786440 | tf_op jit(solution)/shard_map/ppermute | solution.py:448
  105.0 66.1 %collective-permute-start.19 = (bf16[1024,512]{1,0:T(8,128)(2,1)S(1)}, bf16[1024,512]{1,0:T(8,128)(2,1)}, u32[]{:S(2)}, u32[]{:S(2)}) collective-permute-start(bf16[1024,512]{1,0:T(8,128)(2,1)S(1)} %constant_dynamic-update-slice_fusion.41), channel_id=1, source_target_pairs={{0,4},{4,0},{1,5},{5,1},{2,6},{6,2},{3,7},{7,3},{8,12},{12,8},{9,1... | collective-permute-start | bytes 3145736 | tf_op jit(solution)/shard_map/ppermute | solution.py:444
  167.6 71.9 %collective-permute-start.32 = (bf16[1024,384]{1,0:T(8,128)(2,1)}, bf16[1024,384]{1,0:T(8,128)(2,1)}, u32[]{:S(2)}, u32[]{:S(2)}) collective-permute-start(bf16[1024,384]{1,0:T(8,128)(2,1)} %bitcast.274), channel_id=1, source_target_pairs={{0,4},{4,0},{1,5},{5,1},{2,6},{6,2},{3,7},{7,3},{8,12},{12,8},{9,1... | collective-permute-start | bytes 2359304 | tf_op jit(solution)/shard_map/ppermute | solution.py:444
  169.6 79.5 %collective-permute-start.30 = (bf16[1024,384]{1,0:T(8,128)(2,1)}, bf16[1024,384]{1,0:T(8,128)(2,1)}, u32[]{:S(2)}, u32[]{:S(2)}) collective-permute-start(bf16[1024,384]{1,0:T(8,128)(2,1)} %bitcast.266), channel_id=1, source_target_pairs={{0,4},{4,0},{1,5},{5,1},{2,6},{6,2},{3,7},{7,3},{8,12},{12,8},{9,1... | collective-permute-start | bytes 2359304 | tf_op jit(solution)/shard_map/ppermute | solution.py:444
  173.8 99.2 %collective-permute-start.20 = (bf16[2048,512]{1,0:T(8,128)(2,1)}, bf16[2048,512]{1,0:T(8,128)(2,1)}, u32[]{:S(2)}, u32[]{:S(2)}) collective-permute-start(bf16[2048,512]{1,0:T(8,128)(2,1)} %pad_maximum_fusion), channel_id=1, source_target_pairs={{0,1},{1,0},{2,3},{3,2},{4,5},{5,4},{6,7},{7,6},{8,9},{9,8},{10,11... | collective-permute-start | bytes 6291464 | tf_op jit(solution)/shard_map/ppermute | solution.py:444
  176.0 65.7 %collective-permute-start.21 = (bf16[2048,512]{1,0:T(8,128)(2,1)}, bf16[2048,512]{1,0:T(8,128)(2,1)}, u32[]{:S(2)}, u32[]{:S(2)}) collective-permute-start(bf16[2048,512]{1,0:T(8,128)(2,1)} %pad_maximum_fusion), channel_id=1, source_target_pairs={{0,2},{2,0},{1,3},{3,1},{4,6},{6,4},{5,7},{7,5},{8,10},{10,8},{9,1... | collective-permute-start | bytes 6291464 | tf_op jit(solution)/shard_map/ppermute | solution.py:444
  246.2 89.6 %collective-permute-start.34 = (bf16[2048,384]{1,0:T(8,128)(2,1)}, bf16[2048,384]{1,0:T(8,128)(2,1)}, u32[]{:S(2)}, u32[]{:S(2)}) collective-permute-start(bf16[2048,384]{1,0:T(8,128)(2,1)} %pad_maximum_fusion.3), channel_id=1, source_target_pairs={{0,1},{1,0},{2,3},{3,2},{4,5},{5,4},{6,7},{7,6},{8,9},{9,8},{10,11... | collective-permute-start | bytes 4718600 | tf_op jit(solution)/shard_map/ppermute | solution.py:444
  256.4 82.1 %collective-permute-start.33 = (bf16[2048,384]{1,0:T(8,128)(2,1)}, bf16[2048,384]{1,0:T(8,128)(2,1)}, u32[]{:S(2)}, u32[]{:S(2)}) collective-permute-start(bf16[2048,384]{1,0:T(8,128)(2,1)} %pad_maximum_fusion.2), channel_id=1, source_target_pairs={{0,1},{1,0},{2,3},{3,2},{4,5},{5,4},{6,7},{7,6},{8,9},{9,8},{10,11... | collective-permute-start | bytes 4718600 | tf_op jit(solution)/shard_map/ppermute | solution.py:444
  349.9 48.0 %collective-permute-start.42 = (bf16[64,2048]{1,0:T(8,128)(2,1)S(1)}, bf16[64,2048]{1,0:T(8,128)(2,1)S(1)}, u32[]{:S(2)}, u32[]{:S(2)}) collective-permute-start(bf16[64,2048]{1,0:T(8,128)(2,1)S(1)} %get-tuple-element.60), channel_id=1, source_target_pairs={{0,2},{2,0},{1,3},{3,1},{4,6},{6,4},{5,7},{7,5},{8,10},{10,8},{9,1... | collective-permute-start | bytes 786440 | tf_op jit(solution)/shard_map/ppermute | solution.py:444
  404.9 148.4 %collective-permute-start.88 = (bf16[2048,384]{1,0:T(8,128)(2,1)}, bf16[2048,384]{1,0:T(8,128)(2,1)}, u32[]{:S(2)}, u32[]{:S(2)}) collective-permute-start(bf16[2048,384]{1,0:T(8,128)(2,1)} %convolution_convert_fusion.2), channel_id=1, source_target_pairs={{0,1},{1,0},{2,3},{3,2},{4,5},{5,4},{6,7},{7,6},{8,9},{9,8},{10,11... | collective-permute-start | bytes 4718600 | tf_op jit(solution)/shard_map/ppermute | solution.py:444
  407.3 149.1 %collective-permute-start.86 = (bf16[2048,384]{1,0:T(8,128)(2,1)}, bf16[2048,384]{1,0:T(8,128)(2,1)}, u32[]{:S(2)}, u32[]{:S(2)}) collective-permute-start(bf16[2048,384]{1,0:T(8,128)(2,1)} %convolution_convert_fusion.4), channel_id=1, source_target_pairs={{0,1},{1,0},{2,3},{3,2},{4,5},{5,4},{6,7},{7,6},{8,9},{9,8},{10,11... | collective-permute-start | bytes 4718600 | tf_op jit(solution)/shard_map/ppermute | solution.py:444
  458.9 100.2 %collective-permute-start.90 = (bf16[2048,384]{1,0:T(8,128)(2,1)}, bf16[2048,384]{1,0:T(8,128)(2,1)}, u32[]{:S(2)}, u32[]{:S(2)}) collective-permute-start(bf16[2048,384]{1,0:T(8,128)(2,1)} %convolution_convert_fusion), channel_id=1, source_target_pairs={{0,1},{1,0},{2,3},{3,2},{4,5},{5,4},{6,7},{7,6},{8,9},{9,8},{10,11... | collective-permute-start | bytes 4718600 | tf_op jit(solution)/shard_map/ppermute | solution.py:444
  528.7 50.2 %collective-permute-start.81 = (bf16[2048,256]{0,1:T(8,128)(2,1)S(1)}, bf16[2048,256]{0,1:T(8,128)(2,1)S(1)}, u32[]{:S(2)}, u32[]{:S(2)}) collective-permute-start(bf16[2048,256]{0,1:T(8,128)(2,1)S(1)} %pad_maximum_fusion.8), channel_id=1, source_target_pairs={{0,1},{1,0},{2,3},{3,2},{4,5},{5,4},{6,7},{7,6},{8,9},{9,8},{10,11... | collective-permute-start | bytes 3145736 | tf_op jit(solution)/shard_map/ppermute | solution.py:444
  547.9 135.6 %collective-permute-start.83 = (bf16[2048,256]{1,0:T(8,128)(2,1)}, bf16[2048,256]{1,0:T(8,128)(2,1)}, u32[]{:S(2)}, u32[]{:S(2)}) collective-permute-start(bf16[2048,256]{1,0:T(8,128)(2,1)} %convolution_convert_fusion.6), channel_id=1, source_target_pairs={{0,1},{1,0},{2,3},{3,2},{4,5},{5,4},{6,7},{7,6},{8,9},{9,8},{10,11... | collective-permute-start | bytes 3145736 | tf_op jit(solution)/shard_map/ppermute | solution.py:444
  581.8 53.7 %collective-permute-start.89 = (bf16[1024,384]{1,0:T(8,128)(2,1)}, bf16[1024,384]{1,0:T(8,128)(2,1)}, u32[]{:S(2)}, u32[]{:S(2)}) collective-permute-start(bf16[1024,384]{1,0:T(8,128)(2,1)} %slice.593), channel_id=1, source_target_pairs={{0,4},{4,0},{1,5},{5,1},{2,6},{6,2},{3,7},{7,3},{8,12},{12,8},{9,1... | collective-permute-start | bytes 2359304 | tf_op jit(solution)/shard_map/ppermute | solution.py:444
  631.7 45.1 %collective-permute-start.87 = (bf16[1024,384]{1,0:T(8,128)(2,1)}, bf16[1024,384]{1,0:T(8,128)(2,1)}, u32[]{:S(2)}, u32[]{:S(2)}) collective-permute-start(bf16[1024,384]{1,0:T(8,128)(2,1)} %slice.591), channel_id=1, source_target_pairs={{0,4},{4,0},{1,5},{5,1},{2,6},{6,2},{3,7},{7,3},{8,12},{12,8},{9,1... | collective-permute-start | bytes 2359304 | tf_op jit(solution)/shard_map/ppermute | solution.py:444
  633.4 74.3 %collective-permute-start.91 = (bf16[1024,384]{1,0:T(8,128)(2,1)}, bf16[1024,384]{1,0:T(8,128)(2,1)}, u32[]{:S(2)}, u32[]{:S(2)}) collective-permute-start(bf16[1024,384]{1,0:T(8,128)(2,1)} %slice.595), channel_id=1, source_target_pairs={{0,4},{4,0},{1,5},{5,1},{2,6},{6,2},{3,7},{7,3},{8,12},{12,8},{9,1... | collective-permute-start | bytes 2359304 | tf_op jit(solution)/shard_map/ppermute | solution.py:444
  (179 other events, 2995.8 us)

commit v2 on v1

--- a/solution.py
+++ b/solution.py
@@ -438,6 +438,7 @@
 
 
 PLANES = 4
+PLANE = ("far", "x")
 
 
 def pair_swap(values, axis):
@@ -445,25 +446,59 @@
 
 
 def plane_swap(values, step):
-    return lax.ppermute(values, "z", [(i, i ^ step) for i in range(PLANES)])
+    return lax.ppermute(values, PLANE, [(i, i ^ step) for i in range(PLANES)])
+
+
+def side_swap(values, step):
+    return lax.ppermute(values, ("x", "y"), [(i, i ^ step) for i in range(4)])
+
+
+def after(values, *done):
+    return lax.optimization_barrier((values, done))[0]
 
 
 def gather_chunks(chunk):
-    columns = [chunk] + [plane_swap(chunk, step) for step in range(1, PLANES)]
-    return jnp.concatenate(columns + [pair_swap(piece, "y") for piece in columns], axis=0)
-
-
-def sum_chunks(parts):
-    rows = parts.shape[0] // (2 * PLANES)
-    total = None
-    for step in (2, 3, 1, 0):
-        other = PLANES + step
-        got = pair_swap(parts[other * rows : (other + 1) * rows], "y")
-        both = parts[step * rows : (step + 1) * rows].astype(jnp.float32) + got.astype(jnp.float32)
-        if step:
-            both = plane_swap(both.astype(jnp.bfloat16), step).astype(jnp.float32)
-        total = both if total is None else total + both
+    far = pair_swap(chunk, "far")
+    near = [side_swap(chunk, step) for step in range(1, 4)]
+    away = [side_swap(far, step) for step in range(1, 4)]
+    pieces = [chunk, far]
+    for pair in zip(near, away):
+        pieces.extend(pair)
+    return jnp.concatenate(pieces, axis=0)
+
+
+def sum_sends(parts):
+    rows = parts.shape[0] // 8
+
+    def part(step, far):
+        return parts[(2 * step + far) * rows : (2 * step + far + 1) * rows]
+
+    return [
+        [part(0, far)] + [side_swap(part(step, far), step) for step in range(1, 4)]
+        for far in (1, 0)
+    ]
+
+
+def sum_pieces(pieces):
+    total = pieces[0].astype(jnp.float32)
+    for piece in pieces[1:]:
+        total = total + piece.astype(jnp.float32)
     return total
+
+
+def sum_sends_paired(parts):
+    rows = parts.shape[0] // 4
+    return [parts[:rows]] + [
+        side_swap(parts[step * rows : (step + 1) * rows], step) for step in range(1, 4)
+    ]
+
+
+def sum_chunks(parts, *due):
+    away, own = sum_sends(parts)
+    away = sum_pieces(away).astype(jnp.bfloat16)
+    if due:
+        away = after(away, *due)
+    return sum_pieces(own + [pair_swap(away, "far")])
 
 
 def flip_if(values, axis, flag):
@@ -473,7 +508,7 @@
 def to_own_first(values, flag):
     lead = values.shape[:-1]
     width = values.shape[-1]
-    split = values.reshape(lead + (PLANES, 2, width // (2 * PLANES)))
+    split = values.reshape(lead + (2, 2, width // 4))
     zero = split[..., 0, :].reshape(lead + (width // 2,))
     one = split[..., 1, :].reshape(lead + (width // 2,))
     return jnp.concatenate([jnp.where(flag, one, zero), jnp.where(flag, zero, one)], axis=-1)
@@ -482,31 +517,37 @@
 def from_own_first(values, flag):
     lead = values.shape[:-1]
     width = values.shape[-1]
-    block = width // (2 * PLANES)
-    own = values[..., : width // 2].reshape(lead + (PLANES, block))
-    other = values[..., width // 2 :].reshape(lead + (PLANES, block))
+    own = values[..., : width // 2].reshape(lead + (2, width // 4))
+    other = values[..., width // 2 :].reshape(lead + (2, width // 4))
     pair = jnp.stack([jnp.where(flag, other, own), jnp.where(flag, own, other)], axis=-2)
     return pair.reshape(lead + (width,))
 
 
-def spread_weight(local):
-    rows, planes, width = local.shape
-    mine = lax.all_to_all(
-        local.reshape(rows, planes * width), "z", split_axis=1, concat_axis=0, tiled=True
-    )
-    mine = jnp.concatenate([mine, pair_swap(mine, "x")], axis=0)
+def to_plane_owners(local):
+    planes, rows, width = local.shape
+    return lax.all_to_all(
+        local.reshape(planes * rows, width), PLANE, split_axis=0, concat_axis=0, tiled=True
+    )
+
+
+def with_near_and_core(mine, other):
+    mine = jnp.concatenate([mine, other], axis=0)
     return mine, pair_swap(mine, "c")
 
 
-def collect_grad(mine, other):
-    half = mine.shape[0] // 2
+def core_sum(mine, other):
     both = mine.astype(jnp.float32) + pair_swap(other, "c").astype(jnp.float32)
-    both = both.astype(jnp.bfloat16)
-    rows = both[:half].astype(jnp.float32) + pair_swap(both[half:], "x").astype(jnp.float32)
-    back = lax.all_to_all(
-        rows.astype(jnp.bfloat16), "z", split_axis=0, concat_axis=1, tiled=True
-    )
-    return back.reshape(half // PLANES, PLANES, mine.shape[1])
+    return both.astype(jnp.bfloat16)
+
+
+def near_add(both, got):
+    half = both.shape[0] // 2
+    return (both[:half].astype(jnp.float32) + got.astype(jnp.float32)).astype(jnp.bfloat16)
+
+
+def to_row_owners(rows):
+    back = lax.all_to_all(rows, PLANE, split_axis=0, concat_axis=0, tiled=True)
+    return back.reshape(PLANES, rows.shape[0] // PLANES, rows.shape[1])
 
 
 def head_norm(pre, gain):
@@ -535,44 +576,70 @@
     bf16, f32 = jnp.bfloat16, jnp.float32
     block_rows, width = hidden_in.shape
     chunk_rows = block_rows // 4
-    z, x, y, c = (lax.axis_index(name) for name in ("z", "x", "y", "c"))
-    odd_x, odd_c = x == 1, c == 1
+    far, near, x, y, c = (lax.axis_index(name) for name in ("far", "near", "x", "y", "c"))
+    odd_near, odd_c = near == 1, c == 1
     score_scale = HEAD_WIDTH ** (-0.5)
 
-    def by_head(weight, inner):
-        return weight.reshape(block_rows, 2, inner, HEAD_WIDTH)
-
-    queries, gates = by_head(query_weight, 2), by_head(gate_weight, 2)
-    keys, vals = by_head(key_matrix, 1), by_head(value_matrix, 1)
-    half_zero = jnp.concatenate([queries[:, :, 0], gates[:, :, 0], keys[:, :, 0]], axis=-1)
-    half_one = jnp.concatenate([queries[:, :, 1], gates[:, :, 1], vals[:, :, 0]], axis=-1)
+    def heads_of(weight, which, group):
+        width = weight.shape[1] // 2
+        start = which * HEAD_WIDTH if group == 2 else 0
+        return [weight[:, i * width + start : i * width + start + HEAD_WIDTH] for i in range(2)]
+
+    def halves(which):
+        third = key_matrix if which == 0 else value_matrix
+        columns = [
+            heads_of(query_weight, which, 2),
+            heads_of(third, which, 1),
+            heads_of(gate_weight, which, 2),
+            heads_of(out_weight, which, 2),
+        ]
+        return jnp.stack([jnp.concatenate([col[i] for col in columns], axis=1) for i in range(2)])
+
+    half_zero, half_one = halves(0), halves(1)
     kept = jnp.where(odd_c, half_one, half_zero)
     taken = pair_swap(jnp.where(odd_c, half_zero, half_one), "c")
     attn_local = jnp.concatenate(
-        [jnp.where(odd_c, taken, kept), jnp.where(odd_c, kept, taken)], axis=1
-    )
-    attn_mine, attn_other = spread_weight(attn_local)
+        [jnp.where(odd_c, taken, kept), jnp.where(odd_c, kept, taken)], axis=0
+    )
+    low, high = HEAD_WIDTH, 2 * HEAD_WIDTH
+    qk_half = to_plane_owners(attn_local[:, :, :high])
+    qk_mine, qk_other = with_near_and_core(qk_half, pair_swap(qk_half, "near"))
 
     chunk_start = (y * 2 + c) * chunk_rows
     own_hidden = lax.dynamic_slice_in_dim(hidden_in, chunk_start, chunk_rows, 0)
-    own_cotangent = lax.dynamic_slice_in_dim(out_cotangent, chunk_start, chunk_rows, 0)
-    hidden32 = to_own_first(own_hidden, odd_x).astype(f32)
-    cotangent = to_own_first(own_cotangent, odd_x)
-    gain_one = to_own_first(attn_gain, odd_x)
-    gain_two = to_own_first(ffn_gain, odd_x)
+    hidden32 = to_own_first(own_hidden, odd_near).astype(f32)
+    gain_one = to_own_first(attn_gain, odd_near)
     inv_one = lax.rsqrt(jnp.mean(hidden32 * hidden32, axis=1, keepdims=True) + epsilon)
     normed_chunk = (hidden32 * inv_one * gain_one).astype(bf16)
     normed = gather_chunks(normed_chunk)
+
+    (
+        (out_cotangent, ffn_gain, doc_lengths, ffn_gate_weight, ffn_up_weight, ffn_down_weight),
+        (far, near, x, y, c),
+    ) = after(
+        (
+            (out_cotangent, ffn_gain, doc_lengths, ffn_gate_weight, ffn_up_weight, ffn_down_weight),
+            (far, near, x, y, c),
+        ),
+        attn_local,
+        normed_chunk,
+    )
+    odd_near, odd_c = near == 1, c == 1
+    own_cotangent = lax.dynamic_slice_in_dim(
+        out_cotangent, (y * 2 + c) * chunk_rows, chunk_rows, 0
+    )
+    cotangent = to_own_first(own_cotangent, odd_near)
+    gain_two = to_own_first(ffn_gain, odd_near)
     tokens = normed.shape[0]
 
-    def ids_of(x_at, c_at):
-        step = jnp.arange(2 * PLANES, dtype=jnp.int32)
-        z_at, y_at = z ^ (step % PLANES), y ^ (step // PLANES)
-        start = (z_at * 2 + x_at) * block_rows + (y_at * 2 + c_at) * chunk_rows
+    def ids_of(near_at, c_at):
+        step = jnp.arange(8, dtype=jnp.int32)
+        x_at, y_at, far_at = x ^ (step // 4), y ^ (step // 2 % 2), far ^ (step % 2)
+        start = ((far_at * 2 + near_at) * 2 + x_at) * block_rows + (y_at * 2 + c_at) * chunk_rows
         return (start[:, None] + jnp.arange(chunk_rows, dtype=jnp.int32)[None, :]).reshape(-1)
 
-    query_ids = ids_of(x, c)
-    key_ids = jnp.concatenate([query_ids, ids_of(x ^ 1, c), ids_of(x, c ^ 1), ids_of(x ^ 1, c ^ 1)])
+    query_ids = ids_of(near, c)
+    key_ids = jnp.concatenate([query_ids, ids_of(near ^ 1, c), ids_of(near, c ^ 1), ids_of(near ^ 1, c ^ 1)])
     query_seg, positions = doc_tables(doc_lengths, query_ids)
     key_seg = segment_of(doc_lengths, key_ids)
     cos_table, sin_table = rope_tables(positions, HEAD_WIDTH)
@@ -584,21 +651,44 @@
     def turn_back(grads):
         return grads * cos_rows + rotate_back(grads * sin_rows)
 
-    mine = jnp.dot(normed, attn_mine, preferred_element_type=f32)
-    other = jnp.dot(normed, attn_other, preferred_element_type=f32)
-    low, high = HEAD_WIDTH, 2 * HEAD_WIDTH
-    key_pre = jnp.where(odd_c, other[:, high:], mine[:, high:])
-    value_rows = jnp.where(odd_c, mine[:, high:], other[:, high:]).astype(bf16)
+    mine = jnp.dot(normed, qk_mine, preferred_element_type=f32)
+    other = jnp.dot(normed, qk_other, preferred_element_type=f32)
+    key_pre = jnp.where(odd_c, other[:, low:], mine[:, low:])
+    value_rows = jnp.where(odd_c, mine[:, low:], other[:, low:]).astype(bf16)
     inv_key, key_unit, key_scaled = head_norm(key_pre, key_gain)
     key_rows = turn(key_scaled).astype(bf16)
     pair = jnp.concatenate([key_rows, value_rows], axis=1)
-    pair_x = pair_swap(pair, "x")
-    both_x = jnp.concatenate([pair, pair_x], axis=0)
-    all_pairs = jnp.concatenate([both_x, pair_swap(both_x, "c")], axis=0)
+    pair_near = pair_swap(pair, "near")
+    both_near = jnp.concatenate([pair, pair_near], axis=0)
+    all_pairs = jnp.concatenate([both_near, pair_swap(both_near, "c")], axis=0)
     all_keys, all_values = all_pairs[:, :low], all_pairs[:, low:]
 
+    def by_plane(*weights):
+        step = weights[0].shape[1] // PLANES
+        return jnp.stack(
+            [
+                jnp.concatenate([w[:, p * step : (p + 1) * step] for w in weights], axis=1)
+                for p in range(PLANES)
+            ]
+        )
+
+    units = ffn_gate_weight.shape[1] // PLANES
+    og_half = to_plane_owners(after(attn_local[:, :, high:], qk_half))
+    og_near = pair_swap(after(og_half, pair_near), "near")
+    og_mine, og_other = with_near_and_core(og_half, og_near)
+    gate_up_half = to_plane_owners(after(by_plane(ffn_gate_weight, ffn_up_weight), og_half, pair))
+    cotangent_far = pair_swap(after(cotangent, qk_half), "far")
+    cotangent_pair = after(jnp.concatenate([cotangent, cotangent_far], axis=0), pair_near)
+    cotangent_pieces = [cotangent_pair] + [side_swap(cotangent_pair, i) for i in range(1, 4)]
+
     query_pre = jnp.stack([mine[:, :low], other[:, :low]])
-    gate_pre = jnp.stack([mine[:, low:high], other[:, low:high]])
+    gate_pre = jnp.stack(
+        [
+            jnp.dot(normed, side[:, :low], preferred_element_type=f32)
+            for side in (og_mine, og_other)
+        ]
+    )
+    out_sides = (og_mine[:, low:], og_other[:, low:])
     inv_query, query_unit, query_scaled = head_norm(query_pre, query_gain)
     query_rot = turn(query_scaled).astype(bf16)
 
@@ -616,59 +706,21 @@
     gate_sig = jax.nn.sigmoid(gate_pre)
     gated = (attended * gate_sig).astype(bf16)
 
-    out_rows = [out_weight] + [plane_swap(out_weight, step) for step in range(1, PLANES)]
-    out_plane = jnp.zeros((PLANES * block_rows, out_weight.shape[1]), bf16)
-    for step in range(PLANES):
-        out_plane = lax.dynamic_update_slice_in_dim(
-            out_plane, out_rows[step], (z ^ step) * block_rows, 0
-        )
-    out_here = jnp.concatenate([out_plane, pair_swap(out_plane, "x")], axis=0)
-    out_y = pair_swap(out_here, "y")
-    out_blocks = [[out_here, pair_swap(out_here, "c")], [out_y, pair_swap(out_y, "c")]]
-
-    flip_hi, flip_lo = (z // 2) != c, (z % 2) == 1
-
-    def to_blocks(pieces):
-        tiles = pieces.reshape(2, 2, 2, chunk_rows, 2, HEAD_WIDTH)
-        tiles = flip_if(flip_if(flip_if(tiles, 1, flip_hi), 2, flip_lo), 4, odd_c)
-        return tiles.transpose(0, 1, 3, 2, 4, 5).reshape(2, 2, chunk_rows, 4 * HEAD_WIDTH)
-
-    def from_blocks(blocks):
-        tiles = blocks.reshape(2, 2, chunk_rows, 2, 2, HEAD_WIDTH).transpose(0, 1, 3, 2, 4, 5)
-        tiles = flip_if(flip_if(flip_if(tiles, 1, flip_hi), 2, flip_lo), 4, odd_c)
-        return tiles.reshape(2, PLANES, chunk_rows, 2 * HEAD_WIDTH)
-
-    def to_owner(rows):
-        tiles = rows.reshape(2, PLANES, chunk_rows, 2 * HEAD_WIDTH)
-        tiles = jnp.stack(
-            [tiles[:, 0]] + [plane_swap(tiles[:, step], step) for step in range(1, PLANES)], axis=1
-        )
-        return jnp.stack([tiles[0], pair_swap(tiles[1], "y")])
-
-    def from_owner(tiles):
-        tiles = jnp.stack([tiles[0], pair_swap(tiles[1], "y")])
-        tiles = jnp.stack(
-            [tiles[:, 0]] + [plane_swap(tiles[:, step], step) for step in range(1, PLANES)], axis=1
-        )
-        return tiles.reshape(tokens, 2 * HEAD_WIDTH)
-
-    gated_rows = jnp.concatenate([gated[0], gated[1]], axis=1)
-    gated_blocks = to_blocks(to_owner(gated_rows))
-    branch = sum(
-        contract_last(gated_blocks[i, j], out_blocks[i][j]) for i in range(2) for j in range(2)
-    )
+    branch_parts = sum(contract_last(gated[i], out_sides[i]) for i in range(2)).astype(bf16)
+    gate_up_near = pair_swap(after(gate_up_half, og_near, branch_parts), "near")
+    down_half = to_plane_owners(after(by_plane(ffn_down_weight), gate_up_half))
+    branch = sum_chunks(branch_parts, gate_up_half)
     middle = hidden32 + branch
     inv_two = lax.rsqrt(jnp.mean(middle * middle, axis=1, keepdims=True) + epsilon)
     normed_two_chunk = (middle * inv_two * gain_two).astype(bf16)
+    normed_two_chunk, gate_up_near, down_half = after((normed_two_chunk, gate_up_near, down_half))
     normed_two = gather_chunks(normed_two_chunk)
-
-    def by_plane(weight):
-        return weight.reshape(block_rows, PLANES, weight.shape[1] // PLANES)
-
-    ffn_gate = spread_weight(by_plane(ffn_gate_weight))
-    ffn_up = spread_weight(by_plane(ffn_up_weight))
-    ffn_down = spread_weight(by_plane(ffn_down_weight))
-    all_cotangent = gather_chunks(cotangent)
+    gate_up = with_near_and_core(gate_up_half, gate_up_near)
+    ffn_down = with_near_and_core(down_half, pair_swap(down_half, "near"))
+    ffn_gate = [part[:, :units] for part in gate_up]
+    ffn_up = [part[:, units:] for part in gate_up]
+    all_cotangent = jnp.concatenate(after(cotangent_pieces, normed_two_chunk), axis=0)
+
     hidden_acts, grads_gate, grads_up = [], [], []
     for side in range(2):
         ffn_gate_pre = jnp.dot(normed_two, ffn_gate[side], preferred_element_type=f32)
@@ -681,62 +733,36 @@
             (grad_act * ffn_up_pre * gate_act * (1.0 + ffn_gate_pre * (1.0 - gate_act))).astype(bf16)
         )
         grads_up.append((grad_act * silu_gate).astype(bf16))
-    grad_normed_two = sum_chunks(
-        sum(
-            contract_last(grads_gate[side], ffn_gate[side])
-            + contract_last(grads_up[side], ffn_up[side])
-            for side in range(2)
-        ).astype(bf16)
-    )
-    ffn_out = sum_chunks(
-        sum(contract_last(hidden_acts[side], ffn_down[side]) for side in range(2)).astype(bf16)
-    )
-    layer_chunk = (middle + ffn_out).astype(bf16)
+    grad_ffn = [jnp.concatenate([grads_gate[i], grads_up[i]], axis=1) for i in range(2)]
+    grad_two_parts = sum(contract_last(grad_ffn[i], gate_up[i]) for i in range(2)).astype(bf16)
+    grad_normed_two = sum_chunks(grad_two_parts)
+    hidden_acts, all_cotangent, grad_ffn = after(
+        (hidden_acts, all_cotangent, grad_ffn), grad_two_parts
+    )
+    down_parts = sum(contract_last(hidden_acts[i], ffn_down[i]) for i in range(2)).astype(bf16)
+    down_both = core_sum(*(contract_first(all_cotangent, act).astype(bf16) for act in hidden_acts))
+    gate_up_both = core_sum(*(contract_first(normed_two, g).astype(bf16) for g in grad_ffn))
 
     def whole_block(chunk):
-        chunk = from_own_first(chunk, odd_x)
-        by_core = jnp.stack([chunk, pair_swap(chunk, "c")])
-        by_core = flip_if(by_core, 0, odd_c)
-        by_y = jnp.stack([by_core, pair_swap(by_core, "y")])
-        return flip_if(by_y, 0, y == 1).reshape(block_rows, width)
-
-    layer_out = whole_block(layer_chunk)
-    down_grad = collect_grad(
-        *(contract_first(all_cotangent, act).astype(bf16) for act in hidden_acts)
-    )
-    gate_grad = collect_grad(*(contract_first(normed_two, g).astype(bf16) for g in grads_gate))
-    up_grad = collect_grad(*(contract_first(normed_two, g).astype(bf16) for g in grads_up))
+        chunk = from_own_first(chunk, odd_near)
+        by_y = jnp.stack([chunk, pair_swap(chunk, "y")])
+        by_core = jnp.stack([by_y, pair_swap(by_y, "c")], axis=1)
+        return flip_if(flip_if(by_core, 1, odd_c), 0, y == 1).reshape(block_rows, width)
 
     grad_middle = cotangent.astype(f32) + norm_back(grad_normed_two, middle, inv_two, gain_two)
     grad_branch = grad_middle.astype(bf16)
-    grad_blocks = jnp.stack(
-        [
-            jnp.stack(
-                [
-                    jnp.dot(grad_branch, out_blocks[i][j], preferred_element_type=f32).astype(bf16)
-                    for j in range(2)
-                ]
-            )
-            for i in range(2)
-        ]
-    )
-    grad_gated_rows = from_owner(from_blocks(grad_blocks)).astype(f32)
-    grad_gated = jnp.stack([grad_gated_rows[:, :low], grad_gated_rows[:, low:]])
+    grad_branch, down_both, gate_up_both, down_parts = lax.optimization_barrier(
+        (grad_branch, down_both, gate_up_both, down_parts)
+    )
+    all_grad_branch = gather_chunks(grad_branch)
+    grad_gated = jnp.stack(
+        [jnp.dot(all_grad_branch, side, preferred_element_type=f32) for side in out_sides]
+    )
+    down_pieces = sum_sends_paired(after(down_parts, all_grad_branch))
+    gate_up_got = pair_swap(gate_up_both[gate_up_both.shape[0] // 2 :], "near")
+    down_got = pair_swap(down_both[down_both.shape[0] // 2 :], "near")
     grad_attended = (grad_gated * gate_sig).astype(bf16)
     grad_gate_pre = (grad_gated * attended * gate_sig * (1.0 - gate_sig)).astype(bf16)
-    all_grad_branch = gather_chunks(grad_branch)
-    wo_gate_grad = collect_grad(
-        *(
-            jnp.concatenate(
-                [
-                    contract_first(all_grad_branch, gated[i]).astype(bf16),
-                    contract_first(normed, grad_gate_pre[i]).astype(bf16),
-                ],
-                axis=1,
-            )
-            for i in range(2)
-        )
-    )
 
     delta = jnp.sum(grad_attended.astype(f32) * attended, axis=-1, keepdims=True)
     weights = jnp.exp(scores - log_total)
@@ -752,11 +778,36 @@
         "hqk,hqd->kd", weights.astype(bf16), grad_attended, preferred_element_type=f32
     )
     grad_pairs = jnp.concatenate([grad_keys, grad_vals], axis=1).astype(bf16)
-    near = grad_pairs[: 2 * tokens].astype(f32) + pair_swap(grad_pairs[2 * tokens :], "c").astype(
-        f32
-    )
-    near = near.astype(bf16)
-    own_pair = near[:tokens].astype(f32) + pair_swap(near[tokens:], "x").astype(f32)
+    pair_other = pair_swap(grad_pairs[2 * tokens :], "c")
+    down_pieces, gate_up_got, down_got, normed_late, branch_late = after(
+        (down_pieces, gate_up_got, down_got, normed, all_grad_branch), grad_pairs
+    )
+    near_pairs = grad_pairs[: 2 * tokens].astype(f32) + pair_other.astype(f32)
+    near_pairs = near_pairs.astype(bf16)
+    pair_got = pair_swap(near_pairs[tokens:], "near")
+    gate_up_rows, down_rows = near_add(gate_up_both, gate_up_got), near_add(down_both, down_got)
+    gate_up_grad = to_row_owners(gate_up_rows)
+    down_grad = to_row_owners(after(down_rows, gate_up_grad))
+    down_sums = sum_pieces(down_pieces)
+    ffn_out_far = pair_swap(down_sums[chunk_rows:].astype(bf16), "far")
+    og_both = core_sum(
+        *(
+            jnp.concatenate(
+                [
+                    contract_first(normed_late, grad_gate_pre[i]).astype(bf16),
+                    contract_first(branch_late, gated[i]).astype(bf16),
+                ],
+                axis=1,
+            )
+            for i in range(2)
+        )
+    )
+    pair_got, gate_up_rows, down_rows, down_sums = after(
+        (pair_got, gate_up_rows, down_rows, down_sums)
+    )
+    own_pair = near_pairs[:tokens].astype(f32) + pair_got.astype(f32)
+    og_both = after(og_both, own_pair)
+    og_got = pair_swap(og_both[og_both.shape[0] // 2 :], "near")
     grad_key_unit = turn_back(own_pair[:, :low].astype(bf16).astype(f32))
     grad_values = own_pair[:, low:].astype(bf16)
     grad_query_unit = turn_back(grad_query_rot.astype(bf16).astype(f32))
@@ -768,52 +819,57 @@
         jnp.where(odd_c, grad_values, grad_key_pre),
         jnp.where(odd_c, grad_key_pre, grad_values),
     ]
-    attn_sides = (attn_mine, attn_other)
-    grad_pre = [
-        jnp.concatenate([grad_query_pre[i], grad_gate_pre[i], key_or_value[i]], axis=1)
-        for i in range(2)
+    grad_qk = [
+        jnp.concatenate([grad_query_pre[i], key_or_value[i]], axis=1) for i in range(2)
     ]
-    grad_normed = sum_chunks(
-        sum(contract_last(grad_pre[i], attn_sides[i]) for i in range(2)).astype(bf16)
-    )
-    qk_grad = collect_grad(
-        *(
-            contract_first(
-                normed, jnp.concatenate([grad_query_pre[i], key_or_value[i]], axis=1)
-            ).astype(bf16)
-            for i in range(2)
-        )
-    )
-    input_chunk = (grad_middle + norm_back(grad_normed, hidden32, inv_one, gain_one)).astype(bf16)
-    input_grad = whole_block(input_chunk)
-
-    by_z = jnp.concatenate([wo_gate_grad, qk_grad], axis=-1)
-    kept = jnp.where(odd_c, by_z[:, 2:], by_z[:, :2])
-    taken = pair_swap(jnp.where(odd_c, by_z[:, :2], by_z[:, 2:]), "c")
-    heads = jnp.stack([jnp.where(odd_c, taken, kept), jnp.where(odd_c, kept, taken)], axis=2)
-    heads = heads.reshape(block_rows, 2, 2, 4, HEAD_WIDTH).astype(f32)
-
-    def head_columns(which):
-        return heads[:, :, :, which].reshape(block_rows, 4 * HEAD_WIDTH)
-
-    out_weight_grad, gate_weight_grad, query_weight_grad = (head_columns(i) for i in range(3))
-    key_weight_grad = heads[:, :, 0, 3].reshape(block_rows, 2 * HEAD_WIDTH)
-    value_weight_grad = heads[:, :, 1, 3].reshape(block_rows, 2 * HEAD_WIDTH)
-
+    normed_parts = sum(
+        contract_last(grad_qk[i], side) + contract_last(grad_gate_pre[i], gate_side[:, :low])
+        for i, (side, gate_side) in enumerate(((qk_mine, og_mine), (qk_other, og_other)))
+    ).astype(bf16)
+    normed_parts, gate_up_grad = after((normed_parts, gate_up_grad))
+    grad_qk, grad_normed_two, middle, ffn_out_far, og_got, gain_two_late = after(
+        (grad_qk, grad_normed_two, middle, ffn_out_far, og_got, inv_two), normed_parts
+    )
+    og_rows = near_add(og_both, og_got)
+    og_grad = to_row_owners(after(og_rows, down_grad))
+    layer_out = whole_block((middle + down_sums[:chunk_rows] + ffn_out_far.astype(f32)).astype(bf16))
     gains = jnp.concatenate(
         [
-            from_own_first(jnp.sum(grad_normed * hidden32 * inv_one, axis=0), odd_x),
-            from_own_first(jnp.sum(grad_normed_two * middle * inv_two, axis=0), odd_x),
+            from_own_first(jnp.sum(normed_parts.astype(f32) * normed, axis=0) / gain_one, odd_near),
+            from_own_first(jnp.sum(grad_normed_two * middle * gain_two_late, axis=0), odd_near),
             query_gain_part,
             key_gain_part,
         ]
     )
     gains = (gains + plane_swap(gains, 1)) + (plane_swap(gains, 2) + plane_swap(gains, 3))
-    for axis in ("x", "y", "c"):
+    for axis in ("near", "y", "c"):
         gains = gains + pair_swap(gains, axis)
+    grad_normed = sum_chunks(normed_parts, down_grad)
+    qk_both = core_sum(*(contract_first(normed, g).astype(bf16) for g in grad_qk))
+    qk_rows = near_add(qk_both, pair_swap(qk_both[qk_both.shape[0] // 2 :], "near"))
+    qk_grad = to_row_owners(after(qk_rows, og_grad))
+    input_chunk = (grad_middle + norm_back(grad_normed, hidden32, inv_one, gain_one)).astype(bf16)
+    input_grad = whole_block(input_chunk)
+
+    def own_columns(by_z):
+        kept = jnp.where(odd_c, by_z[2:], by_z[:2])
+        taken = pair_swap(jnp.where(odd_c, by_z[:2], by_z[2:]), "c")
+        return jnp.where(odd_c, taken, kept), jnp.where(odd_c, kept, taken)
+
+    def per_head(halves, start):
+        columns = [half[i, :, start : start + low] for i in range(2) for half in halves]
+        return jnp.concatenate(columns, axis=1).astype(f32)
+
+    def per_group(half):
+        return jnp.concatenate([half[0, :, low:], half[1, :, low:]], axis=1).astype(f32)
+
+    og_halves, qk_halves = own_columns(og_grad), own_columns(qk_grad)
+    gate_weight_grad, out_weight_grad = per_head(og_halves, 0), per_head(og_halves, low)
+    query_weight_grad = per_head(qk_halves, 0)
+    key_weight_grad, value_weight_grad = per_group(qk_halves[0]), per_group(qk_halves[1])
 
     def flat(grad):
-        return grad.reshape(block_rows, -1).astype(f32)
+        return jnp.concatenate([grad[p] for p in range(PLANES)], axis=1).astype(f32)
 
     return (
         layer_out,
@@ -823,8 +879,8 @@
         value_weight_grad,
         gate_weight_grad,
         out_weight_grad,
-        flat(gate_grad),
-        flat(up_grad),
+        flat(gate_up_grad[:, :, :units]),
+        flat(gate_up_grad[:, :, units:]),
         flat(down_grad),
         gains[:width],
         gains[width : 2 * width],
@@ -836,9 +892,9 @@
 def solution(mesh):
     wide, head = mesh.shape["wide"], mesh.shape["head"]
     if wide == 2 * PLANES and head == 4:
-        devices = mesh.devices.reshape(PLANES, 2, 2, 2)
-        mesh = Mesh(devices, ("z", "x", "y", "c"))
-        program, rows, columns = on_slice_device, ("z", "x"), ("y", "c")
+        devices = mesh.devices.reshape(2, 2, 2, 2, 2)
+        mesh = Mesh(devices, ("far", "near", "x", "y", "c"))
+        program, rows, columns = on_slice_device, ("far", "near", "x"), ("y", "c")
     else:
         program, rows, columns = on_device, "wide", "head"
     tokens, weight = P(rows, None), P(rows, columns)

time: 767 us -> 550 us (0.72)
  waiting for transfers between devices: 346 us -> 213 us
  local copies, waits for them, and re-layouts: 89.8 us -> 49.5 us
  starting transfers between devices: 151 us -> 117 us
  matrix products: 95.2 us -> 64.7 us
  other arithmetic: 72.2 us -> 93 us
    ppermute x65 -> x38, waiting for transfers between devices: 185 us -> 83.2 us  [pair_swap(): return lax.ppermute(values, axis, [(0, 1), (1, 0)])]
    ppermute x33 -> x45, waiting for transfers between devices: 115 us -> 62.8 us  [the longest x42 62.8 us: side_swap(): return lax.ppermute(values, ('x', 'y'), [(i, i ^ step) for i in range(4)])]
    ppermute x65 -> x38, starting transfers between devices: 49.1 us -> 23.7 us  [pair_swap(): return lax.ppermute(values, axis, [(0, 1), (1, 0)])]
    all_to_all x9 -> x8, waiting for transfers between devices: 44.9 us -> 66.6 us  [the longest x4 38.3 us: to_row_owners(): back = lax.all_to_all(rows, PLANE, split_axis=0, concat_axis=0, tiled=True)]
    unnamed x235 -> x251, local copies, waits for them, and re-layouts: 34 us -> 18.8 us
    convert_element_type x16 -> x21, other arithmetic: 14.4 us -> 27.3 us  [the longest x4 9.26 us: near_add(): (both[:half].astype(jnp.float32) + got.astype(jnp.float32)).astype(jnp.bf...]
    another operation x14 -> x4, local copies, waits for them, and re-layouts: 12.9 us -> 2.53 us  [the longest x1 2.16 us: by_plane(): jnp.stack([jnp.concatenate([w[:, p * step:(p + 1) * step] for w in weight...]
    all_to_all x6 -> x1, local copies, waits for them, and re-layouts: 11.7 us -> 2.04 us  [to_row_owners(): back = lax.all_to_all(rows, PLANE, split_axis=0, concat_axis=0, tiled=True)]
  transfers between devices with their start and end apart: 107 -> 91, of which waited for: 46 -> 34; matrix products, arithmetic and copies ran while one was open for 30% -> 33% of each run, Pallas kernels for 0% -> 0%
where the time goes in v2:
time: 550 us; the launch traced here: 540 us
  waiting for transfers between devices  213 us (39%)
  starting transfers between devices  117 us (21%)
  other arithmetic  93 us (17%)
  matrix products  64.7 us (12%)
  local copies, waits for them, and re-layouts  49.5 us (9%)
    ppermute x38, waiting for transfers between devices, pair_swap(): return lax.ppermute(values, axis, [(0, 1), (1, 0)])  83.2 us
    ppermute x42, waiting for transfers between devices, side_swap(): return lax.ppermute(values, ('x', 'y'), [(i, i ^ step) for i in range(4)])  62.8 us
    ppermute x42, starting transfers between devices, side_swap(): return lax.ppermute(values, ('x', 'y'), [(i, i ^ step) for i in range(4)])  56.3 us
    all_to_all x4, waiting for transfers between devices, to_row_owners(): back = lax.all_to_all(rows, PLANE, split_axis=0, concat_axis=0, tiled=True)  38.3 us
    all_to_all x4, waiting for transfers between devices, to_plane_owners(): lax.all_to_all(local.reshape(planes * rows, width), PLANE, split_axis=0,...  28.3 us
    ppermute x38, starting transfers between devices, pair_swap(): return lax.ppermute(values, axis, [(0, 1), (1, 0)])  23.7 us
    dot_general x10, matrix products, contract_last(): lax.dot_general(left, right, (((1,), (1,)), ((), ())), preferred_element_...  21 us
    unnamed x251, local copies, waits for them, and re-layouts  18.8 us
  transfers between devices with their start and end apart: 91, of which 34 were waited for; matrix products, arithmetic and copies ran while one was open for 33% of the time, Pallas kernels for 0%

profile of v2, /device:TPU:0, one launch (start us, length us, event | category | flops | bytes accessed | tf_op | source)
XLA Modules:
  0.0 540.3 jit_solution(11869506231643792609)
XLA Ops:
  47.8 4.9 all-to-all-done
  58.0 8.3 %collective-permute-done.8 = bf16[1024,256]{1,0:T(8,128)(2,1)S(1)} collective-permute-done((bf16[1024,256]{1,0:T(8,128)(2,1)S(1)}, bf16[1024,256]{1,0:T(8,128)(2,1)S(1)}, u32[]{:S(2)}, u32[]{:S(2)}) %collective-permute-start.8) | collective-permute-done | bytes 524320 | tf_op jit(solution)/shard_map/ppermute | solution.py:445
  82.0 6.5 %all-to-all-done.1 = bf16[4,256,256]{2,1,0:T(8,128)(2,1)S(1)} async-done(((bf16[4,256,256]{2,1,0:T(8,128)(2,1)}), bf16[4,256,256]{2,1,0:T(8,128)(2,1)S(1)}, u32[]{:S(2)}, u32[]{:S(2)}) %all-to-all-start.1) | async-done | bytes 524320 | tf_op jit(solution)/shard_map/all_to_all | solution.py:528
  88.5 5.1 collective-permute-done.10
  98.1 4.8 all-to-all-start.2
  104.4 5.0 collective-permute-done.12
  133.0 13.9 %all-to-all-done.2 = bf16[4,256,768]{2,1,0:T(8,128)(2,1)} async-done(((bf16[4,256,768]{2,1,0:T(8,128)(2,1)}), bf16[4,256,768]{2,1,0:T(8,128)(2,1)}, u32[]{:S(2)}, u32[]{:S(2)}) %all-to-all-start.2) | async-done | bytes 1572896 | tf_op jit(solution)/shard_map/all_to_all | solution.py:528
  166.1 24.6 %collective-permute-done.20 = bf16[64,2048]{1,0:T(8,128)(2,1)} collective-permute-done((bf16[64,2048]{1,0:T(8,128)(2,1)}, bf16[64,2048]{1,0:T(8,128)(2,1)}, u32[]{:S(2)}, u32[]{:S(2)}) %collective-permute-start.20) | collective-permute-done | bytes 262176 | tf_op jit(solution)/shard_map/ppermute | solution.py:445
  215.2 7.0 %collective-permute-done.29 = bf16[64,2048]{1,0:T(8,128)(2,1)S(1)} collective-permute-done((bf16[64,2048]{1,0:T(8,128)(2,1)S(1)}, bf16[64,2048]{1,0:T(8,128)(2,1)S(1)}, u32[]{:S(2)}, u32[]{:S(2)}) %collective-permute-start.29) | collective-permute-done | bytes 262176 | tf_op jit(solution)/shard_map/ppermute | solution.py:453
  225.5 6.0 %collective-permute-done.31 = bf16[64,2048]{1,0:T(8,128)(2,1)S(1)} collective-permute-done((bf16[64,2048]{1,0:T(8,128)(2,1)S(1)}, bf16[64,2048]{1,0:T(8,128)(2,1)S(1)}, u32[]{:S(2)}, u32[]{:S(2)}) %collective-permute-start.31) | collective-permute-done | bytes 262176 | tf_op jit(solution)/shard_map/ppermute | solution.py:453
  231.8 5.1 collective-permute-done.33
  269.1 4.9 collective-permute-done.38
  278.9 6.7 %collective-permute-done.42 = bf16[64,2048]{1,0:T(8,128)(2,1)S(1)} collective-permute-done((bf16[64,2048]{1,0:T(8,128)(2,1)S(1)}, bf16[64,2048]{1,0:T(8,128)(2,1)S(1)}, u32[]{:S(2)}, u32[]{:S(2)}) %collective-permute-start.42) | collective-permute-done | bytes 262176 | tf_op jit(solution)/shard_map/ppermute | solution.py:445
  303.9 7.1 %collective-permute-done.47 = bf16[64,2048]{1,0:T(8,128)(2,1)S(1)} collective-permute-done((bf16[64,2048]{1,0:T(8,128)(2,1)S(1)}, bf16[64,2048]{1,0:T(8,128)(2,1)S(1)}, u32[]{:S(2)}, u32[]{:S(2)}) %collective-permute-start.47) | collective-permute-done | bytes 262176 | tf_op jit(solution)/shard_map/ppermute | solution.py:453
  314.0 6.2 %collective-permute-done.49 = bf16[64,2048]{1,0:T(8,128)(2,1)S(1)} collective-permute-done((bf16[64,2048]{1,0:T(8,128)(2,1)S(1)}, bf16[64,2048]{1,0:T(8,128)(2,1)S(1)}, u32[]{:S(2)}, u32[]{:S(2)}) %collective-permute-start.49) | collective-permute-done | bytes 262176 | tf_op jit(solution)/shard_map/ppermute | solution.py:453
  354.7 10.8 %collective-permute-done.56 = bf16[128,2048]{1,0:T(8,128)(2,1)S(1)} collective-permute-done((bf16[128,2048]{1,0:T(8,128)(2,1)S(1)}, bf16[128,2048]{1,0:T(8,128)(2,1)S(1)}, u32[]{:S(2)}, u32[]{:S(2)}) %collective-permute-start.56) | collective-permute-done | bytes 524320 | tf_op jit(solution)/shard_map/ppermute | solution.py:453
  377.9 4.6 all-to-all-start.4
  395.3 26.9 %all-to-all-done.4 = bf16[4,256,768]{2,1,0:T(8,128)(2,1)} async-done(((bf16[4,256,768]{2,1,0:T(8,128)(2,1)}), bf16[4,256,768]{2,1,0:T(8,128)(2,1)}, u32[]{:S(2)}, u32[]{:S(2)}) %all-to-all-start.4) | async-done | bytes 1572896 | tf_op jit(solution)/shard_map/all_to_all | solution.py:549
  451.4 8.7 %collective-permute-done.80 = f32[4352]{0:T(1024)S(1)} collective-permute-done((f32[4352]{0:T(1024)S(1)}, f32[4352]{0:T(1024)S(1)}, u32[]{:S(2)}, u32[]{:S(2)}) %collective-permute-start.80) | collective-permute-done | bytes 17440 | tf_op jit(solution)/shard_map/ppermute | solution.py:445
  476.2 5.5 %collective-permute-done.65 = bf16[64,2048]{1,0:T(8,128)(2,1)} collective-permute-done((bf16[64,2048]{1,0:T(8,128)(2,1)}, bf16[64,2048]{1,0:T(8,128)(2,1)}, u32[]{:S(2)}, u32[]{:S(2)}) %collective-permute-start.65) | collective-permute-done | bytes 262176 | tf_op jit(solution)/shard_map/ppermute | solution.py:453
  481.7 5.5 %collective-permute-done.70 = bf16[64,2048]{1,0:T(8,128)(2,1)S(1)} collective-permute-done((bf16[64,2048]{1,0:T(8,128)(2,1)}, bf16[64,2048]{1,0:T(8,128)(2,1)S(1)}, u32[]{:S(2)}, u32[]{:S(2)}) %collective-permute-start.70) | collective-permute-done | bytes 262176 | tf_op jit(solution)/shard_map/ppermute | solution.py:445
  498.7 4.5 all-to-all-start.7
  507.8 8.1 %collective-permute-done.74 = bf16[1024,256]{1,0:T(8,128)(2,1)} collective-permute-done((bf16[1024,256]{1,0:T(8,128)(2,1)}, bf16[1024,256]{1,0:T(8,128)(2,1)}, u32[]{:S(2)}, u32[]{:S(2)}) %collective-permute-start.74) | collective-permute-done | bytes 524320 | tf_op jit(solution)/shard_map/ppermute | solution.py:445
  523.3 11.5 %all-to-all-done.6 = bf16[4,256,256]{2,1,0:T(8,128)(2,1)S(1)} async-done(((bf16[4,256,256]{2,1,0:T(8,128)(2,1)}), bf16[4,256,256]{2,1,0:T(8,128)(2,1)S(1)}, u32[]{:S(2)}, u32[]{:S(2)}) %all-to-all-start.6) | async-done | bytes 524320 | tf_op jit(solution)/shard_map/all_to_all | solution.py:549
  (635 shorter events, 334.9 us)
Async XLA Ops:
  5.4 40.9 %collective-permute-start.1 = (bf16[64,2048]{1,0:T(8,128)(2,1)}, bf16[64,2048]{1,0:T(8,128)(2,1)}, u32[]{:S(2)}, u32[]{:S(2)}) collective-permute-start(bf16[64,2048]{1,0:T(8,128)(2,1)} %get-tuple-element.156), channel_id=1, source_target_pairs={{0,16},{16,0},{1,17},{17,1},{2,18},{18,2},{3,19},{19,3},{4,20},{20... | collective-permute-start | bytes 786440 | tf_op jit(solution)/shard_map/ppermute | solution.py:445
  9.4 44.5 %collective-permute-start.2 = (bf16[64,2048]{1,0:T(8,128)(2,1)}, bf16[64,2048]{1,0:T(8,128)(2,1)}, u32[]{:S(2)}, u32[]{:S(2)}) collective-permute-start(bf16[64,2048]{1,0:T(8,128)(2,1)} %get-tuple-element.156), channel_id=1, source_target_pairs={{0,2},{2,0},{4,6},{6,4},{1,3},{3,1},{5,7},{7,5},{8,10},{10,8},{12,... | collective-permute-start | bytes 786440 | tf_op jit(solution)/shard_map/ppermute | solution.py:453
  11.0 56.5 %collective-permute-start.4 = (bf16[64,2048]{1,0:T(8,128)(2,1)}, bf16[64,2048]{1,0:T(8,128)(2,1)}, u32[]{:S(2)}, u32[]{:S(2)}) collective-permute-start(bf16[64,2048]{1,0:T(8,128)(2,1)} %get-tuple-element.156), channel_id=1, source_target_pairs={{0,4},{2,6},{4,0},{6,2},{1,5},{3,7},{5,1},{7,3},{8,12},{10,14},{12... | collective-permute-start | bytes 786440 | tf_op jit(solution)/shard_map/ppermute | solution.py:453
  12.5 56.0 %collective-permute-start.6 = (bf16[64,2048]{1,0:T(8,128)(2,1)}, bf16[64,2048]{1,0:T(8,128)(2,1)}, u32[]{:S(2)}, u32[]{:S(2)}) collective-permute-start(bf16[64,2048]{1,0:T(8,128)(2,1)} %get-tuple-element.156), channel_id=1, source_target_pairs={{0,6},{2,4},{4,2},{6,0},{1,7},{3,5},{5,3},{7,1},{8,14},{10,12},{12... | collective-permute-start | bytes 786440 | tf_op jit(solution)/shard_map/ppermute | solution.py:453
  98.1 48.8 %all-to-all-start.2 = ((bf16[4,256,768]{2,1,0:T(8,128)(2,1)}), bf16[4,256,768]{2,1,0:T(8,128)(2,1)}, u32[]{:S(2)}, u32[]{:S(2)}) async-start(bf16[4,256,768]{2,1,0:T(8,128)(2,1)} %pad_maximum_fusion.1), calls=%async_computation.2 | async-start | bytes 3145728 | tf_op jit(solution)/shard_map/all_to_all | solution.py:528
  130.2 32.4 %collective-permute-start.16 = (bf16[64,2048]{1,0:T(8,128)(2,1)}, bf16[64,2048]{1,0:T(8,128)(2,1)}, u32[]{:S(2)}, u32[]{:S(2)}) collective-permute-start(bf16[64,2048]{1,0:T(8,128)(2,1)} %get-tuple-element.177), channel_id=1, source_target_pairs={{0,6},{2,4},{4,2},{6,0},{1,7},{3,5},{5,3},{7,1},{8,14},{10,12},{12... | collective-permute-start | bytes 786440 | tf_op jit(solution)/shard_map/ppermute | solution.py:453
  149.9 50.0 %collective-permute-start.25 = (bf16[1024,768]{1,0:T(8,128)(2,1)}, bf16[1024,768]{1,0:T(8,128)(2,1)}, u32[]{:S(2)}, u32[]{:S(2)}) collective-permute-start(bf16[1024,768]{1,0:T(8,128)(2,1)} %bitcast.21), channel_id=1, source_target_pairs={{0,8},{8,0},{1,9},{9,1},{2,10},{10,2},{3,11},{11,3},{4,12},{12,4},... | collective-permute-start | bytes 4718600 | tf_op jit(solution)/shard_map/ppermute | solution.py:445
  152.2 38.5 %collective-permute-start.20 = (bf16[64,2048]{1,0:T(8,128)(2,1)}, bf16[64,2048]{1,0:T(8,128)(2,1)}, u32[]{:S(2)}, u32[]{:S(2)}) collective-permute-start(bf16[64,2048]{1,0:T(8,128)(2,1)} %add_convert_fusion.15), channel_id=1, source_target_pairs={{0,16},{16,0},{1,17},{17,1},{2,18},{18,2},{3,19},{19,3},{4,20},{20... | collective-permute-start | bytes 786440 | tf_op jit(solution)/shard_map/ppermute | solution.py:445
  156.4 40.8 %all-to-all-start.3 = ((bf16[4,256,384]{2,1,0:T(8,128)(2,1)}), bf16[4,256,384]{2,1,0:T(8,128)(2,1)}, u32[]{:S(2)}, u32[]{:S(2)}) async-start(bf16[4,256,384]{2,1,0:T(8,128)(2,1)} %pad_maximum_fusion.10), calls=%async_computation.3 | async-start | bytes 1572864 | tf_op jit(solution)/shard_map/all_to_all | solution.py:528
  162.6 40.9 %collective-permute-start.22 = (bf16[128,2048]{1,0:T(8,128)(2,1)}, bf16[128,2048]{1,0:T(8,128)(2,1)}, u32[]{:S(2)}, u32[]{:S(2)}) collective-permute-start(bf16[128,2048]{1,0:T(8,128)(2,1)} %pad_maximum_fusion.17), channel_id=1, source_target_pairs={{0,2},{2,0},{4,6},{6,4},{1,3},{3,1},{5,7},{7,5},{8,10},{10,8},{12,... | collective-permute-start | bytes 1572872 | tf_op jit(solution)/shard_map/ppermute | solution.py:453
  163.1 42.0 %collective-permute-start.23 = (bf16[128,2048]{1,0:T(8,128)(2,1)}, bf16[128,2048]{1,0:T(8,128)(2,1)}, u32[]{:S(2)}, u32[]{:S(2)}) collective-permute-start(bf16[128,2048]{1,0:T(8,128)(2,1)} %pad_maximum_fusion.17), channel_id=1, source_target_pairs={{0,4},{2,6},{4,0},{6,2},{1,5},{3,7},{5,1},{7,3},{8,12},{10,14},{12... | collective-permute-start | bytes 1572872 | tf_op jit(solution)/shard_map/ppermute | solution.py:453
  165.1 41.1 %collective-permute-start.24 = (bf16[128,2048]{1,0:T(8,128)(2,1)}, bf16[128,2048]{1,0:T(8,128)(2,1)}, u32[]{:S(2)}, u32[]{:S(2)}) collective-permute-start(bf16[128,2048]{1,0:T(8,128)(2,1)} %pad_maximum_fusion.17), channel_id=1, source_target_pairs={{0,6},{2,4},{4,2},{6,0},{1,7},{3,5},{5,3},{7,1},{8,14},{10,12},{12... | collective-permute-start | bytes 1572872 | tf_op jit(solution)/shard_map/ppermute | solution.py:453
  205.1 26.4 %collective-permute-start.32 = (bf16[64,2048]{1,0:T(8,128)(2,1)S(1)}, bf16[64,2048]{1,0:T(8,128)(2,1)S(1)}, u32[]{:S(2)}, u32[]{:S(2)}) collective-permute-start(bf16[64,2048]{1,0:T(8,128)(2,1)S(1)} %copy-done.57), channel_id=1, source_target_pairs={{0,6},{2,4},{4,2},{6,0},{1,7},{3,5},{5,3},{7,1},{8,14},{10,12},{12... | collective-permute-start | bytes 786440 | tf_op jit(solution)/shard_map/ppermute | solution.py:453
  215.1 29.1 %collective-permute-start.35 = (bf16[2048,768]{1,0:T(8,128)(2,1)S(1)}, bf16[2048,768]{1,0:T(8,128)(2,1)S(1)}, u32[]{:S(2)}, u32[]{:S(2)}) collective-permute-start(bf16[2048,768]{1,0:T(8,128)(2,1)S(1)} %pad_maximum_fusion), channel_id=1, source_target_pairs={{0,1},{1,0},{2,3},{3,2},{4,5},{5,4},{6,7},{7,6},{8,9},{9,8},{10,11... | collective-permute-start | bytes 9437192 | tf_op jit(solution)/shard_map/ppermute | solution.py:445
  259.1 30.5 %collective-permute-start.44 = (bf16[2048,768]{1,0:T(8,128)(2,1)S(1)}, bf16[2048,768]{1,0:T(8,128)(2,1)S(1)}, u32[]{:S(2)}, u32[]{:S(2)}) collective-permute-start(bf16[2048,768]{1,0:T(8,128)(2,1)S(1)} %convolution_convert_fusion), channel_id=1, source_target_pairs={{0,1},{1,0},{2,3},{3,2},{4,5},{5,4},{6,7},{7,6},{8,9},{9,8},{10,11... | collective-permute-start | bytes 9437192 | tf_op jit(solution)/shard_map/ppermute | solution.py:445
  292.6 27.6 %collective-permute-start.50 = (bf16[64,2048]{1,0:T(8,128)(2,1)S(1)}, bf16[64,2048]{1,0:T(8,128)(2,1)S(1)}, u32[]{:S(2)}, u32[]{:S(2)}) collective-permute-start(bf16[64,2048]{1,0:T(8,128)(2,1)S(1)} %get-tuple-element.104), channel_id=1, source_target_pairs={{0,6},{2,4},{4,2},{6,0},{1,7},{3,5},{5,3},{7,1},{8,14},{10,12},{12... | collective-permute-start | bytes 786440 | tf_op jit(solution)/shard_map/ppermute | solution.py:453
  295.5 69.9 %collective-permute-start.57 = (bf16[1024,768]{1,0:T(8,128)(2,1)}, bf16[1024,768]{1,0:T(8,128)(2,1)}, u32[]{:S(2)}, u32[]{:S(2)}) collective-permute-start(bf16[1024,768]{1,0:T(8,128)(2,1)} %slice.615), channel_id=1, source_target_pairs={{0,8},{8,0},{1,9},{9,1},{2,10},{10,2},{3,11},{11,3},{4,12},{12,4},... | collective-permute-start | bytes 4718600 | tf_op jit(solution)/shard_map/ppermute | solution.py:445
  303.8 48.6 %collective-permute-start.58 = (bf16[1024,384]{1,0:T(8,128)(2,1)}, bf16[1024,384]{1,0:T(8,128)(2,1)}, u32[]{:S(2)}, u32[]{:S(2)}) collective-permute-start(bf16[1024,384]{1,0:T(8,128)(2,1)} %slice.616), channel_id=1, source_target_pairs={{0,8},{8,0},{1,9},{9,1},{2,10},{10,2},{3,11},{11,3},{4,12},{12,4},... | collective-permute-start | bytes 2359304 | tf_op jit(solution)/shard_map/ppermute | solution.py:445
  373.9 48.3 %collective-permute-start.59 = (bf16[64,2048]{1,0:T(8,128)(2,1)}, bf16[64,2048]{1,0:T(8,128)(2,1)}, u32[]{:S(2)}, u32[]{:S(2)}) collective-permute-start(bf16[64,2048]{1,0:T(8,128)(2,1)} %slice.1013), channel_id=1, source_target_pairs={{0,16},{16,0},{1,17},{17,1},{2,18},{18,2},{3,19},{19,3},{4,20},{20... | collective-permute-start | bytes 786440 | tf_op jit(solution)/shard_map/ppermute | solution.py:445
  377.9 44.3 %all-to-all-start.4 = ((bf16[4,256,768]{2,1,0:T(8,128)(2,1)}), bf16[4,256,768]{2,1,0:T(8,128)(2,1)}, u32[]{:S(2)}, u32[]{:S(2)}) async-start(bf16[4,256,768]{2,1,0:T(8,128)(2,1)} %bitcast.245), calls=%async_computation.4 | async-start | bytes 3145728 | tf_op jit(solution)/shard_map/all_to_all | solution.py:549
  389.6 33.1 %collective-permute-start.61 = (bf16[1024,256]{0,1:T(8,128)(2,1)}, bf16[1024,256]{0,1:T(8,128)(2,1)}, u32[]{:S(2)}, u32[]{:S(2)}) collective-permute-start(bf16[1024,256]{0,1:T(8,128)(2,1)} %slice.626), channel_id=1, source_target_pairs={{0,8},{8,0},{1,9},{9,1},{2,10},{10,2},{3,11},{11,3},{4,12},{12,4},... | collective-permute-start | bytes 1572872 | tf_op jit(solution)/shard_map/ppermute | solution.py:445
  434.5 32.8 %collective-permute-start.62 = (bf16[64,2048]{1,0:T(8,128)(2,1)}, bf16[64,2048]{1,0:T(8,128)(2,1)}, u32[]{:S(2)}, u32[]{:S(2)}) collective-permute-start(bf16[64,2048]{1,0:T(8,128)(2,1)} %reshape.550), channel_id=1, source_target_pairs={{0,2},{2,0},{1,3},{3,1},{4,6},{6,4},{5,7},{7,5},{8,10},{10,8},{9,1... | collective-permute-start | bytes 786440 | tf_op jit(solution)/shard_map/ppermute | solution.py:445
  435.8 33.3 %collective-permute-start.69 = (bf16[64,2048]{1,0:T(8,128)(2,1)}, bf16[64,2048]{1,0:T(8,128)(2,1)}, u32[]{:S(2)}, u32[]{:S(2)}) collective-permute-start(bf16[64,2048]{1,0:T(8,128)(2,1)} %get-tuple-element.158), channel_id=1, source_target_pairs={{0,6},{2,4},{4,2},{6,0},{1,7},{3,5},{5,3},{7,1},{8,14},{10,12},{12... | collective-permute-start | bytes 786440 | tf_op jit(solution)/shard_map/ppermute | solution.py:453
  437.9 36.1 %all-to-all-start.5 = ((bf16[4,256,384]{2,1,0:T(8,128)(2,1)}), bf16[4,256,384]{2,1,0:T(8,128)(2,1)}, u32[]{:S(2)}, u32[]{:S(2)}) async-start(bf16[4,256,384]{2,1,0:T(8,128)(2,1)} %bitcast.45), calls=%async_computation.5 | async-start | bytes 1572864 | tf_op jit(solution)/shard_map/all_to_all | solution.py:549
  (175 other events, 1657.5 us)

commit v3 on v0

--- a/solution.py
+++ b/solution.py
@@ -1,6 +1,9 @@
 import jax
 import jax.numpy as jnp
 from jax import lax
+from jax.experimental import pallas as pl
+from jax.experimental.pallas import tpu as pltpu
+from jax.sharding import Mesh
 from jax.sharding import PartitionSpec as P
 
 HEAD_WIDTH = 128
@@ -240,40 +243,21 @@
         contract_last(hidden_act, full_ffn_down).astype(jnp.bfloat16), "head"
     ).astype(jnp.float32)
     layer_out = (middle + ffn_out).astype(jnp.bfloat16)
-    (
-        back_query,
-        back_key,
-        back_value,
-        back_gate,
-        back_out,
-        back_ffn_gate,
-        back_ffn_up,
-        back_ffn_down,
-    ) = (
-        lax.all_gather(query_weight, "wide", axis=0, tiled=True),
-        lax.all_gather(key_matrix, "wide", axis=0, tiled=True),
-        lax.all_gather(value_matrix, "wide", axis=0, tiled=True),
-        lax.all_gather(gate_weight, "wide", axis=0, tiled=True),
-        lax.all_gather(out_weight, "wide", axis=0, tiled=True),
-        lax.all_gather(ffn_gate_weight, "wide", axis=0, tiled=True),
-        lax.all_gather(ffn_up_weight, "wide", axis=0, tiled=True),
-        lax.all_gather(ffn_down_weight, "wide", axis=0, tiled=True),
-    )
     grad32 = out_cotangent.astype(jnp.float32)
-    grad_hidden = jnp.dot(out_cotangent, back_ffn_down, preferred_element_type=jnp.float32)
+    grad_hidden = jnp.dot(out_cotangent, full_ffn_down, preferred_element_type=jnp.float32)
     grad_ffn_gate = (
         grad_hidden * ffn_up_pre * gate_act * (1.0 + ffn_gate_pre * (1.0 - gate_act))
     ).astype(jnp.bfloat16)
     grad_ffn_up = (grad_hidden * silu_gate).astype(jnp.bfloat16)
     grad_normed_two = lax.psum(
         (
-            contract_last(grad_ffn_gate, back_ffn_gate) + contract_last(grad_ffn_up, back_ffn_up)
+            contract_last(grad_ffn_gate, full_ffn_gate) + contract_last(grad_ffn_up, full_ffn_up)
         ).astype(jnp.bfloat16),
         "head",
     ).astype(jnp.float32)
     grad_middle = grad32 + norm_back(grad_normed_two, middle, inv_two, ffn_gain)
     grad_branch = grad_middle.astype(jnp.bfloat16)
-    grad_gated = jnp.dot(grad_branch, back_out, preferred_element_type=jnp.float32)
+    grad_gated = jnp.dot(grad_branch, full_out, preferred_element_type=jnp.float32)
     grad_attended = (grad_gated * gate_sig).astype(jnp.bfloat16)
     grad_gate_pre = (grad_gated * attended * gate_sig * (1.0 - gate_sig)).astype(jnp.bfloat16)
     grad_heads = (
@@ -282,10 +266,7 @@
         .reshape(kv_heads, query_rows, HEAD_WIDTH)
     )
     delta = jnp.sum(grad_heads.astype(jnp.float32) * attended_heads, axis=-1)
-    all_keys, all_values = (
-        lax.all_gather(key_rows, "wide", axis=0, tiled=True),
-        lax.all_gather(value_rows, "wide", axis=0, tiled=True),
-    )
+    all_keys, all_values = key_piece, value_piece
     key_step = 512
     key_count = row_length // key_step
     all_ids = jnp.arange(row_length, dtype=jnp.int32)
@@ -391,10 +372,10 @@
         .astype(jnp.bfloat16)
     )
     grad_normed_part = (
-        contract_last(grad_query_pre, back_query)
-        + contract_last(grad_key_pre, back_key)
-        + contract_last(grad_values, back_value)
-        + contract_last(grad_gate_pre, back_gate)
+        contract_last(grad_query_pre, full_query)
+        + contract_last(grad_key_pre, full_key)
+        + contract_last(grad_values, full_value)
+        + contract_last(grad_gate_pre, full_gate)
     )
     grad_normed = lax.psum(grad_normed_part.astype(jnp.bfloat16), "head").astype(jnp.float32)
     input_grad = (grad_middle + norm_back(grad_normed, hidden32, inv_one, attn_gain)).astype(
@@ -458,42 +439,752 @@
     )
 
 
+PLANES = 4
+PLANE = ("far", "x")
+
+
+def pair_swap(values, axis):
+    return lax.ppermute(values, axis, [(0, 1), (1, 0)])
+
+
+def plane_swap(values, step):
+    return lax.ppermute(values, PLANE, [(i, i ^ step) for i in range(PLANES)])
+
+
+def side_swap(values, step):
+    return lax.ppermute(values, ("x", "y"), [(i, i ^ step) for i in range(4)])
+
+
+def after(values, *done):
+    return lax.optimization_barrier((values, done))[0]
+
+
+def gather_chunks(chunk):
+    far = pair_swap(chunk, "far")
+    near = [side_swap(chunk, step) for step in range(1, 4)]
+    away = [side_swap(far, step) for step in range(1, 4)]
+    pieces = [chunk, far]
+    for pair in zip(near, away):
+        pieces.extend(pair)
+    return pieces
+
+
+def sum_sends(parts):
+    return [
+        [parts[far]] + [side_swap(parts[2 * step + far], step) for step in range(1, 4)]
+        for far in (1, 0)
+    ]
+
+
+def sum_pieces(pieces):
+    total = pieces[0].astype(jnp.float32)
+    for piece in pieces[1:]:
+        total = total + piece.astype(jnp.float32)
+    return total
+
+
+def flip_if(values, axis, flag):
+    return jnp.where(flag, jnp.flip(values, axis), values)
+
+
+def to_own_first(values, flag):
+    lead = values.shape[:-1]
+    width = values.shape[-1]
+    split = values.reshape(lead + (2, 2, width // 4))
+    zero = split[..., 0, :].reshape(lead + (width // 2,))
+    one = split[..., 1, :].reshape(lead + (width // 2,))
+    return jnp.concatenate([jnp.where(flag, one, zero), jnp.where(flag, zero, one)], axis=-1)
+
+
+def from_own_first(values, flag):
+    lead = values.shape[:-1]
+    width = values.shape[-1]
+    own = values[..., : width // 2].reshape(lead + (2, width // 4))
+    other = values[..., width // 2 :].reshape(lead + (2, width // 4))
+    pair = jnp.stack([jnp.where(flag, other, own), jnp.where(flag, own, other)], axis=-2)
+    return pair.reshape(lead + (width,))
+
+
+def to_plane_owners(local):
+    planes, rows, width = local.shape
+    return lax.all_to_all(
+        local.reshape(planes * rows, width), PLANE, split_axis=0, concat_axis=0, tiled=True
+    )
+
+
+HEADS = ("far", "x", "c")
+
+
+def head_pairs(a, b, back):
+    pairs = []
+    for f in range(2):
+        for x in range(2):
+            for c in range(2):
+                pairs.append((4 * f + 2 * x + c, 4 * c + 2 * (x ^ a) + (f ^ b)))
+    return [(j, i) for i, j in pairs] if back else pairs
+
+
+def to_head_owners(columns, far, x, c):
+    turned = flip_if(flip_if(columns, 0, x == 1), 1, far == 1)
+    sent = [
+        [lax.ppermute(turned[a, b], HEADS, head_pairs(a, b, False)) for a in range(2)]
+        for b in range(2)
+    ]
+    pieces = jnp.stack([jnp.stack(row) for row in sent])
+    rows = flip_if(flip_if(pieces, 0, c == 1), 1, x == 1)
+    return rows.reshape(PLANES * columns.shape[2], columns.shape[3]), sent
+
+
+def from_head_owners(rows, far, x, c):
+    blocks = rows.reshape(2, 2, rows.shape[0] // PLANES, rows.shape[1])
+    blocks = flip_if(flip_if(blocks, 0, c == 1), 1, x == 1)
+    pieces = jnp.stack(
+        [
+            jnp.stack(
+                [lax.ppermute(blocks[b, a], HEADS, head_pairs(a, b, True)) for b in range(2)]
+            )
+            for a in range(2)
+        ]
+    )
+    return flip_if(flip_if(pieces, 0, x == 1), 1, far == 1)
+
+
+def core_sum(mine, other):
+    both = mine.astype(jnp.float32) + pair_swap(other, "c").astype(jnp.float32)
+    return both.astype(jnp.bfloat16)
+
+
+def near_add(both, got):
+    half = both.shape[0] // 2
+    return (both[:half].astype(jnp.float32) + got.astype(jnp.float32)).astype(jnp.bfloat16)
+
+
+def to_row_owners(rows):
+    back = lax.all_to_all(rows, PLANE, split_axis=0, concat_axis=0, tiled=True)
+    return back.reshape(PLANES, rows.shape[0] // PLANES, rows.shape[1])
+
+
+VMEM_BYTES = 56 * 1024 * 1024
+
+
+def kernel_call(body, operands, outs, scratch=(), flags=None, flops=0):
+    specs = [pl.BlockSpec(memory_space=pltpu.VMEM)] * len(operands)
+    if flags is not None:
+        operands = [flags] + list(operands)
+        specs = [pl.BlockSpec(memory_space=pltpu.SMEM)] + specs
+    moved = sum(v.size * v.dtype.itemsize for v in operands)
+    moved += sum(v.size * v.dtype.itemsize for v in outs)
+    return pl.pallas_call(
+        body,
+        out_shape=outs,
+        in_specs=specs,
+        out_specs=[pl.BlockSpec(memory_space=pltpu.VMEM)] * len(outs),
+        scratch_shapes=list(scratch),
+        compiler_params=pltpu.CompilerParams(vmem_limit_bytes=VMEM_BYTES),
+        cost_estimate=pl.CostEstimate(flops=flops, bytes_accessed=moved, transcendentals=0),
+    )(*operands)
+
+
+def shaped(shape, dtype):
+    return jax.ShapeDtypeStruct(shape, dtype)
+
+
+def dot_nn(left, right):
+    return jnp.dot(left, right, preferred_element_type=jnp.float32)
+
+
+def turned(values, cosine, signed_sine):
+    return values * cosine + pltpu.roll(values, HEAD_WIDTH // 2, 1) * signed_sine
+
+
+def turned_back(grads, cosine, signed_sine):
+    return grads * cosine - pltpu.roll(grads, HEAD_WIDTH // 2, 1) * signed_sine
+
+
+def sigmoid(values):
+    return 1.0 / (1.0 + jnp.exp(-values))
+
+
+def project_kernel(flag, *refs):
+    hidden = refs[:8]
+    gain, mine_own, mine_near, other_own, other_near, cosine, sine, qgain, kgain = refs[8:17]
+    normed, pair, query_rot, query_pre, key_pre, scratch = refs[17:]
+    rows = hidden[0].shape[0]
+    for i in range(8):
+        h = hidden[i][...].astype(jnp.float32)
+        inverse = lax.rsqrt(jnp.mean(h * h, axis=1, keepdims=True) + epsilon)
+        normed[i * rows : (i + 1) * rows, :] = (h * inverse * gain[...]).astype(jnp.bfloat16)
+    half = normed.shape[1] // 2
+    left, right = normed[:, :half], normed[:, half:]
+    for i, (own, near) in enumerate(((mine_own, mine_near), (other_own, other_near))):
+        scratch[i] = dot_nn(left, own[...]) + dot_nn(right, near[...])
+    cos, sin = cosine[...], sine[...]
+    swapped = flag[0] == 1
+    mine, other = scratch[0, :, HEAD_WIDTH:], scratch[1, :, HEAD_WIDTH:]
+    pre = jnp.where(swapped, other, mine)
+    key_pre[...] = pre
+    pair[:, HEAD_WIDTH:] = jnp.where(swapped, mine, other).astype(jnp.bfloat16)
+    unit = pre * lax.rsqrt(jnp.mean(pre * pre, axis=1, keepdims=True) + epsilon)
+    pair[:, :HEAD_WIDTH] = turned(unit * kgain[...], cos, sin).astype(jnp.bfloat16)
+    for i in range(2):
+        pre = scratch[i, :, :HEAD_WIDTH]
+        query_pre[i] = pre
+        unit = pre * lax.rsqrt(jnp.mean(pre * pre, axis=1, keepdims=True) + epsilon)
+        query_rot[i] = turned(unit * qgain[...], cos, sin).astype(jnp.bfloat16)
+
+
+def attend_kernel(query_rot, first, second, third, fourth, bounds, key_ids, gate_pre, *refs):
+    outs_w, gated, attended, log_total, parts, total = refs[:4], *refs[4:7], refs[7:15], refs[15]
+    scale = HEAD_WIDTH ** (-0.5)
+    pairs = (first, second, third, fourth)
+    rows = first.shape[0]
+    tile = rows // 2
+
+    def step(i, carry):
+        head, at = i // 2, pl.multiple_of(i % 2 * tile, tile)
+        query = query_rot[head, pl.ds(at, tile), :]
+        start, last = bounds[pl.ds(at, tile), 0:1], bounds[pl.ds(at, tile), 1:2]
+        scores = []
+        for j, pair in enumerate(pairs):
+            ids = key_ids[:, j * rows : (j + 1) * rows]
+            allowed = (ids >= start) & (ids <= last)
+            score = contract_last(query, pair[:, :HEAD_WIDTH]) * scale
+            scores.append(jnp.where(allowed, score, masked_score))
+        top = jnp.max(scores[0], axis=1, keepdims=True)
+        for score in scores[1:]:
+            top = jnp.maximum(top, jnp.max(score, axis=1, keepdims=True))
+        total = jnp.zeros_like(top)
+        result = jnp.zeros((tile, HEAD_WIDTH), jnp.float32)
+        for score, pair in zip(scores, pairs):
+            raised = jnp.exp(score - top)
+            total = total + jnp.sum(raised, axis=1, keepdims=True)
+            result = result + dot_nn(raised.astype(jnp.bfloat16), pair[:, HEAD_WIDTH:])
+        result = result / total
+        attended[head, pl.ds(at, tile), :] = result
+        log_total[head, pl.ds(at, tile), :] = jnp.broadcast_to(top + jnp.log(total), result.shape)
+        gate = sigmoid(gate_pre[head, pl.ds(at, tile), :])
+        gated[head, pl.ds(at, tile), :] = (result * gate).astype(jnp.bfloat16)
+        return carry
+
+    lax.fori_loop(0, 4, step, 0)
+    half = total.shape[1] // 2
+    for near in range(2):
+        total[:, near * half : (near + 1) * half] = contract_last(
+            gated[0], outs_w[near][:, HEAD_WIDTH:]
+        ) + contract_last(gated[1], outs_w[2 + near][:, HEAD_WIDTH:])
+    rows = parts[0].shape[0]
+    for i in range(8):
+        parts[i][...] = total[i * rows : (i + 1) * rows, :].astype(jnp.bfloat16)
+
+
+def ffn_kernel(*refs):
+    chunks, cotangent, gate_up, down = refs[:8], refs[8:12], refs[12:16], refs[16:20]
+    acts, grads, two_parts, down_parts = refs[20:22], refs[22:24], refs[24:32], refs[32:36]
+    normed_two, cot, total = refs[36:]
+    rows = chunks[0].shape[0]
+    for i in range(8):
+        normed_two[i * rows : (i + 1) * rows, :] = chunks[i][...]
+    rows = cotangent[0].shape[0]
+    for i in range(4):
+        cot[i * rows : (i + 1) * rows, :] = cotangent[i][...]
+    half = cot.shape[1] // 2
+    units = down[0].shape[1]
+    tile = cot.shape[0] // 2
+
+    def step(i, carry):
+        at = pl.multiple_of(i * tile, tile)
+        rows_at = pl.ds(at, tile)
+        for side in range(2):
+            wide = [gate_up[2 * side][...], gate_up[2 * side + 1][...]]
+            pre = dot_nn(normed_two[rows_at, :half], wide[0]) + dot_nn(
+                normed_two[rows_at, half:], wide[1]
+            )
+            grad = dot_nn(cot[rows_at, :half], down[2 * side][...]) + dot_nn(
+                cot[rows_at, half:], down[2 * side + 1][...]
+            )
+            gate, up = pre[:, :units], pre[:, units:]
+            act = sigmoid(gate)
+            silu = gate * act
+            acts[side][rows_at, :] = (silu * up).astype(jnp.bfloat16)
+            grads[side][rows_at, :units] = (
+                grad * up * act * (1.0 + gate * (1.0 - act))
+            ).astype(jnp.bfloat16)
+            grads[side][rows_at, units:] = (grad * silu).astype(jnp.bfloat16)
+        for near in range(2):
+            total[0, rows_at, near * half : (near + 1) * half] = contract_last(
+                grads[0][rows_at, :], gate_up[near][...]
+            ) + contract_last(grads[1][rows_at, :], gate_up[2 + near][...])
+            total[1, rows_at, near * half : (near + 1) * half] = contract_last(
+                acts[0][rows_at, :], down[near][...]
+            ) + contract_last(acts[1][rows_at, :], down[2 + near][...])
+        return carry
+
+    lax.fori_loop(0, 2, step, 0)
+    rows = two_parts[0].shape[0]
+    for i in range(8):
+        two_parts[i][...] = total[0, i * rows : (i + 1) * rows, :].astype(jnp.bfloat16)
+    rows = down_parts[0].shape[0]
+    for i in range(4):
+        down_parts[i][...] = total[1, i * rows : (i + 1) * rows, :].astype(jnp.bfloat16)
+
+
+def attend_back_kernel(*refs):
+    chunks, outs_w, pairs = refs[:8], refs[8:12], refs[12:16]
+    bounds, key_ids, query_rot, query_pre, gate_pre, attended, log_total = refs[16:23]
+    cosine, sine, qgain = refs[23:26]
+    branch, grad_gate, grad_query, grad_pairs, gain_part = refs[26:31]
+    gated_grad, keys_acc, vals_acc = refs[31:]
+    scale = HEAD_WIDTH ** (-0.5)
+    rows = chunks[0].shape[0]
+    for i in range(8):
+        branch[i * rows : (i + 1) * rows, :] = chunks[i][...]
+    half = branch.shape[1] // 2
+    for side in range(2):
+        gated_grad[side] = dot_nn(branch[:, :half], outs_w[2 * side][:, HEAD_WIDTH:]) + dot_nn(
+            branch[:, half:], outs_w[2 * side + 1][:, HEAD_WIDTH:]
+        )
+    keys_acc[...] = jnp.zeros_like(keys_acc)
+    vals_acc[...] = jnp.zeros_like(vals_acc)
+    gain_part[...] = jnp.zeros_like(gain_part)
+    rows = pairs[0].shape[0]
+    tile = rows // 2
+
+    def step(i, carry):
+        head, at = i // 2, pl.multiple_of(i % 2 * tile, tile)
+        rows_at = pl.ds(at, tile)
+        grad = gated_grad[head, rows_at, :]
+        gate = sigmoid(gate_pre[head, rows_at, :])
+        out = attended[head, rows_at, :]
+        grad_gate[head, rows_at, :] = (grad * out * gate * (1.0 - gate)).astype(jnp.bfloat16)
+        grad_out = (grad * gate).astype(jnp.bfloat16)
+        delta = jnp.sum(grad_out.astype(jnp.float32) * out, axis=1, keepdims=True)
+        query = query_rot[head, rows_at, :]
+        start, last = bounds[rows_at, 0:1], bounds[rows_at, 1:2]
+        log = log_total[head, rows_at, 0:1]
+        grad_rot = jnp.zeros((tile, HEAD_WIDTH), jnp.float32)
+        for j, pair in enumerate(pairs):
+            ids = key_ids[:, j * rows : (j + 1) * rows]
+            allowed = (ids >= start) & (ids <= last)
+            keys, vals = pair[:, :HEAD_WIDTH], pair[:, HEAD_WIDTH:]
+            score = jnp.where(allowed, contract_last(query, keys) * scale, masked_score)
+            weight = jnp.exp(score - log)
+            grad_score = (weight * (contract_last(grad_out, vals) - delta)).astype(jnp.bfloat16)
+            grad_rot = grad_rot + dot_nn(grad_score, keys)
+            at_keys = slice(j * rows, (j + 1) * rows)
+            keys_acc[at_keys, :] += contract_first(grad_score, query)
+            vals_acc[at_keys, :] += contract_first(weight.astype(jnp.bfloat16), grad_out)
+        grad_rot = (grad_rot * scale).astype(jnp.bfloat16).astype(jnp.float32)
+        grad_unit = turned_back(grad_rot, cosine[rows_at, :], sine[rows_at, :])
+        pre = query_pre[head, rows_at, :]
+        inverse = lax.rsqrt(jnp.mean(pre * pre, axis=1, keepdims=True) + epsilon)
+        gain_part[...] += jnp.sum(grad_unit * (pre * inverse), axis=0, keepdims=True)
+        grad_query[head, rows_at, :] = norm_back(grad_unit, pre, inverse, qgain[...]).astype(
+            jnp.bfloat16
+        )
+        return carry
+
+    lax.fori_loop(0, 4, step, 0)
+    grad_pairs[:, :HEAD_WIDTH] = (keys_acc[...] * scale).astype(jnp.bfloat16)
+    grad_pairs[:, HEAD_WIDTH:] = vals_acc[...].astype(jnp.bfloat16)
+
+
+def tables_kernel(lengths, coords, frequency, bounds, key_ids, angles):
+    far, near, x, y, c = (coords[i] for i in range(5))
+    rows = bounds.shape[0] // 8
+
+    def ids_of(at, near_at, c_at):
+        chunk, row = at // rows, at % rows
+        x_at, y_at, far_at = x ^ (chunk // 4), y ^ (chunk // 2 % 2), far ^ (chunk % 2)
+        return (((far_at * 2 + near_at) * 2 + x_at) * 4 + y_at * 2 + c_at) * rows + row
+
+    at = lax.broadcasted_iota(jnp.int32, bounds.shape, 0)
+    lane = lax.broadcasted_iota(jnp.int32, bounds.shape, 1)
+    ids = ids_of(at, near, c)
+    start = jnp.zeros_like(ids)
+    end = jnp.int32(0)
+    for i in range(lengths.shape[0]):
+        end = end + lengths[i]
+        start = jnp.where(ids >= end, end, start)
+    bounds[...] = jnp.where(lane == 0, start, ids)
+    angles[...] = (ids - start).astype(jnp.float32) * frequency[...]
+    at = lax.broadcasted_iota(jnp.int32, key_ids.shape, 1)
+    group = at // (8 * rows)
+    key_ids[...] = ids_of(at % (8 * rows), near ^ (group % 2), c ^ (group // 2))
+
+
+def gate_kernel(normed, mine_own, mine_near, other_own, other_near, gate_pre):
+    half = normed.shape[1] // 2
+    for i, (own, near) in enumerate(((mine_own, mine_near), (other_own, other_near))):
+        gate_pre[i] = dot_nn(normed[:, :half], own[:, :HEAD_WIDTH]) + dot_nn(
+            normed[:, half:], near[:, :HEAD_WIDTH]
+        )
+
+
+def input_kernel(flag, *refs):
+    own_pair, got_pair, key_pre, cosine, sine, kgain, grad_query, grad_gate, normed = refs[:9]
+    qk, og = refs[9:13], refs[13:17]
+    grad_qk, parts, key_gain, input_gain, total = refs[17:19], refs[19:27], refs[27], refs[28], refs[29]
+    pair = own_pair[...].astype(jnp.float32) + got_pair[...].astype(jnp.float32)
+    grad_unit = turned_back(
+        pair[:, :HEAD_WIDTH].astype(jnp.bfloat16).astype(jnp.float32), cosine[...], sine[...]
+    )
+    pre = key_pre[...]
+    inverse = lax.rsqrt(jnp.mean(pre * pre, axis=1, keepdims=True) + epsilon)
+    key_gain[...] = jnp.sum(grad_unit * (pre * inverse), axis=0, keepdims=True)
+    grad_key = norm_back(grad_unit, pre, inverse, kgain[...]).astype(jnp.bfloat16)
+    grad_value = pair[:, HEAD_WIDTH:].astype(jnp.bfloat16)
+    swapped = flag[0] == 1
+    for side in range(2):
+        grad_qk[side][:, :HEAD_WIDTH] = grad_query[side]
+        first, second = (grad_key, grad_value) if side == 0 else (grad_value, grad_key)
+        grad_qk[side][:, HEAD_WIDTH:] = jnp.where(swapped, second, first)
+    half = total.shape[1] // 2
+    tile = total.shape[0] // 2
+
+    def step(i, carry):
+        rows_at = pl.ds(pl.multiple_of(i * tile, tile), tile)
+        for near in range(2):
+            acc = None
+            for side in range(2):
+                part = contract_last(grad_qk[side][rows_at, :], qk[2 * side + near][...])
+                part = part + contract_last(
+                    grad_gate[side, rows_at, :], og[2 * side + near][:, :HEAD_WIDTH]
+                )
+                acc = part if acc is None else acc + part
+            total[rows_at, near * half : (near + 1) * half] = acc
+        return carry
+
+    lax.fori_loop(0, 2, step, 0)
+    rows = parts[0].shape[0]
+    gain = jnp.zeros(input_gain.shape, jnp.float32)
+    for i in range(8):
+        part = total[i * rows : (i + 1) * rows, :]
+        parts[i][...] = part.astype(jnp.bfloat16)
+        gain = gain + jnp.sum(
+            part * normed[i * rows : (i + 1) * rows, :].astype(jnp.float32), axis=0, keepdims=True
+        )
+    input_gain[...] = gain
+
+
+def on_slice_device(
+    hidden_in,
+    out_cotangent,
+    doc_lengths,
+    query_weight,
+    key_matrix,
+    value_matrix,
+    gate_weight,
+    out_weight,
+    ffn_gate_weight,
+    ffn_up_weight,
+    ffn_down_weight,
+    attn_gain,
+    ffn_gain,
+    query_gain,
+    key_gain,
+):
+    bf16, f32 = jnp.bfloat16, jnp.float32
+    block_rows, width = hidden_in.shape
+    chunk_rows = block_rows // 4
+    tokens = 8 * chunk_rows
+    low = HEAD_WIDTH
+    units = ffn_gate_weight.shape[1] // PLANES
+    coords = [lax.axis_index(name) for name in ("far", "near", "x", "y", "c")]
+    far, near, x, y, c = coords
+    odd_near = near == 1
+    core_flag = c.reshape(1)
+
+    def columns(x_at, head):
+        at = (2 * x_at + head) * low
+        third = (key_matrix if head == 0 else value_matrix)[:, x_at * low : (x_at + 1) * low]
+        parts = (query_weight[:, at : at + low], third)
+        parts += (gate_weight[:, at : at + low], out_weight[:, at : at + low])
+        return jnp.concatenate(parts, axis=1)
+
+    own_hidden = to_own_first(
+        lax.dynamic_slice_in_dim(hidden_in, (y * 2 + c) * chunk_rows, chunk_rows, 0), odd_near
+    )
+    hidden = gather_chunks(own_hidden)
+    attn_half, attn_sent = to_head_owners(
+        jnp.stack([jnp.stack([columns(i, j) for j in range(2)]) for i in range(2)]), far, x, c
+    )
+    qk_half, og_half = attn_half[:, : 2 * low], attn_half[:, 2 * low :]
+    qk_near = pair_swap(qk_half, "near")
+    og_near = pair_swap(after(og_half, qk_near), "near")
+    qk = [qk_half, qk_near, pair_swap(qk_half, "c"), pair_swap(after(qk_near, hidden), "c")]
+    gain_one = to_own_first(attn_gain, odd_near)
+    out_cotangent, ffn_gain = after((out_cotangent, ffn_gain), hidden[1])
+    cotangent = to_own_first(
+        lax.dynamic_slice_in_dim(out_cotangent, (y * 2 + c) * chunk_rows, chunk_rows, 0), odd_near
+    )
+    gain_two = to_own_first(ffn_gain, odd_near)
+    cotangent_far = pair_swap(cotangent, "far")
+    hidden, cotangent_far = after((hidden, cotangent_far))
+    ffn_gate_weight, ffn_up_weight, ffn_down_weight = after(
+        (ffn_gate_weight, ffn_up_weight, ffn_down_weight), qk_near, hidden, cotangent_far
+    )
+    cotangent_pair = jnp.concatenate([cotangent, cotangent_far], axis=0)
+    cotangents = [cotangent_pair] + [side_swap(cotangent_pair, i) for i in range(1, 4)]
+
+    def by_plane(*weights):
+        return jnp.stack(
+            [
+                jnp.concatenate([w[:, p * units : (p + 1) * units] for w in weights], axis=1)
+                for p in range(PLANES)
+            ]
+        )
+
+    gate_up_half = to_plane_owners(by_plane(ffn_gate_weight, ffn_up_weight))
+
+    half_width = low // 2
+    frequency = rope_base ** (-2.0 * jnp.arange(half_width, dtype=f32) / low)
+    frequency = jnp.concatenate([frequency, frequency])[None, :]
+    bounds, key_ids, angles = pl.pallas_call(
+        tables_kernel,
+        out_shape=[
+            shaped((tokens, low), jnp.int32),
+            shaped((1, 4 * tokens), jnp.int32),
+            shaped((tokens, low), f32),
+        ],
+        in_specs=[pl.BlockSpec(memory_space=pltpu.SMEM)] * 2
+        + [pl.BlockSpec(memory_space=pltpu.VMEM)],
+        out_specs=[pl.BlockSpec(memory_space=pltpu.VMEM)] * 3,
+    )(after(doc_lengths, qk_near), jnp.stack(coords), frequency)
+    sign = jnp.where(jnp.arange(low) < half_width, -1.0, 1.0).astype(f32)
+    cosine, sine = jnp.cos(angles), jnp.sin(angles) * sign[None, :]
+    query_gain, key_gain = query_gain[None, :], key_gain[None, :]
+
+    normed, pair, query_rot, query_pre, key_pre = kernel_call(
+        project_kernel,
+        hidden + [gain_one[None, :]] + qk + [cosine, sine, query_gain, key_gain],
+        [
+            shaped((tokens, width), bf16),
+            shaped((tokens, 2 * low), bf16),
+            shaped((2, tokens, low), bf16),
+            shaped((2, tokens, low), f32),
+            shaped((tokens, low), f32),
+        ],
+        [pltpu.VMEM((2, tokens, 2 * low), f32)],
+        core_flag,
+        4 * tokens * width * 2 * low,
+    )
+    pair_near = pair_swap(pair, "near")
+    pairs = [pair, pair_near, pair_swap(pair, "c"), pair_swap(pair_near, "c")]
+
+    og = [og_half, og_near] + [pair_swap(after(part, pair), "c") for part in (og_half, og_near)]
+    gate_up_near = pair_swap(after(gate_up_half, pair_near), "near")
+    down_half = to_plane_owners(after(by_plane(ffn_down_weight), gate_up_half))
+    query_rot, cotangents, gate_up_half = after((query_rot, cotangents, gate_up_half))
+
+    (gate_pre,) = kernel_call(
+        gate_kernel,
+        [normed] + og,
+        [shaped((2, tokens, low), f32)],
+        flops=4 * tokens * width * low,
+    )
+    outs = kernel_call(
+        attend_kernel,
+        [query_rot] + pairs + [bounds, key_ids, gate_pre] + og,
+        [shaped((2, tokens, low), bf16)]
+        + [shaped((2, tokens, low), f32)] * 2
+        + [shaped((chunk_rows, width), bf16)] * 8,
+        [pltpu.VMEM((tokens, width), f32)],
+        None,
+        8 * tokens * 4 * tokens * low,
+    )
+    gated, attended, log_total, branch_parts = outs[0], outs[1], outs[2], outs[3:]
+    away, own = sum_sends(branch_parts)
+    away, gate_up_near, down_half = after((sum_pieces(away).astype(bf16), gate_up_near, down_half))
+    hidden32 = own_hidden.astype(f32)
+    middle = hidden32 + sum_pieces(own + [pair_swap(away, "far")])
+    inv_two = lax.rsqrt(jnp.mean(middle * middle, axis=1, keepdims=True) + epsilon)
+    normed_two_chunk = (middle * inv_two * gain_two).astype(bf16)
+    normed_two_pieces = gather_chunks(normed_two_chunk)
+    gate_up = [
+        gate_up_half,
+        gate_up_near,
+        pair_swap(gate_up_half, "c"),
+        pair_swap(gate_up_near, "c"),
+    ]
+    down_near = pair_swap(after(down_half, gate_up_near), "near")
+    down = [down_half, down_near, pair_swap(down_half, "c"), pair_swap(down_near, "c")]
+
+    outs = kernel_call(
+        ffn_kernel,
+        normed_two_pieces + cotangents + gate_up + down,
+        [shaped((tokens, units), bf16)] * 2
+        + [shaped((tokens, 2 * units), bf16)] * 2
+        + [shaped((chunk_rows, width), bf16)] * 8
+        + [shaped((2 * chunk_rows, width), bf16)] * 4
+        + [shaped((tokens, width), bf16)] * 2,
+        [pltpu.VMEM((2, tokens, width), f32)],
+        None,
+        24 * tokens * width * units,
+    )
+    hidden_acts, grad_ffn, two_parts, down_parts = outs[:2], outs[2:4], outs[4:12], outs[12:16]
+    normed_two, all_cotangent = outs[16:]
+    away, own = sum_sends(two_parts)
+    two_far = pair_swap(sum_pieces(away).astype(bf16), "far")
+    two_away = own, two_far
+    gate_up_both = core_sum(*(contract_first(normed_two, g).astype(bf16) for g in grad_ffn))
+    down_both = core_sum(*(contract_first(all_cotangent, act).astype(bf16) for act in hidden_acts))
+
+    (own, two_far), down_both, gate_up_both = after((two_away, down_both, gate_up_both))
+    grad_normed_two = sum_pieces(own + [two_far])
+
+    def whole_block(chunk):
+        chunk = from_own_first(chunk, odd_near)
+        by_y = jnp.stack([chunk, pair_swap(chunk, "y")])
+        by_core = jnp.stack([by_y, pair_swap(by_y, "c")], axis=1)
+        return flip_if(flip_if(by_core, 1, c == 1), 0, y == 1).reshape(block_rows, width)
+
+    grad_middle = cotangent.astype(f32) + norm_back(grad_normed_two, middle, inv_two, gain_two)
+    grad_branch = grad_middle.astype(bf16)
+    branch_pieces = gather_chunks(grad_branch)
+    down_parts = after(down_parts, branch_pieces)
+    down_pieces = [down_parts[0]] + [side_swap(down_parts[i], i) for i in range(1, 4)]
+    half = width // 2
+    gate_up_got = pair_swap(gate_up_both[half:], "near")
+    down_got = pair_swap(down_both[half:], "near")
+
+    all_branch, grad_gate, grad_query, grad_pairs, query_gain_part = kernel_call(
+        attend_back_kernel,
+        branch_pieces
+        + og
+        + pairs
+        + [bounds, key_ids, query_rot, query_pre, gate_pre, attended, log_total]
+        + [cosine, sine, query_gain],
+        [
+            shaped((tokens, width), bf16),
+            shaped((2, tokens, low), bf16),
+            shaped((2, tokens, low), bf16),
+            shaped((4 * tokens, 2 * low), bf16),
+            shaped((1, low), f32),
+        ],
+        [
+            pltpu.VMEM((2, tokens, low), f32),
+            pltpu.VMEM((4 * tokens, low), f32),
+            pltpu.VMEM((4 * tokens, low), f32),
+        ],
+        None,
+        20 * tokens * 4 * tokens * low,
+    )
+    pair_other = pair_swap(grad_pairs[2 * tokens :], "c")
+    gate_up_got, down_got, down_pieces, normed_later = after(
+        (gate_up_got, down_got, down_pieces, normed), grad_pairs
+    )
+    near_pairs = grad_pairs[: 2 * tokens].astype(f32) + pair_other.astype(f32)
+    near_pairs = near_pairs.astype(bf16)
+    pair_got = pair_swap(near_pairs[tokens:], "near")
+    gate_up_rows = near_add(gate_up_both, gate_up_got)
+    down_got, gate_up_rows = after((down_got, gate_up_rows))
+    down_rows = near_add(down_both, down_got)
+    gate_up_grad = to_row_owners(gate_up_rows)
+    down_grad = to_row_owners(after(down_rows, gate_up_grad))
+    down_sums = sum_pieces(down_pieces)
+    down_far = pair_swap(down_sums[chunk_rows:].astype(bf16), "far")
+    og_both = core_sum(
+        *(
+            jnp.concatenate(
+                [
+                    contract_first(normed_later, grad_gate[i]).astype(bf16),
+                    contract_first(all_branch, gated[i]).astype(bf16),
+                ],
+                axis=1,
+            )
+            for i in range(2)
+        )
+    )
+    key_pre, gate_up_rows, down_rows, down_sums = after(
+        (key_pre, gate_up_rows, down_rows, down_sums)
+    )
+    og_got = pair_swap(after(og_both, pair_got)[half:], "near")
+    outs = kernel_call(
+        input_kernel,
+        [near_pairs[:tokens], pair_got, key_pre, cosine, sine, key_gain]
+        + [grad_query, grad_gate, normed]
+        + qk
+        + og,
+        [shaped((tokens, 2 * low), bf16)] * 2
+        + [shaped((chunk_rows, width), bf16)] * 8
+        + [shaped((1, low), f32), shaped((1, width), f32)],
+        [pltpu.VMEM((tokens, width), f32)],
+        core_flag,
+        12 * tokens * width * low,
+    )
+    grad_qk, normed_parts, key_gain_part, input_gain_part = outs[:2], outs[2:10], outs[10], outs[11]
+    away, own = sum_sends(normed_parts)
+    away = sum_pieces(away).astype(bf16)
+    qk_sides = [contract_first(normed, g).astype(bf16) for g in after(grad_qk, normed_parts[1])]
+    qk_other = pair_swap(qk_sides[1], "c")
+    away, qk_other, gate_up_grad = after((away, qk_other, gate_up_grad))
+    qk_both = (qk_sides[0].astype(f32) + qk_other.astype(f32)).astype(bf16)
+    qk_got = pair_swap(qk_both[half:], "near")
+    grad_far = pair_swap(away, "far")
+    grad_normed = sum_pieces(own + [grad_far])
+    inv_one = lax.rsqrt(jnp.mean(hidden32 * hidden32, axis=1, keepdims=True) + epsilon)
+    input_chunk = (grad_middle + norm_back(grad_normed, hidden32, inv_one, gain_one)).astype(bf16)
+    input_grad = whole_block(input_chunk)
+    og_got, down_far, down_grad, gain_parts = after(
+        (og_got, down_far, down_grad, (input_gain_part, query_gain_part, key_gain_part)), grad_far
+    )
+    attn_rows = jnp.concatenate([near_add(qk_both, qk_got), near_add(og_both, og_got)], axis=1)
+    attn_grad = from_head_owners(attn_rows, far, x, c)
+    qk_grad, og_grad = attn_grad[..., : 2 * low], attn_grad[..., 2 * low :]
+    layer_out = whole_block((middle + down_sums[:chunk_rows] + down_far.astype(f32)).astype(bf16))
+    gains = jnp.concatenate(
+        [
+            from_own_first(gain_parts[0][0] / gain_one, odd_near),
+            from_own_first(jnp.sum(grad_normed_two * middle * inv_two, axis=0), odd_near),
+            gain_parts[1][0],
+            gain_parts[2][0],
+        ]
+    )
+    gains = (gains + plane_swap(gains, 1)) + (plane_swap(gains, 2) + plane_swap(gains, 3))
+    for axis in ("near", "y", "c"):
+        gains = gains + pair_swap(gains, axis)
+
+    def per_head(grad, start):
+        columns = [grad[i, j, :, start : start + low] for i in range(2) for j in range(2)]
+        return jnp.concatenate(columns, axis=1).astype(f32)
+
+    def per_group(grad, j):
+        return jnp.concatenate([grad[0, j, :, low:], grad[1, j, :, low:]], axis=1).astype(f32)
+
+    def flat(grad):
+        return jnp.concatenate([grad[p] for p in range(PLANES)], axis=1).astype(f32)
+
+    return (
+        layer_out,
+        input_grad,
+        per_head(qk_grad, 0),
+        per_group(qk_grad, 0),
+        per_group(qk_grad, 1),
+        per_head(og_grad, 0),
+        per_head(og_grad, low),
+        flat(gate_up_grad[:, :, :units]),
+        flat(gate_up_grad[:, :, units:]),
+        flat(down_grad),
+        gains[:width],
+        gains[width : 2 * width],
+        gains[2 * width : 2 * width + low],
+        gains[2 * width + low :],
+    )
+
+
 def solution(mesh):
+    wide, head = mesh.shape["wide"], mesh.shape["head"]
+    if wide == 2 * PLANES and head == 4:
+        devices = mesh.devices.reshape(2, 2, 2, 2, 2)
+        mesh = Mesh(devices, ("far", "near", "x", "y", "c"))
+        program, rows, columns = on_slice_device, ("far", "near", "x"), ("y", "c")
+    else:
+        program, rows, columns = on_device, "wide", "head"
+    tokens, weight = P(rows, None), P(rows, columns)
     return jax.shard_map(
-        on_device,
+        program,
         mesh=mesh,
-        in_specs=(
-            P("wide", None),
-            P("wide", None),
-            P(),
-            P("wide", "head"),
-            P("wide", "head"),
-            P("wide", "head"),
-            P("wide", "head"),
-            P("wide", "head"),
-            P("wide", "head"),
-            P("wide", "head"),
-            P("wide", "head"),
-            P(),
-            P(),
-            P(),
-            P(),
-        ),
-        out_specs=(
-            P("wide", None),
-            P("wide", None),
-            P("wide", "head"),
-            P("wide", "head"),
-            P("wide", "head"),
-            P("wide", "head"),
-            P("wide", "head"),
-            P("wide", "head"),
-            P("wide", "head"),
-            P("wide", "head"),
-            P(),
-            P(),
-            P(),
-            P(),
-        ),
+        in_specs=(tokens, tokens, P()) + (weight,) * 8 + (P(),) * 4,
+        out_specs=(tokens, tokens) + (weight,) * 8 + (P(),) * 4,
         check_vma=False,
     )

time: 1410 us -> 532 us (0.38)
  waiting for transfers between devices: 1150 us -> 246 us
  starting transfers between devices: 2.23 us -> 119 us
  matrix products: 87.3 us -> 18.3 us
  Pallas kernels: 0 us -> 65.5 us
  blocking collectives: 43.8 us -> 0 us
  local copies, waits for them, and re-layouts: 61.6 us -> 31.8 us
    all_gather x10 -> x0, waiting for transfers between devices: 552 us -> none  [the longest x1 98.1 us: on_device(): lax.all_gather(ffn_up_weight, 'wide', axis=0, tiled=True)]
    reduce_scatter x3 -> x0, waiting for transfers between devices: 498 us -> none  [the longest x1 389 us: on_device(): lax.psum_scatter(jnp.concatenate([contract_first(normed_input, grad_query...]
    ppermute x0 -> x93, waiting for transfers between devices: none -> 246 us  [the longest x40 143 us: pair_swap(): return lax.ppermute(values, axis, [(0, 1), (1, 0)])]
    ppermute x0 -> x93, starting transfers between devices: none -> 99.4 us  [the longest x42 52 us: side_swap(): return lax.ppermute(values, ('x', 'y'), [(i, i ^ step) for i in range(4)])]
    psum x3 -> x0, waiting for transfers between devices: 92.1 us -> none  [the longest x1 33.2 us: on_device(): lax.psum((contract_last(grad_ffn_gate, back_ffn_gate) + contract_last(gra...]
    pallas_call x0 -> x7, Pallas kernels: none -> 65.5 us  [the longest x6 63.5 us: kernel_call(): pl.pallas_call(body, out_shape=outs, in_specs=specs, out_specs=[pl.BlockS...]
    dot_general x23 -> x0, matrix products: 61.1 us -> none  [the longest x8 20.2 us: contract_last(): lax.dot_general(left, right, (((1,), (1,)), ((), ())), preferred_element_...]
    psum x1 -> x0, blocking collectives: 43.8 us -> none  [on_device(): lax.psum((attn_gain_part * head_first, ffn_gain_part * head_first, query_...]
  transfers between devices with their start and end apart: 16 -> 97, of which waited for: 16 -> 42; matrix products, arithmetic and copies ran while one was open for 8% -> 12% of each run, Pallas kernels for 0% -> 9%
where the time goes in v3:
time: 532 us; the launch traced here: 523 us
  waiting for transfers between devices  246 us (46%)
  starting transfers between devices  119 us (22%)
  Pallas kernels  65.5 us (12%)
  other arithmetic  38.4 us (7%)
  local copies, waits for them, and re-layouts  31.8 us (6%)
  matrix products  18.3 us (3%)
    ppermute x40, waiting for transfers between devices, pair_swap(): return lax.ppermute(values, axis, [(0, 1), (1, 0)])  143 us
    ppermute x42, waiting for transfers between devices, side_swap(): return lax.ppermute(values, ('x', 'y'), [(i, i ^ step) for i in range(4)])  90.3 us
    pallas_call x6, Pallas kernels, kernel_call(): pl.pallas_call(body, out_shape=outs, in_specs=specs, out_specs=[pl.BlockS...  63.5 us
    ppermute x42, starting transfers between devices, side_swap(): return lax.ppermute(values, ('x', 'y'), [(i, i ^ step) for i in range(4)])  52 us
    ppermute x40, starting transfers between devices, pair_swap(): return lax.ppermute(values, axis, [(0, 1), (1, 0)])  32.2 us
    dot_general x10, matrix products, contract_first(): lax.dot_general(left, right, (((0,), (0,)), ((), ())), preferred_element_...  18.3 us
    unnamed x230, local copies, waits for them, and re-layouts  12.7 us
    all_to_all x2, starting transfers between devices, to_plane_owners(): lax.all_to_all(local.reshape(planes * rows, width), PLANE, split_axis=0,...  11 us
  transfers between devices with their start and end apart: 97, of which 42 were waited for; matrix products, arithmetic and copies ran while one was open for 12% of the time, Pallas kernels for 9%

profile of v3, /device:TPU:0, one launch (start us, length us, event | category | flops | bytes accessed | tf_op | source)
XLA Modules:
  0.0 522.6 jit_solution(10649302206945165845)
XLA Ops:
  15.2 12.8 %collective-permute-done.refs_1_ = bf16[64,2048]{1,0:T(8,128)(2,1)S(1)} collective-permute-done((bf16[64,2048]{1,0:T(8,128)(2,1)S(1)}, bf16[64,2048]{1,0:T(8,128)(2,1)S(1)}, u32[]{:S(2)}, u32[]{:S(2)}) %collective-permute-start) | collective-permute-done | bytes 262176 | tf_op jit(solution)/shard_map/ppermute | solution.py:447
  32.5 6.8 %collective-permute-done.10 = bf16[256,512]{1,0:T(8,128)(2,1)S(1)} collective-permute-done((bf16[256,512]{1,0:T(8,128)(2,1)S(1)}, bf16[256,512]{1,0:T(8,128)(2,1)S(1)}, u32[]{:S(2)}, u32[]{:S(2)}) %collective-permute-start.10) | collective-permute-done | bytes 262176 | tf_op jit(solution)/shard_map/ppermute | solution.py:530
  52.4 8.3 %collective-permute-done.7 = bf16[64,2048]{1,0:T(8,128)(2,1)S(1)} collective-permute-done((bf16[64,2048]{1,0:T(8,128)(2,1)S(1)}, bf16[64,2048]{1,0:T(8,128)(2,1)S(1)}, u32[]{:S(2)}, u32[]{:S(2)}) %collective-permute-start.7) | collective-permute-done | bytes 262176 | tf_op jit(solution)/shard_map/ppermute | solution.py:447
  81.0 5.7 %shard_map.255 = (bf16[512,2048]{1,0:T(8,128)(2,1)}, bf16[512,256]{1,0:T(8,128)(2,1)}, bf16[2,512,128]{2,1,0:T(8,128)(2,1)}, f32[2,512,128]{2,1,0:T(8,128)}, f32[512,128]{1,0:T(8,128)}) custom-call(s32[1]{0:T(128)} %bitcast.flag, bf16[64,2048]{1,0:T(8,128)(2,1)} %copy-done.9, bf16[64,2048]{1,0:T(8,128)(2,1)} %copy-done.52, ...), custom_call_target="tpu_custom_call" | custom-call | flops 1073741824 | bytes 8135684 | tf_op jit(solution)/shard_map/pallas_call | solution.py:577
  87.4 11.4 %collective-permute-done.21.mine_near.refs_1_.refs_9_.refs_14_ = bf16[1024,256]{1,0:T(8,128)(2,1)S(1)} collective-permute-done((bf16[1024,256]{1,0:T(8,128)(2,1)S(1)}, bf16[1024,256]{1,0:T(8,128)(2,1)S(1)}, u32[]{:S(2)}, u32[]{:S(2)}) %collective-permute-start.21) | collective-permute-done | bytes 524320 | tf_op jit(solution)/shard_map/ppermute | solution.py:447
  99.3 11.2 %collective-permute-done.18.second.refs_13_ = bf16[512,256]{1,0:T(8,128)(2,1)S(1)} collective-permute-done((bf16[512,256]{1,0:T(8,128)(2,1)}, bf16[512,256]{1,0:T(8,128)(2,1)S(1)}, u32[]{:S(2)}, u32[]{:S(2)}) %collective-permute-start.18) | collective-permute-done | bytes 262176 | tf_op jit(solution)/shard_map/ppermute | solution.py:447
  116.4 6.0 %all-to-all-start.1 = ((bf16[4,256,384]{2,1,0:T(8,128)(2,1)}), bf16[4,256,384]{2,1,0:T(8,128)(2,1)S(1)}, u32[]{:S(2)}, u32[]{:S(2)}) async-start(bf16[4,256,384]{2,1,0:T(8,128)(2,1)} %pad_maximum_fusion.8), calls=%async_computation.1 | async-start | bytes 1572864 | tf_op jit(solution)/shard_map/all_to_all | solution.py:510
  128.1 14.1 %collective-permute-done.17.refs_11_ = bf16[128,2048]{1,0:T(8,128)(2,1)} collective-permute-done((bf16[128,2048]{1,0:T(8,128)(2,1)}, bf16[128,2048]{1,0:T(8,128)(2,1)}, u32[]{:S(2)}, u32[]{:S(2)}) %collective-permute-start.17) | collective-permute-done | bytes 524320 | tf_op jit(solution)/shard_map/ppermute | solution.py:455
  143.1 9.7 %shard_map.257 = (bf16[2,512,128]{2,1,0:T(8,128)(2,1)}, f32[2,512,128]{2,1,0:T(8,128)}, f32[2,512,128]{2,1,0:T(8,128)}, bf16[64,2048]{1,0:T(8,128)(2,1)}, bf16[6...) custom-call(bf16[2,512,128]{2,1,0:T(8,128)(2,1)} %get-tuple-element., ...), custom_call_target="tpu_custom_call" | custom-call | flops 1073741824 | bytes 7610368 | tf_op jit(solution)/shard_map/pallas_call | solution.py:577
  156.8 7.1 %collective-permute-done.27 = bf16[64,2048]{1,0:T(8,128)(2,1)S(1)} collective-permute-done((bf16[64,2048]{1,0:T(8,128)(2,1)}, bf16[64,2048]{1,0:T(8,128)(2,1)S(1)}, u32[]{:S(2)}, u32[]{:S(2)}) %collective-permute-start.27) | collective-permute-done | bytes 262176 | tf_op jit(solution)/shard_map/ppermute | solution.py:455
  176.8 9.1 %collective-permute-done.31 = bf16[64,2048]{1,0:T(8,128)(2,1)S(1)} collective-permute-done((bf16[64,2048]{1,0:T(8,128)(2,1)S(1)}, bf16[64,2048]{1,0:T(8,128)(2,1)S(1)}, u32[]{:S(2)}, u32[]{:S(2)}) %collective-permute-start.31) | collective-permute-done | bytes 262176 | tf_op jit(solution)/shard_map/ppermute | solution.py:447
  188.0 15.5 %collective-permute-done.41.refs_17_ = bf16[1024,384]{1,0:T(8,128)(2,1)S(1)} collective-permute-done((bf16[1024,384]{1,0:T(8,128)(2,1)S(1)}, bf16[1024,384]{1,0:T(8,128)(2,1)S(1)}, u32[]{:S(2)}, u32[]{:S(2)}) %collective-permute-start.41) | collective-permute-done | bytes 786464 | tf_op jit(solution)/shard_map/ppermute | solution.py:447
  206.7 6.0 %collective-permute-done.35.refs_4_ = bf16[64,2048]{1,0:T(8,128)(2,1)S(1)} collective-permute-done((bf16[64,2048]{1,0:T(8,128)(2,1)S(1)}, bf16[64,2048]{1,0:T(8,128)(2,1)S(1)}, u32[]{:S(2)}, u32[]{:S(2)}) %collective-permute-start.35) | collective-permute-done | bytes 262176 | tf_op jit(solution)/shard_map/ppermute | solution.py:455
  234.7 20.8 %shard_map.258 = (bf16[512,384]{1,0:T(8,128)(2,1)}, bf16[512,384]{1,0:T(8,128)(2,1)}, bf16[512,768]{1,0:T(8,128)(2,1)}, bf16[512,768]{1,0:T(8,128)(2,1)}, bf16[6...) custom-call(bf16[64,2048]{1,0:T(8,128)(2,1)} %copy-done.68, ...), custom_call_target="tpu_custom_call" | custom-call | flops 9663676416 | bytes 24379392 | tf_op jit(solution)/shard_map/pallas_call | solution.py:577
  297.1 10.0 %collective-permute-done.55.refs_1_ = bf16[64,2048]{1,0:T(8,128)(2,1)S(1)} collective-permute-done((bf16[64,2048]{1,0:T(8,128)(2,1)S(1)}, bf16[64,2048]{1,0:T(8,128)(2,1)S(1)}, u32[]{:S(2)}, u32[]{:S(2)}) %collective-permute-start.55) | collective-permute-done | bytes 262176 | tf_op jit(solution)/shard_map/ppermute | solution.py:447
  317.2 5.2 collective-permute-done.61.refs_7_
  322.4 15.4 %shard_map.259 = (bf16[512,2048]{1,0:T(8,128)(2,1)}, bf16[2,512,128]{2,1,0:T(8,128)(2,1)}, bf16[2,512,128]{2,1,0:T(8,128)(2,1)}, bf16[2048,256]{1,0:T(8,128)(2,1)}, f32[1,128]{1,0:T(1,128)}) custom-call(bf16[64,2048]{1,0:T(8,128)(2,1)} %copy-done.59, bf16[64,2048]{1,0:T(8,128)(2,1)} %copy-done.90, bf16[64,2048]{1,0:T(8,128)(2,1)} %copy-done.93, ...), custom_call_target="tpu_custom_call" | custom-call | flops 2684354560 | bytes 12067840 | tf_op jit(solution)/shard_map/pallas_call | solution.py:577
  347.9 16.9 %collective-permute-done.54 = bf16[1024,384]{1,0:T(8,128)(2,1)S(1)} collective-permute-done((bf16[1024,384]{1,0:T(8,128)(2,1)S(1)}, bf16[1024,384]{1,0:T(8,128)(2,1)S(1)}, u32[]{:S(2)}, u32[]{:S(2)}) %collective-permute-start.54) | collective-permute-done | bytes 786464 | tf_op jit(solution)/shard_map/ppermute | solution.py:447
  379.0 7.7 %shard_map.260 = (bf16[512,256]{1,0:T(8,128)(2,1)}, bf16[512,256]{1,0:T(8,128)(2,1)}, bf16[64,2048]{1,0:T(8,128)(2,1)}, bf16[64,2048]{1,0:T(8,128)(2,1)}, bf16[6...) custom-call(s32[1]{0:T(128)} %bitcast.flag, ...), custom_call_target="tpu_custom_call" | custom-call | flops 1610612736 | bytes 10757124 | tf_op jit(solution)/shard_map/pallas_call | solution.py:577
  401.1 5.3 %collective-permute-done.71 = bf16[64,2048]{1,0:T(8,128)(2,1)S(1)} collective-permute-done((bf16[64,2048]{1,0:T(8,128)(2,1)S(1)}, bf16[64,2048]{1,0:T(8,128)(2,1)S(1)}, u32[]{:S(2)}, u32[]{:S(2)}) %collective-permute-start.71) | collective-permute-done | bytes 262176 | tf_op jit(solution)/shard_map/ppermute | solution.py:455
  433.1 20.2 %collective-permute-done.74 = bf16[64,2048]{1,0:T(8,128)(2,1)S(1)} collective-permute-done((bf16[64,2048]{1,0:T(8,128)(2,1)}, bf16[64,2048]{1,0:T(8,128)(2,1)S(1)}, u32[]{:S(2)}, u32[]{:S(2)}) %collective-permute-start.74) | collective-permute-done | bytes 262176 | tf_op jit(solution)/shard_map/ppermute | solution.py:447
  456.3 11.9 %collective-permute-done.82 = bf16[1024,256]{0,1:T(8,128)(2,1)S(1)} collective-permute-done((bf16[1024,256]{0,1:T(8,128)(2,1)S(1)}, bf16[1024,256]{0,1:T(8,128)(2,1)S(1)}, u32[]{:S(2)}, u32[]{:S(2)}) %collective-permute-start.82) | collective-permute-done | bytes 524320 | tf_op jit(solution)/shard_map/ppermute | solution.py:447
  483.5 5.8 %collective-permute-done.90 = f32[4352]{0:T(1024)S(1)} collective-permute-done((f32[4352]{0:T(1024)S(1)}, f32[4352]{0:T(1024)S(1)}, u32[]{:S(2)}, u32[]{:S(2)}) %collective-permute-start.90) | collective-permute-done | bytes 17440 | tf_op jit(solution)/shard_map/ppermute | solution.py:447
  507.9 7.7 %collective-permute-start.81 = (bf16[2,64,2048]{2,1,0:T(8,128)(2,1)S(1)}, bf16[2,64,2048]{2,1,0:T(8,128)(2,1)S(1)}, u32[]{:S(2)}, u32[]{:S(2)}) collective-permute-start(bf16[2,64,2048]{2,1,0:T(8,128)(2,1)S(1)} %get-tuple-element.318), channel_id=1, source_target_pairs={{0,1},{1,0},{2,3},{3,2},{4,5},{5,4},{6,7},{7,6},{8,9},{9,8},{10,11... | collective-permute-start | bytes 1572872 | tf_op jit(solution)/shard_map/ppermute | solution.py:447
  (555 shorter events, 268.9 us)
Async XLA Ops:
  11.1 34.4 %collective-permute-start.1 = (bf16[64,2048]{1,0:T(8,128)(2,1)S(1)}, bf16[64,2048]{1,0:T(8,128)(2,1)}, u32[]{:S(2)}, u32[]{:S(2)}) collective-permute-start(bf16[64,2048]{1,0:T(8,128)(2,1)S(1)} %constant_dynamic-update-slice_fusion.refs_0_), channel_id=1, source_target_pairs={{0,2},{2,0},{4,6},{6,4},{1,3},{3,1},{5,7},{7,5},{8,10},{10,8},{12,... | collective-permute-start | bytes 786440 | tf_op jit(solution)/shard_map/ppermute | solution.py:455
  12.6 26.7 %collective-permute-start.10 = (bf16[256,512]{1,0:T(8,128)(2,1)S(1)}, bf16[256,512]{1,0:T(8,128)(2,1)S(1)}, u32[]{:S(2)}, u32[]{:S(2)}) collective-permute-start(bf16[256,512]{1,0:T(8,128)(2,1)S(1)} %get-tuple-element.299), channel_id=1, source_target_pairs={{0,1},{1,17},{4,5},{5,21},{16,0},{17,16},{20,4},{21,20},{2,3},{3,1... | collective-permute-start | bytes 786440 | tf_op jit(solution)/shard_map/ppermute | solution.py:530
  64.4 46.1 %all-to-all-start = ((bf16[4,256,768]{2,1,0:T(8,128)(2,1)}), bf16[4,256,768]{2,1,0:T(8,128)(2,1)}, u32[]{:S(2)}, u32[]{:S(2)}) async-start(bf16[4,256,768]{2,1,0:T(8,128)(2,1)} %pad_maximum_fusion), calls=%async_computation | async-start | bytes 3145728 | tf_op jit(solution)/shard_map/all_to_all | solution.py:510
  72.7 40.0 %collective-permute-start.15 = (bf16[128,2048]{1,0:T(8,128)(2,1)}, bf16[128,2048]{1,0:T(8,128)(2,1)}, u32[]{:S(2)}, u32[]{:S(2)}) collective-permute-start(bf16[128,2048]{1,0:T(8,128)(2,1)} %pad_maximum_fusion.9.refs_8_), channel_id=1, source_target_pairs={{0,2},{2,0},{4,6},{6,4},{1,3},{3,1},{5,7},{7,5},{8,10},{10,8},{12,... | collective-permute-start | bytes 1572872 | tf_op jit(solution)/shard_map/ppermute | solution.py:455
  110.5 60.0 %collective-permute-start.30 = (bf16[1024,768]{1,0:T(8,128)(2,1)}, bf16[1024,768]{1,0:T(8,128)(2,1)}, u32[]{:S(2)}, u32[]{:S(2)}) collective-permute-start(bf16[1024,768]{1,0:T(8,128)(2,1)} %bitcast.31.refs_12_), channel_id=1, source_target_pairs={{0,8},{8,0},{1,9},{9,1},{2,10},{10,2},{3,11},{11,3},{4,12},{12,4},... | collective-permute-start | bytes 4718600 | tf_op jit(solution)/shard_map/ppermute | solution.py:447
  112.6 29.6 %collective-permute-start.17 = (bf16[128,2048]{1,0:T(8,128)(2,1)}, bf16[128,2048]{1,0:T(8,128)(2,1)}, u32[]{:S(2)}, u32[]{:S(2)}) collective-permute-start(bf16[128,2048]{1,0:T(8,128)(2,1)} %pad_maximum_fusion.9.refs_8_), channel_id=1, source_target_pairs={{0,6},{2,4},{4,2},{6,0},{1,7},{3,5},{5,3},{7,1},{8,14},{10,12},{12... | collective-permute-start | bytes 1572872 | tf_op jit(solution)/shard_map/ppermute | solution.py:455
  116.4 54.1 %all-to-all-start.1 = ((bf16[4,256,384]{2,1,0:T(8,128)(2,1)}), bf16[4,256,384]{2,1,0:T(8,128)(2,1)S(1)}, u32[]{:S(2)}, u32[]{:S(2)}) async-start(bf16[4,256,384]{2,1,0:T(8,128)(2,1)} %pad_maximum_fusion.8), calls=%async_computation.1 | async-start | bytes 1572864 | tf_op jit(solution)/shard_map/all_to_all | solution.py:510
  172.2 60.3 %collective-permute-start.40 = (bf16[1024,768]{1,0:T(8,128)(2,1)}, bf16[1024,768]{1,0:T(8,128)(2,1)S(1)}, u32[]{:S(2)}, u32[]{:S(2)}) collective-permute-start(bf16[1024,768]{1,0:T(8,128)(2,1)} %collective-permute-done.30.refs_13_), channel_id=1, source_target_pairs={{0,1},{1,0},{2,3},{3,2},{4,5},{5,4},{6,7},{7,6},{8,9},{9,8},{10,11... | collective-permute-start | bytes 4718600 | tf_op jit(solution)/shard_map/ppermute | solution.py:447
  172.7 47.8 %collective-permute-start.42 = (bf16[1024,384]{1,0:T(8,128)(2,1)S(1)}, bf16[1024,384]{1,0:T(8,128)(2,1)S(1)}, u32[]{:S(2)}, u32[]{:S(2)}) collective-permute-start(bf16[1024,384]{1,0:T(8,128)(2,1)S(1)} %bitcast.217), channel_id=1, source_target_pairs={{0,1},{1,0},{2,3},{3,2},{4,5},{5,4},{6,7},{7,6},{8,9},{9,8},{10,11... | collective-permute-start | bytes 2359304 | tf_op jit(solution)/shard_map/ppermute | solution.py:447
  176.3 27.2 %collective-permute-start.41 = (bf16[1024,384]{1,0:T(8,128)(2,1)S(1)}, bf16[1024,384]{1,0:T(8,128)(2,1)S(1)}, u32[]{:S(2)}, u32[]{:S(2)}) collective-permute-start(bf16[1024,384]{1,0:T(8,128)(2,1)S(1)} %bitcast.218), channel_id=1, source_target_pairs={{0,8},{8,0},{1,9},{9,1},{2,10},{10,2},{3,11},{11,3},{4,12},{12,4},... | collective-permute-start | bytes 2359304 | tf_op jit(solution)/shard_map/ppermute | solution.py:447
  203.5 29.1 %collective-permute-start.43 = (bf16[1024,384]{1,0:T(8,128)(2,1)S(1)}, bf16[1024,384]{1,0:T(8,128)(2,1)S(1)}, u32[]{:S(2)}, u32[]{:S(2)}) collective-permute-start(bf16[1024,384]{1,0:T(8,128)(2,1)S(1)} %collective-permute-done.41.refs_17_), channel_id=1, source_target_pairs={{0,1},{1,0},{2,3},{3,2},{4,5},{5,4},{6,7},{7,6},{8,9},{9,8},{10,11... | collective-permute-start | bytes 2359304 | tf_op jit(solution)/shard_map/ppermute | solution.py:447
  312.3 55.2 %collective-permute-start.53 = (bf16[1024,768]{1,0:T(8,128)(2,1)S(1)}, bf16[1024,768]{1,0:T(8,128)(2,1)S(1)}, u32[]{:S(2)}, u32[]{:S(2)}) collective-permute-start(bf16[1024,768]{1,0:T(8,128)(2,1)S(1)} %slice.401), channel_id=1, source_target_pairs={{0,8},{8,0},{1,9},{9,1},{2,10},{10,2},{3,11},{11,3},{4,12},{12,4},... | collective-permute-start | bytes 4718600 | tf_op jit(solution)/shard_map/ppermute | solution.py:447
  312.4 52.4 %collective-permute-start.54 = (bf16[1024,384]{1,0:T(8,128)(2,1)S(1)}, bf16[1024,384]{1,0:T(8,128)(2,1)S(1)}, u32[]{:S(2)}, u32[]{:S(2)}) collective-permute-start(bf16[1024,384]{1,0:T(8,128)(2,1)S(1)} %slice.402), channel_id=1, source_target_pairs={{0,8},{8,0},{1,9},{9,1},{2,10},{10,2},{3,11},{11,3},{4,12},{12,4},... | collective-permute-start | bytes 2359304 | tf_op jit(solution)/shard_map/ppermute | solution.py:447
  339.0 26.1 %collective-permute-start.62 = (bf16[128,2048]{1,0:T(8,128)(2,1)S(1)}, bf16[128,2048]{1,0:T(8,128)(2,1)S(1)}, u32[]{:S(2)}, u32[]{:S(2)}) collective-permute-start(bf16[128,2048]{1,0:T(8,128)(2,1)S(1)} %copy-done.84), channel_id=1, source_target_pairs={{0,2},{2,0},{4,6},{6,4},{1,3},{3,1},{5,7},{7,5},{8,10},{10,8},{12,... | collective-permute-start | bytes 1572872 | tf_op jit(solution)/shard_map/ppermute | solution.py:455
  339.3 25.7 %collective-permute-start.63 = (bf16[128,2048]{1,0:T(8,128)(2,1)S(1)}, bf16[128,2048]{1,0:T(8,128)(2,1)S(1)}, u32[]{:S(2)}, u32[]{:S(2)}) collective-permute-start(bf16[128,2048]{1,0:T(8,128)(2,1)S(1)} %copy-done.83), channel_id=1, source_target_pairs={{0,4},{2,6},{4,0},{6,2},{1,5},{3,7},{5,1},{7,3},{8,12},{10,14},{12... | collective-permute-start | bytes 1572872 | tf_op jit(solution)/shard_map/ppermute | solution.py:455
  369.1 48.6 %all-to-all-start.2 = ((bf16[4,256,768]{2,1,0:T(8,128)(2,1)}), bf16[4,256,768]{2,1,0:T(8,128)(2,1)}, u32[]{:S(2)}, u32[]{:S(2)}) async-start(bf16[4,256,768]{2,1,0:T(8,128)(2,1)} %bitcast.211), calls=%async_computation.2 | async-start | bytes 3145728 | tf_op jit(solution)/shard_map/all_to_all | solution.py:563
  374.8 39.7 %collective-permute-start.65 = (bf16[2048,256]{0,1:T(8,128)(2,1)S(1)}, bf16[2048,256]{0,1:T(8,128)(2,1)S(1)}, u32[]{:S(2)}, u32[]{:S(2)}) collective-permute-start(bf16[2048,256]{0,1:T(8,128)(2,1)S(1)} %pad_maximum_fusion.3), channel_id=1, source_target_pairs={{0,1},{1,0},{2,3},{3,2},{4,5},{5,4},{6,7},{7,6},{8,9},{9,8},{10,11... | collective-permute-start | bytes 3145736 | tf_op jit(solution)/shard_map/ppermute | solution.py:447
  389.5 32.8 %collective-permute-start.73 = (bf16[2048,256]{0,1:T(8,128)(2,1)}, bf16[2048,256]{0,1:T(8,128)(2,1)}, u32[]{:S(2)}, u32[]{:S(2)}) collective-permute-start(bf16[2048,256]{0,1:T(8,128)(2,1)} %convolution_convert_fusion.5), channel_id=1, source_target_pairs={{0,1},{1,0},{2,3},{3,2},{4,5},{5,4},{6,7},{7,6},{8,9},{9,8},{10,11... | collective-permute-start | bytes 3145736 | tf_op jit(solution)/shard_map/ppermute | solution.py:447
  398.2 71.0 %collective-permute-start.69 = (bf16[64,2048]{1,0:T(8,128)(2,1)}, bf16[64,2048]{1,0:T(8,128)(2,1)}, u32[]{:S(2)}, u32[]{:S(2)}) collective-permute-start(bf16[64,2048]{1,0:T(8,128)(2,1)} %slice.604), channel_id=1, source_target_pairs={{0,16},{16,0},{1,17},{17,1},{2,18},{18,2},{3,19},{19,3},{4,20},{20... | collective-permute-start | bytes 786440 | tf_op jit(solution)/shard_map/ppermute | solution.py:447
  406.4 24.7 %collective-permute-start.77 = (bf16[64,2048]{1,0:T(8,128)(2,1)}, bf16[64,2048]{1,0:T(8,128)(2,1)S(1)}, u32[]{:S(2)}, u32[]{:S(2)}) collective-permute-start(bf16[64,2048]{1,0:T(8,128)(2,1)} %get-tuple-element.243), channel_id=1, source_target_pairs={{0,2},{2,0},{4,6},{6,4},{1,3},{3,1},{5,7},{7,5},{8,10},{10,8},{12,... | collective-permute-start | bytes 786440 | tf_op jit(solution)/shard_map/ppermute | solution.py:455
  417.7 51.5 %all-to-all-start.3 = ((bf16[4,256,384]{2,1,0:T(8,128)(2,1)}), bf16[4,256,384]{2,1,0:T(8,128)(2,1)}, u32[]{:S(2)}, u32[]{:S(2)}) async-start(bf16[4,256,384]{2,1,0:T(8,128)(2,1)} %bitcast.214), calls=%async_computation.3 | async-start | bytes 1572864 | tf_op jit(solution)/shard_map/all_to_all | solution.py:563
  422.3 31.1 %collective-permute-start.74 = (bf16[64,2048]{1,0:T(8,128)(2,1)}, bf16[64,2048]{1,0:T(8,128)(2,1)S(1)}, u32[]{:S(2)}, u32[]{:S(2)}) collective-permute-start(bf16[64,2048]{1,0:T(8,128)(2,1)} %add_convert_fusion.9), channel_id=1, source_target_pairs={{0,16},{16,0},{1,17},{17,1},{2,18},{18,2},{3,19},{19,3},{4,20},{20... | collective-permute-start | bytes 786440 | tf_op jit(solution)/shard_map/ppermute | solution.py:447
  431.0 38.1 %collective-permute-start.68 = (bf16[1024,256]{0,1:T(8,128)(2,1)S(1)}, bf16[1024,256]{0,1:T(8,128)(2,1)S(1)}, u32[]{:S(2)}, u32[]{:S(2)}) collective-permute-start(bf16[1024,256]{0,1:T(8,128)(2,1)S(1)} %copy-done.39), channel_id=1, source_target_pairs={{0,8},{8,0},{1,9},{9,1},{2,10},{10,2},{3,11},{11,3},{4,12},{12,4},... | collective-permute-start | bytes 1572872 | tf_op jit(solution)/shard_map/ppermute | solution.py:447
  431.7 36.5 %collective-permute-start.82 = (bf16[1024,256]{0,1:T(8,128)(2,1)S(1)}, bf16[1024,256]{0,1:T(8,128)(2,1)S(1)}, u32[]{:S(2)}, u32[]{:S(2)}) collective-permute-start(bf16[1024,256]{0,1:T(8,128)(2,1)S(1)} %slice.485), channel_id=1, source_target_pairs={{0,8},{8,0},{1,9},{9,1},{2,10},{10,2},{3,11},{11,3},{4,12},{12,4},... | collective-permute-start | bytes 1572872 | tf_op jit(solution)/shard_map/ppermute | solution.py:447
  (182 other events, 2180.8 us)

commit v4 on v3

--- a/solution.py
+++ b/solution.py
@@ -1045,7 +1045,6 @@
     down_pieces = [down_parts[0]] + [side_swap(down_parts[i], i) for i in range(1, 4)]
     half = width // 2
     gate_up_got = pair_swap(gate_up_both[half:], "near")
-    down_got = pair_swap(down_both[half:], "near")
 
     all_branch, grad_gate, grad_query, grad_pairs, query_gain_part = kernel_call(
         attend_back_kernel,
@@ -1070,19 +1069,13 @@
         20 * tokens * 4 * tokens * low,
     )
     pair_other = pair_swap(grad_pairs[2 * tokens :], "c")
-    gate_up_got, down_got, down_pieces, normed_later = after(
-        (gate_up_got, down_got, down_pieces, normed), grad_pairs
-    )
+    gate_up_got, normed_later = after((gate_up_got, normed), grad_pairs)
     near_pairs = grad_pairs[: 2 * tokens].astype(f32) + pair_other.astype(f32)
     near_pairs = near_pairs.astype(bf16)
     pair_got = pair_swap(near_pairs[tokens:], "near")
     gate_up_rows = near_add(gate_up_both, gate_up_got)
-    down_got, gate_up_rows = after((down_got, gate_up_rows))
-    down_rows = near_add(down_both, down_got)
+    down_got = pair_swap(after(down_both, pair_got)[half:], "near")
     gate_up_grad = to_row_owners(gate_up_rows)
-    down_grad = to_row_owners(after(down_rows, gate_up_grad))
-    down_sums = sum_pieces(down_pieces)
-    down_far = pair_swap(down_sums[chunk_rows:].astype(bf16), "far")
     og_both = core_sum(
         *(
             jnp.concatenate(
@@ -1095,9 +1088,7 @@
             for i in range(2)
         )
     )
-    key_pre, gate_up_rows, down_rows, down_sums = after(
-        (key_pre, gate_up_rows, down_rows, down_sums)
-    )
+    key_pre, gate_up_rows = after((key_pre, gate_up_rows))
     og_got = pair_swap(after(og_both, pair_got)[half:], "near")
     outs = kernel_call(
         input_kernel,
@@ -1121,15 +1112,23 @@
     qk_both = (qk_sides[0].astype(f32) + qk_other.astype(f32)).astype(bf16)
     qk_got = pair_swap(qk_both[half:], "near")
     grad_far = pair_swap(away, "far")
+    grad_far, down_got = after((grad_far, down_got))
+    down_pieces = after(down_pieces, grad_far)
+    down_sums = sum_pieces(down_pieces)
+    down_far = pair_swap(down_sums[chunk_rows:].astype(bf16), "far")
+    down_rows = near_add(down_both, down_got)
+    grad_far, qk_got = after((grad_far, qk_got))
     grad_normed = sum_pieces(own + [grad_far])
     inv_one = lax.rsqrt(jnp.mean(hidden32 * hidden32, axis=1, keepdims=True) + epsilon)
     input_chunk = (grad_middle + norm_back(grad_normed, hidden32, inv_one, gain_one)).astype(bf16)
     input_grad = whole_block(input_chunk)
-    og_got, down_far, down_grad, gain_parts = after(
-        (og_got, down_far, down_grad, (input_gain_part, query_gain_part, key_gain_part)), grad_far
+    og_got = after(og_got, grad_far)
+    down_far, gain_parts = after(
+        (down_far, (input_gain_part, query_gain_part, key_gain_part)), grad_far
     )
     attn_rows = jnp.concatenate([near_add(qk_both, qk_got), near_add(og_both, og_got)], axis=1)
     attn_grad = from_head_owners(attn_rows, far, x, c)
+    down_grad = to_row_owners(after(down_rows, grad_far, gate_up_grad))
     qk_grad, og_grad = attn_grad[..., : 2 * low], attn_grad[..., 2 * low :]
     layer_out = whole_block((middle + down_sums[:chunk_rows] + down_far.astype(f32)).astype(bf16))
     gains = jnp.concatenate(
@@ -1141,7 +1140,7 @@
         ]
     )
     gains = (gains + plane_swap(gains, 1)) + (plane_swap(gains, 2) + plane_swap(gains, 3))
-    for axis in ("near", "y", "c"):
+    for axis in ("y", "c", "near"):
         gains = gains + pair_swap(gains, axis)
 
     def per_head(grad, start):

time: 532 us -> 520 us (0.977)
  waiting for transfers between devices: 246 us -> 232 us
    ppermute x40, waiting for transfers between devices: 143 us -> 116 us  [pair_swap(): return lax.ppermute(values, axis, [(0, 1), (1, 0)])]
    ppermute x42, waiting for transfers between devices: 90.3 us -> 96.8 us  [side_swap(): return lax.ppermute(values, ('x', 'y'), [(i, i ^ step) for i in range(4)])]
    unnamed x230 -> x196, local copies, waits for them, and re-layouts: 12.7 us -> 12.3 us
  transfers between devices with their start and end apart: 97 -> 97, of which waited for: 42 -> 46; matrix products, arithmetic and copies ran while one was open for 12% -> 12% of each run, Pallas kernels for 9% -> 9%
where the time goes in v4:
time: 520 us; the launch traced here: 511 us
  waiting for transfers between devices  232 us (45%)
  starting transfers between devices  123 us (24%)
  Pallas kernels  65.5 us (13%)
  other arithmetic  42 us (8%)
  local copies, waits for them, and re-layouts  28.2 us (5%)
  matrix products  16.5 us (3%)
    ppermute x40, waiting for transfers between devices, pair_swap(): return lax.ppermute(values, axis, [(0, 1), (1, 0)])  116 us
    ppermute x42, waiting for transfers between devices, side_swap(): return lax.ppermute(values, ('x', 'y'), [(i, i ^ step) for i in range(4)])  96.8 us
    pallas_call x6, Pallas kernels, kernel_call(): pl.pallas_call(body, out_shape=outs, in_specs=specs, out_specs=[pl.BlockS...  63.6 us
    ppermute x42, starting transfers between devices, side_swap(): return lax.ppermute(values, ('x', 'y'), [(i, i ^ step) for i in range(4)])  53.3 us
    ppermute x40, starting transfers between devices, pair_swap(): return lax.ppermute(values, axis, [(0, 1), (1, 0)])  32.8 us
    dot_general x10, matrix products, contract_first(): lax.dot_general(left, right, (((0,), (0,)), ((), ())), preferred_element_...  16.5 us
    unnamed x196, local copies, waits for them, and re-layouts  12.3 us
    all_to_all x2, starting transfers between devices, to_plane_owners(): lax.all_to_all(local.reshape(planes * rows, width), PLANE, split_axis=0,...  11.1 us
  transfers between devices with their start and end apart: 97, of which 46 were waited for; matrix products, arithmetic and copies ran while one was open for 12% of the time, Pallas kernels for 9%

profile of v4, /device:TPU:0, one launch (start us, length us, event | category | flops | bytes accessed | tf_op | source)
XLA Modules:
  0.0 510.6 jit_solution(1456790837102549814)
XLA Ops:
  15.2 12.8 %collective-permute-done.refs_1_ = bf16[64,2048]{1,0:T(8,128)(2,1)S(1)} collective-permute-done((bf16[64,2048]{1,0:T(8,128)(2,1)S(1)}, bf16[64,2048]{1,0:T(8,128)(2,1)S(1)}, u32[]{:S(2)}, u32[]{:S(2)}) %collective-permute-start) | collective-permute-done | bytes 262176 | tf_op jit(solution)/shard_map/ppermute | solution.py:447
  32.5 6.8 %collective-permute-done.10 = bf16[256,512]{1,0:T(8,128)(2,1)S(1)} collective-permute-done((bf16[256,512]{1,0:T(8,128)(2,1)S(1)}, bf16[256,512]{1,0:T(8,128)(2,1)S(1)}, u32[]{:S(2)}, u32[]{:S(2)}) %collective-permute-start.10) | collective-permute-done | bytes 262176 | tf_op jit(solution)/shard_map/ppermute | solution.py:530
  52.4 8.3 %collective-permute-done.7 = bf16[64,2048]{1,0:T(8,128)(2,1)S(1)} collective-permute-done((bf16[64,2048]{1,0:T(8,128)(2,1)S(1)}, bf16[64,2048]{1,0:T(8,128)(2,1)S(1)}, u32[]{:S(2)}, u32[]{:S(2)}) %collective-permute-start.7) | collective-permute-done | bytes 262176 | tf_op jit(solution)/shard_map/ppermute | solution.py:447
  64.4 5.0 all-to-all-start
  81.0 5.7 %shard_map.255 = (bf16[512,2048]{1,0:T(8,128)(2,1)}, bf16[512,256]{1,0:T(8,128)(2,1)}, bf16[2,512,128]{2,1,0:T(8,128)(2,1)}, f32[2,512,128]{2,1,0:T(8,128)}, f32[512,128]{1,0:T(8,128)}) custom-call(s32[1]{0:T(128)} %bitcast.flag, bf16[64,2048]{1,0:T(8,128)(2,1)} %copy-done.9, bf16[64,2048]{1,0:T(8,128)(2,1)} %copy-done.35, ...), custom_call_target="tpu_custom_call" | custom-call | flops 1073741824 | bytes 8135684 | tf_op jit(solution)/shard_map/pallas_call | solution.py:577
  87.5 11.3 %collective-permute-done.21.mine_near.refs_1_.refs_9_.refs_14_ = bf16[1024,256]{1,0:T(8,128)(2,1)S(1)} collective-permute-done((bf16[1024,256]{1,0:T(8,128)(2,1)S(1)}, bf16[1024,256]{1,0:T(8,128)(2,1)S(1)}, u32[]{:S(2)}, u32[]{:S(2)}) %collective-permute-start.21) | collective-permute-done | bytes 524320 | tf_op jit(solution)/shard_map/ppermute | solution.py:447
  99.3 11.3 %collective-permute-done.18.second.refs_13_ = bf16[512,256]{1,0:T(8,128)(2,1)S(1)} collective-permute-done((bf16[512,256]{1,0:T(8,128)(2,1)}, bf16[512,256]{1,0:T(8,128)(2,1)S(1)}, u32[]{:S(2)}, u32[]{:S(2)}) %collective-permute-start.18) | collective-permute-done | bytes 262176 | tf_op jit(solution)/shard_map/ppermute | solution.py:447
  116.4 6.1 %all-to-all-start.1 = ((bf16[4,256,384]{2,1,0:T(8,128)(2,1)}), bf16[4,256,384]{2,1,0:T(8,128)(2,1)S(1)}, u32[]{:S(2)}, u32[]{:S(2)}) async-start(bf16[4,256,384]{2,1,0:T(8,128)(2,1)} %pad_maximum_fusion.8), calls=%async_computation.1 | async-start | bytes 1572864 | tf_op jit(solution)/shard_map/all_to_all | solution.py:510
  128.1 14.2 %collective-permute-done.17.refs_11_ = bf16[128,2048]{1,0:T(8,128)(2,1)} collective-permute-done((bf16[128,2048]{1,0:T(8,128)(2,1)}, bf16[128,2048]{1,0:T(8,128)(2,1)}, u32[]{:S(2)}, u32[]{:S(2)}) %collective-permute-start.17) | collective-permute-done | bytes 524320 | tf_op jit(solution)/shard_map/ppermute | solution.py:455
  143.1 9.7 %shard_map.257 = (bf16[2,512,128]{2,1,0:T(8,128)(2,1)}, f32[2,512,128]{2,1,0:T(8,128)}, f32[2,512,128]{2,1,0:T(8,128)}, bf16[64,2048]{1,0:T(8,128)(2,1)}, bf16[6...) custom-call(bf16[2,512,128]{2,1,0:T(8,128)(2,1)} %get-tuple-element., ...), custom_call_target="tpu_custom_call" | custom-call | flops 1073741824 | bytes 7610368 | tf_op jit(solution)/shard_map/pallas_call | solution.py:577
  156.9 7.0 %collective-permute-done.27 = bf16[64,2048]{1,0:T(8,128)(2,1)S(1)} collective-permute-done((bf16[64,2048]{1,0:T(8,128)(2,1)}, bf16[64,2048]{1,0:T(8,128)(2,1)S(1)}, u32[]{:S(2)}, u32[]{:S(2)}) %collective-permute-start.27) | collective-permute-done | bytes 262176 | tf_op jit(solution)/shard_map/ppermute | solution.py:455
  176.8 9.2 %collective-permute-done.31 = bf16[64,2048]{1,0:T(8,128)(2,1)S(1)} collective-permute-done((bf16[64,2048]{1,0:T(8,128)(2,1)S(1)}, bf16[64,2048]{1,0:T(8,128)(2,1)S(1)}, u32[]{:S(2)}, u32[]{:S(2)}) %collective-permute-start.31) | collective-permute-done | bytes 262176 | tf_op jit(solution)/shard_map/ppermute | solution.py:447
  188.0 15.4 %collective-permute-done.41.refs_17_ = bf16[1024,384]{1,0:T(8,128)(2,1)S(1)} collective-permute-done((bf16[1024,384]{1,0:T(8,128)(2,1)S(1)}, bf16[1024,384]{1,0:T(8,128)(2,1)S(1)}, u32[]{:S(2)}, u32[]{:S(2)}) %collective-permute-start.41) | collective-permute-done | bytes 786464 | tf_op jit(solution)/shard_map/ppermute | solution.py:447
  206.8 5.9 %collective-permute-done.35.refs_4_ = bf16[64,2048]{1,0:T(8,128)(2,1)S(1)} collective-permute-done((bf16[64,2048]{1,0:T(8,128)(2,1)S(1)}, bf16[64,2048]{1,0:T(8,128)(2,1)S(1)}, u32[]{:S(2)}, u32[]{:S(2)}) %collective-permute-start.35) | collective-permute-done | bytes 262176 | tf_op jit(solution)/shard_map/ppermute | solution.py:455
  234.6 20.9 %shard_map.258 = (bf16[512,384]{1,0:T(8,128)(2,1)}, bf16[512,384]{1,0:T(8,128)(2,1)}, bf16[512,768]{1,0:T(8,128)(2,1)}, bf16[512,768]{1,0:T(8,128)(2,1)}, bf16[6...) custom-call(bf16[64,2048]{1,0:T(8,128)(2,1)} %copy-done.51, ...), custom_call_target="tpu_custom_call" | custom-call | flops 9663676416 | bytes 24379392 | tf_op jit(solution)/shard_map/pallas_call | solution.py:577
  297.3 10.0 %collective-permute-done.53.refs_1_ = bf16[64,2048]{1,0:T(8,128)(2,1)S(1)} collective-permute-done((bf16[64,2048]{1,0:T(8,128)(2,1)S(1)}, bf16[64,2048]{1,0:T(8,128)(2,1)S(1)}, u32[]{:S(2)}, u32[]{:S(2)}) %collective-permute-start.53) | collective-permute-done | bytes 262176 | tf_op jit(solution)/shard_map/ppermute | solution.py:447
  317.3 5.2 %collective-permute-done.59.refs_7_ = bf16[64,2048]{1,0:T(8,128)(2,1)} collective-permute-done((bf16[64,2048]{1,0:T(8,128)(2,1)S(1)}, bf16[64,2048]{1,0:T(8,128)(2,1)}, u32[]{:S(2)}, u32[]{:S(2)}) %collective-permute-start.59) | collective-permute-done | bytes 262176 | tf_op jit(solution)/shard_map/ppermute | solution.py:455
  322.5 15.3 %shard_map.259 = (bf16[512,2048]{1,0:T(8,128)(2,1)}, bf16[2,512,128]{2,1,0:T(8,128)(2,1)}, bf16[2,512,128]{2,1,0:T(8,128)(2,1)}, bf16[2048,256]{1,0:T(8,128)(2,1)}, f32[1,128]{1,0:T(1,128)}) custom-call(bf16[64,2048]{1,0:T(8,128)(2,1)} %copy-done.43, bf16[64,2048]{1,0:T(8,128)(2,1)} %copy-done.74, bf16[64,2048]{1,0:T(8,128)(2,1)} %copy-done.76, ...), custom_call_target="tpu_custom_call" | custom-call | flops 2684354560 | bytes 12067840 | tf_op jit(solution)/shard_map/pallas_call | solution.py:577
  356.6 7.7 %shard_map.260 = (bf16[512,256]{1,0:T(8,128)(2,1)}, bf16[512,256]{1,0:T(8,128)(2,1)}, bf16[64,2048]{1,0:T(8,128)(2,1)}, bf16[64,2048]{1,0:T(8,128)(2,1)}, bf16[6...) custom-call(s32[1]{0:T(128)} %bitcast.flag, ...), custom_call_target="tpu_custom_call" | custom-call | flops 1610612736 | bytes 10757124 | tf_op jit(solution)/shard_map/pallas_call | solution.py:577
  376.2 8.8 %collective-permute-done.67 = bf16[64,2048]{1,0:T(8,128)(2,1)S(1)} collective-permute-done((bf16[64,2048]{1,0:T(8,128)(2,1)S(1)}, bf16[64,2048]{1,0:T(8,128)(2,1)S(1)}, u32[]{:S(2)}, u32[]{:S(2)}) %collective-permute-start.67) | collective-permute-done | bytes 262176 | tf_op jit(solution)/shard_map/ppermute | solution.py:455
  404.9 13.2 %collective-permute-done.71 = bf16[1024,384]{1,0:T(8,128)(2,1)} collective-permute-done((bf16[1024,384]{1,0:T(8,128)(2,1)}, bf16[1024,384]{1,0:T(8,128)(2,1)}, u32[]{:S(2)}, u32[]{:S(2)}) %collective-permute-start.71) | collective-permute-done | bytes 786464 | tf_op jit(solution)/shard_map/ppermute | solution.py:447
  427.8 11.4 %collective-permute-done.73 = bf16[1024,256]{1,0:T(8,128)(2,1)} collective-permute-done((bf16[1024,256]{1,0:T(8,128)(2,1)S(1)}, bf16[1024,256]{1,0:T(8,128)(2,1)}, u32[]{:S(2)}, u32[]{:S(2)}) %collective-permute-start.73) | collective-permute-done | bytes 524320 | tf_op jit(solution)/shard_map/ppermute | solution.py:447
  441.8 6.4 %all-to-all-start.3 = ((bf16[4,256,384]{2,1,0:T(8,128)(2,1)}), bf16[4,256,384]{2,1,0:T(8,128)(2,1)}, u32[]{:S(2)}, u32[]{:S(2)}) async-start(bf16[4,256,384]{2,1,0:T(8,128)(2,1)} %bitcast.214), calls=%async_computation.3 | async-start | bytes 1572864 | tf_op jit(solution)/shard_map/all_to_all | solution.py:563
  487.3 13.6 %collective-permute-start.80 = (bf16[2,64,2048]{2,1,0:T(8,128)(2,1)S(1)}, bf16[2,64,2048]{2,1,0:T(8,128)(2,1)S(1)}, u32[]{:S(2)}, u32[]{:S(2)}) collective-permute-start(bf16[2,64,2048]{2,1,0:T(8,128)(2,1)S(1)} %get-tuple-element.318), channel_id=1, source_target_pairs={{0,1},{1,0},{2,3},{3,2},{4,5},{5,4},{6,7},{7,6},{8,9},{9,8},{10,11... | collective-permute-start | bytes 1572872 | tf_op jit(solution)/shard_map/ppermute | solution.py:447
  (520 shorter events, 266.4 us)
Async XLA Ops:
  3.6 24.5 %collective-permute-start = (bf16[64,2048]{1,0:T(8,128)(2,1)S(1)}, bf16[64,2048]{1,0:T(8,128)(2,1)S(1)}, u32[]{:S(2)}, u32[]{:S(2)}) collective-permute-start(bf16[64,2048]{1,0:T(8,128)(2,1)S(1)} %constant_dynamic-update-slice_fusion.refs_0_), channel_id=1, source_target_pairs={{0,16},{16,0},{1,17},{17,1},{2,18},{18,2},{3,19},{19,3},{4,20},{20... | collective-permute-start | bytes 786440 | tf_op jit(solution)/shard_map/ppermute | solution.py:447
  11.1 34.4 %collective-permute-start.1 = (bf16[64,2048]{1,0:T(8,128)(2,1)S(1)}, bf16[64,2048]{1,0:T(8,128)(2,1)}, u32[]{:S(2)}, u32[]{:S(2)}) collective-permute-start(bf16[64,2048]{1,0:T(8,128)(2,1)S(1)} %constant_dynamic-update-slice_fusion.refs_0_), channel_id=1, source_target_pairs={{0,2},{2,0},{4,6},{6,4},{1,3},{3,1},{5,7},{7,5},{8,10},{10,8},{12,... | collective-permute-start | bytes 786440 | tf_op jit(solution)/shard_map/ppermute | solution.py:455
  12.6 26.7 %collective-permute-start.10 = (bf16[256,512]{1,0:T(8,128)(2,1)S(1)}, bf16[256,512]{1,0:T(8,128)(2,1)S(1)}, u32[]{:S(2)}, u32[]{:S(2)}) collective-permute-start(bf16[256,512]{1,0:T(8,128)(2,1)S(1)} %get-tuple-element.299), channel_id=1, source_target_pairs={{0,1},{1,17},{4,5},{5,21},{16,0},{17,16},{20,4},{21,20},{2,3},{3,1... | collective-permute-start | bytes 786440 | tf_op jit(solution)/shard_map/ppermute | solution.py:530
  64.4 46.2 %all-to-all-start = ((bf16[4,256,768]{2,1,0:T(8,128)(2,1)}), bf16[4,256,768]{2,1,0:T(8,128)(2,1)}, u32[]{:S(2)}, u32[]{:S(2)}) async-start(bf16[4,256,768]{2,1,0:T(8,128)(2,1)} %pad_maximum_fusion), calls=%async_computation | async-start | bytes 3145728 | tf_op jit(solution)/shard_map/all_to_all | solution.py:510
  72.7 39.9 %collective-permute-start.15 = (bf16[128,2048]{1,0:T(8,128)(2,1)}, bf16[128,2048]{1,0:T(8,128)(2,1)}, u32[]{:S(2)}, u32[]{:S(2)}) collective-permute-start(bf16[128,2048]{1,0:T(8,128)(2,1)} %pad_maximum_fusion.9.refs_8_), channel_id=1, source_target_pairs={{0,2},{2,0},{4,6},{6,4},{1,3},{3,1},{5,7},{7,5},{8,10},{10,8},{12,... | collective-permute-start | bytes 1572872 | tf_op jit(solution)/shard_map/ppermute | solution.py:455
  74.2 24.5 %collective-permute-start.21 = (bf16[1024,256]{1,0:T(8,128)(2,1)S(1)}, bf16[1024,256]{1,0:T(8,128)(2,1)S(1)}, u32[]{:S(2)}, u32[]{:S(2)}) collective-permute-start(bf16[1024,256]{1,0:T(8,128)(2,1)S(1)} %get-tuple-element.156.mine_own.refs_0_.refs_8_.refs_13_), channel_id=1, source_target_pairs={{0,8},{8,0},{1,9},{9,1},{2,10},{10,2},{3,11},{11,3},{4,12},{12,4},... | collective-permute-start | bytes 1572872 | tf_op jit(solution)/shard_map/ppermute | solution.py:447
  110.6 59.9 %collective-permute-start.30 = (bf16[1024,768]{1,0:T(8,128)(2,1)}, bf16[1024,768]{1,0:T(8,128)(2,1)}, u32[]{:S(2)}, u32[]{:S(2)}) collective-permute-start(bf16[1024,768]{1,0:T(8,128)(2,1)} %bitcast.31.refs_12_), channel_id=1, source_target_pairs={{0,8},{8,0},{1,9},{9,1},{2,10},{10,2},{3,11},{11,3},{4,12},{12,4},... | collective-permute-start | bytes 4718600 | tf_op jit(solution)/shard_map/ppermute | solution.py:447
  112.7 29.6 %collective-permute-start.17 = (bf16[128,2048]{1,0:T(8,128)(2,1)}, bf16[128,2048]{1,0:T(8,128)(2,1)}, u32[]{:S(2)}, u32[]{:S(2)}) collective-permute-start(bf16[128,2048]{1,0:T(8,128)(2,1)} %pad_maximum_fusion.9.refs_8_), channel_id=1, source_target_pairs={{0,6},{2,4},{4,2},{6,0},{1,7},{3,5},{5,3},{7,1},{8,14},{10,12},{12... | collective-permute-start | bytes 1572872 | tf_op jit(solution)/shard_map/ppermute | solution.py:455
  116.4 54.1 %all-to-all-start.1 = ((bf16[4,256,384]{2,1,0:T(8,128)(2,1)}), bf16[4,256,384]{2,1,0:T(8,128)(2,1)S(1)}, u32[]{:S(2)}, u32[]{:S(2)}) async-start(bf16[4,256,384]{2,1,0:T(8,128)(2,1)} %pad_maximum_fusion.8), calls=%async_computation.1 | async-start | bytes 1572864 | tf_op jit(solution)/shard_map/all_to_all | solution.py:510
  172.2 60.3 %collective-permute-start.40 = (bf16[1024,768]{1,0:T(8,128)(2,1)}, bf16[1024,768]{1,0:T(8,128)(2,1)S(1)}, u32[]{:S(2)}, u32[]{:S(2)}) collective-permute-start(bf16[1024,768]{1,0:T(8,128)(2,1)} %collective-permute-done.30.refs_13_), channel_id=1, source_target_pairs={{0,1},{1,0},{2,3},{3,2},{4,5},{5,4},{6,7},{7,6},{8,9},{9,8},{10,11... | collective-permute-start | bytes 4718600 | tf_op jit(solution)/shard_map/ppermute | solution.py:447
  172.7 47.8 %collective-permute-start.42 = (bf16[1024,384]{1,0:T(8,128)(2,1)S(1)}, bf16[1024,384]{1,0:T(8,128)(2,1)S(1)}, u32[]{:S(2)}, u32[]{:S(2)}) collective-permute-start(bf16[1024,384]{1,0:T(8,128)(2,1)S(1)} %bitcast.217), channel_id=1, source_target_pairs={{0,1},{1,0},{2,3},{3,2},{4,5},{5,4},{6,7},{7,6},{8,9},{9,8},{10,11... | collective-permute-start | bytes 2359304 | tf_op jit(solution)/shard_map/ppermute | solution.py:447
  176.3 27.2 %collective-permute-start.41 = (bf16[1024,384]{1,0:T(8,128)(2,1)S(1)}, bf16[1024,384]{1,0:T(8,128)(2,1)S(1)}, u32[]{:S(2)}, u32[]{:S(2)}) collective-permute-start(bf16[1024,384]{1,0:T(8,128)(2,1)S(1)} %bitcast.218), channel_id=1, source_target_pairs={{0,8},{8,0},{1,9},{9,1},{2,10},{10,2},{3,11},{11,3},{4,12},{12,4},... | collective-permute-start | bytes 2359304 | tf_op jit(solution)/shard_map/ppermute | solution.py:447
  203.5 29.0 %collective-permute-start.43 = (bf16[1024,384]{1,0:T(8,128)(2,1)S(1)}, bf16[1024,384]{1,0:T(8,128)(2,1)S(1)}, u32[]{:S(2)}, u32[]{:S(2)}) collective-permute-start(bf16[1024,384]{1,0:T(8,128)(2,1)S(1)} %collective-permute-done.41.refs_17_), channel_id=1, source_target_pairs={{0,1},{1,0},{2,3},{3,2},{4,5},{5,4},{6,7},{7,6},{8,9},{9,8},{10,11... | collective-permute-start | bytes 2359304 | tf_op jit(solution)/shard_map/ppermute | solution.py:447
  310.9 35.8 %collective-permute-start.65 = (bf16[1024,768]{1,0:T(8,128)(2,1)S(1)}, bf16[1024,768]{1,0:T(8,128)(2,1)}, u32[]{:S(2)}, u32[]{:S(2)}) collective-permute-start(bf16[1024,768]{1,0:T(8,128)(2,1)S(1)} %slice.422), channel_id=1, source_target_pairs={{0,8},{8,0},{1,9},{9,1},{2,10},{10,2},{3,11},{11,3},{4,12},{12,4},... | collective-permute-start | bytes 4718600 | tf_op jit(solution)/shard_map/ppermute | solution.py:447
  349.6 46.8 %all-to-all-start.2 = ((bf16[4,256,768]{2,1,0:T(8,128)(2,1)}), bf16[4,256,768]{2,1,0:T(8,128)(2,1)}, u32[]{:S(2)}, u32[]{:S(2)}) async-start(bf16[4,256,768]{2,1,0:T(8,128)(2,1)} %bitcast.211), calls=%async_computation.2 | async-start | bytes 3145728 | tf_op jit(solution)/shard_map/all_to_all | solution.py:563
  365.5 28.8 %collective-permute-start.81 = (bf16[2048,256]{1,0:T(8,128)(2,1)S(1)}, bf16[2048,256]{1,0:T(8,128)(2,1)S(1)}, u32[]{:S(2)}, u32[]{:S(2)}) collective-permute-start(bf16[2048,256]{1,0:T(8,128)(2,1)S(1)} %pad_maximum_fusion.5), channel_id=1, source_target_pairs={{0,1},{1,0},{2,3},{3,2},{4,5},{5,4},{6,7},{7,6},{8,9},{9,8},{10,11... | collective-permute-start | bytes 3145736 | tf_op jit(solution)/shard_map/ppermute | solution.py:447
  367.1 29.3 %collective-permute-start.69 = (bf16[2048,256]{1,0:T(8,128)(2,1)S(1)}, bf16[2048,256]{1,0:T(8,128)(2,1)}, u32[]{:S(2)}, u32[]{:S(2)}) collective-permute-start(bf16[2048,256]{1,0:T(8,128)(2,1)S(1)} %convolution_convert_fusion.5), channel_id=1, source_target_pairs={{0,1},{1,0},{2,3},{3,2},{4,5},{5,4},{6,7},{7,6},{8,9},{9,8},{10,11... | collective-permute-start | bytes 3145736 | tf_op jit(solution)/shard_map/ppermute | solution.py:447
  375.9 43.9 %collective-permute-start.60 = (bf16[128,2048]{1,0:T(8,128)(2,1)}, bf16[128,2048]{1,0:T(8,128)(2,1)}, u32[]{:S(2)}, u32[]{:S(2)}) collective-permute-start(bf16[128,2048]{1,0:T(8,128)(2,1)} %get-tuple-element.203), channel_id=1, source_target_pairs={{0,2},{2,0},{4,6},{6,4},{1,3},{3,1},{5,7},{7,5},{8,10},{10,8},{12,... | collective-permute-start | bytes 1572872 | tf_op jit(solution)/shard_map/ppermute | solution.py:455
  384.9 36.7 %collective-permute-start.61 = (bf16[128,2048]{1,0:T(8,128)(2,1)}, bf16[128,2048]{1,0:T(8,128)(2,1)}, u32[]{:S(2)}, u32[]{:S(2)}) collective-permute-start(bf16[128,2048]{1,0:T(8,128)(2,1)} %get-tuple-element.204), channel_id=1, source_target_pairs={{0,4},{2,6},{4,0},{6,2},{1,5},{3,7},{5,1},{7,3},{8,12},{10,14},{12... | collective-permute-start | bytes 1572872 | tf_op jit(solution)/shard_map/ppermute | solution.py:455
  391.3 30.5 %collective-permute-start.62 = (bf16[128,2048]{1,0:T(8,128)(2,1)}, bf16[128,2048]{1,0:T(8,128)(2,1)}, u32[]{:S(2)}, u32[]{:S(2)}) collective-permute-start(bf16[128,2048]{1,0:T(8,128)(2,1)} %get-tuple-element.205), channel_id=1, source_target_pairs={{0,6},{2,4},{4,2},{6,0},{1,7},{3,5},{5,3},{7,1},{8,14},{10,12},{12... | collective-permute-start | bytes 1572872 | tf_op jit(solution)/shard_map/ppermute | solution.py:455
  418.1 40.4 %collective-permute-start.76 = (bf16[64,2048]{1,0:T(8,128)(2,1)}, bf16[64,2048]{1,0:T(8,128)(2,1)}, u32[]{:S(2)}, u32[]{:S(2)}) collective-permute-start(bf16[64,2048]{1,0:T(8,128)(2,1)} %get-tuple-element.239), channel_id=1, source_target_pairs={{0,2},{2,0},{4,6},{6,4},{1,3},{3,1},{5,7},{7,5},{8,10},{10,8},{12,... | collective-permute-start | bytes 786440 | tf_op jit(solution)/shard_map/ppermute | solution.py:455
  419.3 39.3 %collective-permute-start.77 = (bf16[64,2048]{1,0:T(8,128)(2,1)}, bf16[64,2048]{1,0:T(8,128)(2,1)}, u32[]{:S(2)}, u32[]{:S(2)}) collective-permute-start(bf16[64,2048]{1,0:T(8,128)(2,1)} %get-tuple-element.240), channel_id=1, source_target_pairs={{0,4},{2,6},{4,0},{6,2},{1,5},{3,7},{5,1},{7,3},{8,12},{10,14},{12... | collective-permute-start | bytes 786440 | tf_op jit(solution)/shard_map/ppermute | solution.py:455
  419.8 38.8 %collective-permute-start.78 = (bf16[64,2048]{1,0:T(8,128)(2,1)}, bf16[64,2048]{1,0:T(8,128)(2,1)}, u32[]{:S(2)}, u32[]{:S(2)}) collective-permute-start(bf16[64,2048]{1,0:T(8,128)(2,1)} %get-tuple-element.241), channel_id=1, source_target_pairs={{0,6},{2,4},{4,2},{6,0},{1,7},{3,5},{5,3},{7,1},{8,14},{10,12},{12... | collective-permute-start | bytes 786440 | tf_op jit(solution)/shard_map/ppermute | solution.py:455
  441.8 65.7 %all-to-all-start.3 = ((bf16[4,256,384]{2,1,0:T(8,128)(2,1)}), bf16[4,256,384]{2,1,0:T(8,128)(2,1)}, u32[]{:S(2)}, u32[]{:S(2)}) async-start(bf16[4,256,384]{2,1,0:T(8,128)(2,1)} %bitcast.214), calls=%async_computation.3 | async-start | bytes 1572864 | tf_op jit(solution)/shard_map/all_to_all | solution.py:563
  (165 other events, 2007.9 us)

commit v5 on v4

--- a/solution.py
+++ b/solution.py
@@ -567,8 +567,9 @@
 VMEM_BYTES = 56 * 1024 * 1024
 
 
-def kernel_call(body, operands, outs, scratch=(), flags=None, flops=0):
-    specs = [pl.BlockSpec(memory_space=pltpu.VMEM)] * len(operands)
+def kernel_call(body, operands, outs, scratch=(), flags=None, flops=0, far_operands=0):
+    specs = [pl.BlockSpec(memory_space=pltpu.VMEM)] * (len(operands) - far_operands)
+    specs += [pl.BlockSpec(memory_space=pl.ANY)] * far_operands
     if flags is not None:
         operands = [flags] + list(operands)
         specs = [pl.BlockSpec(memory_space=pltpu.SMEM)] + specs
@@ -679,8 +680,17 @@
 
 def ffn_kernel(*refs):
     chunks, cotangent, gate_up, down = refs[:8], refs[8:12], refs[12:16], refs[16:20]
-    acts, grads, two_parts, down_parts = refs[20:22], refs[22:24], refs[24:32], refs[32:36]
-    normed_two, cot, total = refs[36:]
+    acts, grads, two_parts = refs[20:22], refs[22:24], refs[24:32]
+    normed_two, cot, total = refs[32:35]
+    gate_up_here, down_here, sems = refs[35:39], refs[39:43], refs[43]
+    copies = []
+    for side in range(2):
+        for i in (2 * side, 2 * side + 1):
+            copies.append(pltpu.make_async_copy(gate_up[i], gate_up_here[i], sems.at[len(copies)]))
+        for i in (2 * side, 2 * side + 1):
+            copies.append(pltpu.make_async_copy(down[i], down_here[i], sems.at[len(copies)]))
+    for copy in copies:
+        copy.start()
     rows = chunks[0].shape[0]
     for i in range(8):
         normed_two[i * rows : (i + 1) * rows, :] = chunks[i][...]
@@ -688,19 +698,20 @@
     for i in range(4):
         cot[i * rows : (i + 1) * rows, :] = cotangent[i][...]
     half = cot.shape[1] // 2
-    units = down[0].shape[1]
+    units = down_here[0].shape[1]
     tile = cot.shape[0] // 2
-
-    def step(i, carry):
-        at = pl.multiple_of(i * tile, tile)
-        rows_at = pl.ds(at, tile)
-        for side in range(2):
-            wide = [gate_up[2 * side][...], gate_up[2 * side + 1][...]]
-            pre = dot_nn(normed_two[rows_at, :half], wide[0]) + dot_nn(
-                normed_two[rows_at, half:], wide[1]
+    for side in range(2):
+        for copy in copies[4 * side : 4 * side + 4]:
+            copy.wait()
+
+        def step(i, carry, side=side):
+            rows_at = pl.ds(pl.multiple_of(i * tile, tile), tile)
+            own, near = 2 * side, 2 * side + 1
+            pre = dot_nn(normed_two[rows_at, :half], gate_up_here[own][...]) + dot_nn(
+                normed_two[rows_at, half:], gate_up_here[near][...]
             )
-            grad = dot_nn(cot[rows_at, :half], down[2 * side][...]) + dot_nn(
-                cot[rows_at, half:], down[2 * side + 1][...]
+            grad = dot_nn(cot[rows_at, :half], down_here[own][...]) + dot_nn(
+                cot[rows_at, half:], down_here[near][...]
             )
             gate, up = pre[:, :units], pre[:, units:]
             act = sigmoid(gate)
@@ -710,22 +721,30 @@
                 grad * up * act * (1.0 + gate * (1.0 - act))
             ).astype(jnp.bfloat16)
             grads[side][rows_at, units:] = (grad * silu).astype(jnp.bfloat16)
-        for near in range(2):
-            total[0, rows_at, near * half : (near + 1) * half] = contract_last(
-                grads[0][rows_at, :], gate_up[near][...]
-            ) + contract_last(grads[1][rows_at, :], gate_up[2 + near][...])
-            total[1, rows_at, near * half : (near + 1) * half] = contract_last(
-                acts[0][rows_at, :], down[near][...]
-            ) + contract_last(acts[1][rows_at, :], down[2 + near][...])
-        return carry
-
-    lax.fori_loop(0, 2, step, 0)
+            for i_near in range(2):
+                part = contract_last(
+                    grads[side][rows_at, :], gate_up_here[2 * side + i_near][...]
+                )
+                columns = slice(i_near * half, (i_near + 1) * half)
+                total[rows_at, columns] = part if side == 0 else total[rows_at, columns] + part
+            return carry
+
+        lax.fori_loop(0, 2, step, 0)
     rows = two_parts[0].shape[0]
     for i in range(8):
-        two_parts[i][...] = total[0, i * rows : (i + 1) * rows, :].astype(jnp.bfloat16)
-    rows = down_parts[0].shape[0]
+        two_parts[i][...] = total[i * rows : (i + 1) * rows, :].astype(jnp.bfloat16)
+
+
+def down_kernel(*refs):
+    acts, down, parts, total = refs[:2], refs[2:6], refs[6:10], refs[10]
+    half = total.shape[1] // 2
+    for near in range(2):
+        total[:, near * half : (near + 1) * half] = contract_last(
+            acts[0][...], down[near][...]
+        ) + contract_last(acts[1][...], down[2 + near][...])
+    rows = parts[0].shape[0]
     for i in range(4):
-        down_parts[i][...] = total[1, i * rows : (i + 1) * rows, :].astype(jnp.bfloat16)
+        parts[i][...] = total[i * rows : (i + 1) * rows, :].astype(jnp.bfloat16)
 
 
 def attend_back_kernel(*refs):
@@ -1014,17 +1033,32 @@
         normed_two_pieces + cotangents + gate_up + down,
         [shaped((tokens, units), bf16)] * 2
         + [shaped((tokens, 2 * units), bf16)] * 2
-        + [shaped((chunk_rows, width), bf16)] * 8
-        + [shaped((2 * chunk_rows, width), bf16)] * 4
-        + [shaped((tokens, width), bf16)] * 2,
-        [pltpu.VMEM((2, tokens, width), f32)],
+        + [shaped((chunk_rows, width), bf16)] * 8,
+        [pltpu.VMEM((tokens, width), bf16)] * 2
+        + [pltpu.VMEM((tokens, width), f32)]
+        + [pltpu.VMEM((width // 2, 2 * units), bf16)] * 4
+        + [pltpu.VMEM((width // 2, units), bf16)] * 4
+        + [pltpu.SemaphoreType.DMA((8,))],
         None,
-        24 * tokens * width * units,
-    )
-    hidden_acts, grad_ffn, two_parts, down_parts = outs[:2], outs[2:4], outs[4:12], outs[12:16]
-    normed_two, all_cotangent = outs[16:]
+        20 * tokens * width * units,
+        8,
+    )
+    hidden_acts, grad_ffn, two_parts = outs[:2], outs[2:4], outs[4:12]
     away, own = sum_sends(two_parts)
     two_far = pair_swap(sum_pieces(away).astype(bf16), "far")
+    pieces_late, hidden_acts, grad_ffn, cotangents = after(
+        (normed_two_pieces, hidden_acts, grad_ffn, cotangents), two_parts[1]
+    )
+    normed_two = jnp.concatenate(pieces_late, axis=0)
+    all_cotangent = jnp.concatenate(cotangents, axis=0)
+    down_parts = kernel_call(
+        down_kernel,
+        list(hidden_acts) + list(down),
+        [shaped((2 * chunk_rows, width), bf16)] * 4,
+        [pltpu.VMEM((tokens, width), f32)],
+        None,
+        4 * tokens * width * units,
+    )
     two_away = own, two_far
     gate_up_both = core_sum(*(contract_first(normed_two, g).astype(bf16) for g in grad_ffn))
     down_both = core_sum(*(contract_first(all_cotangent, act).astype(bf16) for act in hidden_acts))
@@ -1034,9 +1068,11 @@
 
     def whole_block(chunk):
         chunk = from_own_first(chunk, odd_near)
-        by_y = jnp.stack([chunk, pair_swap(chunk, "y")])
+        other = pair_swap(chunk, "y")
+        by_y = jnp.stack([chunk, other])
         by_core = jnp.stack([by_y, pair_swap(by_y, "c")], axis=1)
-        return flip_if(flip_if(by_core, 1, c == 1), 0, y == 1).reshape(block_rows, width)
+        whole = flip_if(flip_if(by_core, 1, c == 1), 0, y == 1).reshape(block_rows, width)
+        return other, whole
 
     grad_middle = cotangent.astype(f32) + norm_back(grad_normed_two, middle, inv_two, gain_two)
     grad_branch = grad_middle.astype(bf16)
@@ -1088,7 +1124,7 @@
             for i in range(2)
         )
     )
-    key_pre, gate_up_rows = after((key_pre, gate_up_rows))
+    key_pre, gate_up_rows, down_pieces = after((key_pre, gate_up_rows, down_pieces))
     og_got = pair_swap(after(og_both, pair_got)[half:], "near")
     outs = kernel_call(
         input_kernel,
@@ -1121,16 +1157,17 @@
     grad_normed = sum_pieces(own + [grad_far])
     inv_one = lax.rsqrt(jnp.mean(hidden32 * hidden32, axis=1, keepdims=True) + epsilon)
     input_chunk = (grad_middle + norm_back(grad_normed, hidden32, inv_one, gain_one)).astype(bf16)
-    input_grad = whole_block(input_chunk)
+    input_y, input_grad = whole_block(input_chunk)
     og_got = after(og_got, grad_far)
-    down_far, gain_parts = after(
-        (down_far, (input_gain_part, query_gain_part, key_gain_part)), grad_far
-    )
+    gain_parts = after((input_gain_part, query_gain_part, key_gain_part), input_y)
+    down_far = after(down_far, grad_far)
     attn_rows = jnp.concatenate([near_add(qk_both, qk_got), near_add(og_both, og_got)], axis=1)
     attn_grad = from_head_owners(attn_rows, far, x, c)
     down_grad = to_row_owners(after(down_rows, grad_far, gate_up_grad))
     qk_grad, og_grad = attn_grad[..., : 2 * low], attn_grad[..., 2 * low :]
-    layer_out = whole_block((middle + down_sums[:chunk_rows] + down_far.astype(f32)).astype(bf16))
+    layer_y, layer_out = whole_block(
+        (middle + down_sums[:chunk_rows] + down_far.astype(f32)).astype(bf16)
+    )
     gains = jnp.concatenate(
         [
             from_own_first(gain_parts[0][0] / gain_one, odd_near),

time: 520 us -> 519 us (level)
  waiting for transfers between devices: 232 us -> 202 us
  starting transfers between devices: 123 us -> 145 us
  local copies, waits for them, and re-layouts: 28.2 us -> 35.2 us
    ppermute x3, starting transfers between devices: 3.8 us -> 26.8 us  [plane_swap(): return lax.ppermute(values, PLANE, [(i, i ^ step) for i in range(PLANES)])]
    ppermute x40, waiting for transfers between devices: 116 us -> 102 us  [pair_swap(): return lax.ppermute(values, axis, [(0, 1), (1, 0)])]
    ppermute x42, waiting for transfers between devices: 96.8 us -> 89.5 us  [side_swap(): return lax.ppermute(values, ('x', 'y'), [(i, i ^ step) for i in range(4)])]
    unnamed x196 -> x216, local copies, waits for them, and re-layouts: 12.3 us -> 16.2 us
    pallas_call x6 -> x7, Pallas kernels: 63.6 us -> 64.7 us  [kernel_call(): pl.pallas_call(body, out_shape=outs, in_specs=specs, out_specs=[pl.BlockS...]
  transfers between devices with their start and end apart: 97 -> 97, of which waited for: 46 -> 39; matrix products, arithmetic and copies ran while one was open for 12% -> 14% of each run, Pallas kernels for 9% -> 10%
where the time goes in v5:
time: 519 us; the launch traced here: 509 us
  waiting for transfers between devices  202 us (39%)
  starting transfers between devices  145 us (28%)
  Pallas kernels  66.6 us (13%)
  other arithmetic  42.8 us (8%)
  local copies, waits for them, and re-layouts  35.2 us (7%)
  matrix products  14.6 us (3%)
    ppermute x40, waiting for transfers between devices, pair_swap(): return lax.ppermute(values, axis, [(0, 1), (1, 0)])  102 us
    ppermute x42, waiting for transfers between devices, side_swap(): return lax.ppermute(values, ('x', 'y'), [(i, i ^ step) for i in range(4)])  89.5 us
    pallas_call x7, Pallas kernels, kernel_call(): pl.pallas_call(body, out_shape=outs, in_specs=specs, out_specs=[pl.BlockS...  64.7 us
    ppermute x42, starting transfers between devices, side_swap(): return lax.ppermute(values, ('x', 'y'), [(i, i ^ step) for i in range(4)])  50 us
    ppermute x40, starting transfers between devices, pair_swap(): return lax.ppermute(values, axis, [(0, 1), (1, 0)])  35.4 us
    ppermute x3, starting transfers between devices, plane_swap(): return lax.ppermute(values, PLANE, [(i, i ^ step) for i in range(PLANES)])  26.8 us
    unnamed x216, local copies, waits for them, and re-layouts  16.2 us
    dot_general x10, matrix products, contract_first(): lax.dot_general(left, right, (((0,), (0,)), ((), ())), preferred_element_...  14.6 us
  transfers between devices with their start and end apart: 97, of which 39 were waited for; matrix products, arithmetic and copies ran while one was open for 14% of the time, Pallas kernels for 10%

profile of v5, /device:TPU:0, one launch (start us, length us, event | category | flops | bytes accessed | tf_op | source)
XLA Modules:
  0.0 508.9 jit_solution(4389945355669107846)
XLA Ops:
  15.9 12.1 %collective-permute-done.refs_1_ = bf16[64,2048]{1,0:T(8,128)(2,1)S(1)} collective-permute-done((bf16[64,2048]{1,0:T(8,128)(2,1)S(1)}, bf16[64,2048]{1,0:T(8,128)(2,1)S(1)}, u32[]{:S(2)}, u32[]{:S(2)}) %collective-permute-start) | collective-permute-done | bytes 262176 | tf_op jit(solution)/shard_map/ppermute | solution.py:447
  32.5 6.8 %collective-permute-done.10 = bf16[256,512]{1,0:T(8,128)(2,1)S(1)} collective-permute-done((bf16[256,512]{1,0:T(8,128)(2,1)}, bf16[256,512]{1,0:T(8,128)(2,1)S(1)}, u32[]{:S(2)}, u32[]{:S(2)}) %collective-permute-start.10) | collective-permute-done | bytes 262176 | tf_op jit(solution)/shard_map/ppermute | solution.py:530
  52.4 8.3 %collective-permute-done.7 = bf16[64,2048]{1,0:T(8,128)(2,1)S(1)} collective-permute-done((bf16[64,2048]{1,0:T(8,128)(2,1)S(1)}, bf16[64,2048]{1,0:T(8,128)(2,1)S(1)}, u32[]{:S(2)}, u32[]{:S(2)}) %collective-permute-start.7) | collective-permute-done | bytes 262176 | tf_op jit(solution)/shard_map/ppermute | solution.py:447
  80.2 5.7 %shard_map.255 = (bf16[512,2048]{1,0:T(8,128)(2,1)}, bf16[512,256]{1,0:T(8,128)(2,1)}, bf16[2,512,128]{2,1,0:T(8,128)(2,1)}, f32[2,512,128]{2,1,0:T(8,128)}, f32[512,128]{1,0:T(8,128)}) custom-call(s32[1]{0:T(128)} %bitcast.flag, bf16[64,2048]{1,0:T(8,128)(2,1)} %copy-done.9, bf16[64,2048]{1,0:T(8,128)(2,1)} %copy-done.37, bf16[64,2048]{1,0:T(8,128)(2,1)} %copy-done.38, ...), custom_call_target="tpu_custom_call" | custom-call | flops 1073741824 | bytes 8135684 | tf_op jit(solution)/shard_map/pallas_call | solution.py:578
  86.7 12.2 %collective-permute-done.21.mine_near.refs_1_.refs_9_.refs_14_ = bf16[1024,256]{1,0:T(8,128)(2,1)S(1)} collective-permute-done((bf16[1024,256]{1,0:T(8,128)(2,1)S(1)}, bf16[1024,256]{1,0:T(8,128)(2,1)S(1)}, u32[]{:S(2)}, u32[]{:S(2)}) %collective-permute-start.21) | collective-permute-done | bytes 524320 | tf_op jit(solution)/shard_map/ppermute | solution.py:447
  99.4 10.2 %collective-permute-done.18.second.refs_13_ = bf16[512,256]{1,0:T(8,128)(2,1)S(1)} collective-permute-done((bf16[512,256]{1,0:T(8,128)(2,1)}, bf16[512,256]{1,0:T(8,128)(2,1)S(1)}, u32[]{:S(2)}, u32[]{:S(2)}) %collective-permute-start.18) | collective-permute-done | bytes 262176 | tf_op jit(solution)/shard_map/ppermute | solution.py:447
  115.7 5.7 %all-to-all-start.1 = ((bf16[4,256,384]{2,1,0:T(8,128)(2,1)}), bf16[4,256,384]{2,1,0:T(8,128)(2,1)}, u32[]{:S(2)}, u32[]{:S(2)}) async-start(bf16[4,256,384]{2,1,0:T(8,128)(2,1)} %pad_maximum_fusion.8), calls=%async_computation.1 | async-start | bytes 1572864 | tf_op jit(solution)/shard_map/all_to_all | solution.py:510
  126.8 14.3 %collective-permute-done.17.refs_11_ = bf16[128,2048]{1,0:T(8,128)(2,1)} collective-permute-done((bf16[128,2048]{1,0:T(8,128)(2,1)S(1)}, bf16[128,2048]{1,0:T(8,128)(2,1)}, u32[]{:S(2)}, u32[]{:S(2)}) %collective-permute-start.17) | collective-permute-done | bytes 524320 | tf_op jit(solution)/shard_map/ppermute | solution.py:455
  141.9 9.7 %shard_map.257 = (bf16[2,512,128]{2,1,0:T(8,128)(2,1)}, f32[2,512,128]{2,1,0:T(8,128)}, f32[2,512,128]{2,1,0:T(8,128)}, bf16[64,2048]{1,0:T(8,128)(2,1)}, bf16[6...) custom-call(bf16[2,512,128]{2,1,0:T(8,128)(2,1)} %get-tuple-element., ...), custom_call_target="tpu_custom_call" | custom-call | flops 1073741824 | bytes 7610368 | tf_op jit(solution)/shard_map/pallas_call | solution.py:578
  155.7 6.3 %collective-permute-done.27 = bf16[64,2048]{1,0:T(8,128)(2,1)S(1)} collective-permute-done((bf16[64,2048]{1,0:T(8,128)(2,1)}, bf16[64,2048]{1,0:T(8,128)(2,1)S(1)}, u32[]{:S(2)}, u32[]{:S(2)}) %collective-permute-start.27) | collective-permute-done | bytes 262176 | tf_op jit(solution)/shard_map/ppermute | solution.py:455
  175.9 8.9 %collective-permute-done.31 = bf16[64,2048]{1,0:T(8,128)(2,1)S(1)} collective-permute-done((bf16[64,2048]{1,0:T(8,128)(2,1)S(1)}, bf16[64,2048]{1,0:T(8,128)(2,1)S(1)}, u32[]{:S(2)}, u32[]{:S(2)}) %collective-permute-start.31) | collective-permute-done | bytes 262176 | tf_op jit(solution)/shard_map/ppermute | solution.py:447
  186.8 15.8 %collective-permute-done.41.refs_17_.refs_3_ = bf16[1024,384]{1,0:T(8,128)(2,1)S(1)} collective-permute-done((bf16[1024,384]{1,0:T(8,128)(2,1)}, bf16[1024,384]{1,0:T(8,128)(2,1)S(1)}, u32[]{:S(2)}, u32[]{:S(2)}) %collective-permute-start.41) | collective-permute-done | bytes 786464 | tf_op jit(solution)/shard_map/ppermute | solution.py:447
  204.6 7.1 %collective-permute-done.35.refs_4_ = bf16[64,2048]{1,0:T(8,128)(2,1)S(1)} collective-permute-done((bf16[64,2048]{1,0:T(8,128)(2,1)S(1)}, bf16[64,2048]{1,0:T(8,128)(2,1)S(1)}, u32[]{:S(2)}, u32[]{:S(2)}) %collective-permute-start.35) | collective-permute-done | bytes 262176 | tf_op jit(solution)/shard_map/ppermute | solution.py:455
  226.4 5.3 %collective-permute-done.38.refs_7_ = bf16[64,2048]{1,0:T(8,128)(2,1)S(1)} collective-permute-done((bf16[64,2048]{1,0:T(8,128)(2,1)S(1)}, bf16[64,2048]{1,0:T(8,128)(2,1)S(1)}, u32[]{:S(2)}, u32[]{:S(2)}) %collective-permute-start.38) | collective-permute-done | bytes 262176 | tf_op jit(solution)/shard_map/ppermute | solution.py:455
  233.8 16.4 %shard_map.258 = (bf16[512,384]{1,0:T(8,128)(2,1)}, bf16[512,384]{1,0:T(8,128)(2,1)}, bf16[512,768]{1,0:T(8,128)(2,1)}, bf16[512,768]{1,0:T(8,128)(2,1)}, bf16[6...) custom-call(bf16[64,2048]{1,0:T(8,128)(2,1)} %copy-done.28, ...), custom_call_target="tpu_custom_call" | custom-call | flops 8053063680 | bytes 18087936 | tf_op jit(solution)/shard_map/pallas_call | solution.py:578
  296.9 9.3 %collective-permute-done.54.refs_1_ = bf16[64,2048]{1,0:T(8,128)(2,1)S(1)} collective-permute-done((bf16[64,2048]{1,0:T(8,128)(2,1)S(1)}, bf16[64,2048]{1,0:T(8,128)(2,1)S(1)}, u32[]{:S(2)}, u32[]{:S(2)}) %collective-permute-start.54) | collective-permute-done | bytes 262176 | tf_op jit(solution)/shard_map/ppermute | solution.py:447
  310.9 5.7 %shard_map.260 = (bf16[128,2048]{1,0:T(8,128)(2,1)}, bf16[128,2048]{1,0:T(8,128)(2,1)}, bf16[128,2048]{1,0:T(8,128)(2,1)}, bf16[128,2048]{1,0:T(8,128)(2,1)}) custom-call(bf16[512,384]{1,0:T(8,128)(2,1)} %get-tuple-element.214.refs_0_, bf16[512,384]{1,0:T(8,128)(2,1)} %get-tuple-element.215.refs_1_, bf16[1024,384]{1,0:T(8,128)(2,1)} %bitcast.36.refs_16_.refs_2_, ...), custom_call_target="tpu_custom_call" | custom-call | flops 1610612736 | bytes 6029312 | tf_op jit(solution)/shard_map/pallas_call | solution.py:578
  322.0 15.3 %shard_map.259 = (bf16[512,2048]{1,0:T(8,128)(2,1)}, bf16[2,512,128]{2,1,0:T(8,128)(2,1)}, bf16[2,512,128]{2,1,0:T(8,128)(2,1)}, bf16[2048,256]{1,0:T(8,128)(2,1)}, f32[1,128]{1,0:T(1,128)}) custom-call(bf16[64,2048]{1,0:T(8,128)(2,1)} %copy-done.46, bf16[64,2048]{1,0:T(8,128)(2,1)} %copy-done.84, bf16[64,2048]{1,0:T(8,128)(2,1)} %copy-done.86, ...), custom_call_target="tpu_custom_call" | custom-call | flops 2684354560 | bytes 12067840 | tf_op jit(solution)/shard_map/pallas_call | solution.py:578
  357.1 10.4 %collective-permute-done.63 = bf16[128,2048]{1,0:T(8,128)(2,1)} collective-permute-done((bf16[128,2048]{1,0:T(8,128)(2,1)}, bf16[128,2048]{1,0:T(8,128)(2,1)}, u32[]{:S(2)}, u32[]{:S(2)}) %collective-permute-start.63) | collective-permute-done | bytes 524320 | tf_op jit(solution)/shard_map/ppermute | solution.py:455
  367.6 7.7 %shard_map.261 = (bf16[512,256]{1,0:T(8,128)(2,1)}, bf16[512,256]{1,0:T(8,128)(2,1)}, bf16[64,2048]{1,0:T(8,128)(2,1)}, bf16[64,2048]{1,0:T(8,128)(2,1)}, bf16[6...) custom-call(s32[1]{0:T(128)} %bitcast.flag, ...), custom_call_target="tpu_custom_call" | custom-call | flops 1610612736 | bytes 10757124 | tf_op jit(solution)/shard_map/pallas_call | solution.py:578
  386.9 8.0 %collective-permute-start.71 = (bf16[1024,384]{1,0:T(8,128)(2,1)}, bf16[1024,384]{1,0:T(8,128)(2,1)}, u32[]{:S(2)}, u32[]{:S(2)}) collective-permute-start(bf16[1024,384]{1,0:T(8,128)(2,1)} %slice.423), channel_id=1, source_target_pairs={{0,8},{8,0},{1,9},{9,1},{2,10},{10,2},{3,11},{11,3},{4,12},{12,4},... | collective-permute-start | bytes 2359304 | tf_op jit(solution)/shard_map/ppermute | solution.py:447
  412.6 5.6 %collective-permute-done.71 = bf16[1024,384]{1,0:T(8,128)(2,1)} collective-permute-done((bf16[1024,384]{1,0:T(8,128)(2,1)}, bf16[1024,384]{1,0:T(8,128)(2,1)}, u32[]{:S(2)}, u32[]{:S(2)}) %collective-permute-start.71) | collective-permute-done | bytes 786464 | tf_op jit(solution)/shard_map/ppermute | solution.py:447
  424.8 12.0 %collective-permute-done.73 = bf16[1024,256]{1,0:T(8,128)(2,1)S(1)} collective-permute-done((bf16[1024,256]{1,0:T(8,128)(2,1)S(1)}, bf16[1024,256]{1,0:T(8,128)(2,1)S(1)}, u32[]{:S(2)}, u32[]{:S(2)}) %collective-permute-start.73) | collective-permute-done | bytes 524320 | tf_op jit(solution)/shard_map/ppermute | solution.py:447
  464.5 20.8 %collective-permute-start.88 = (f32[4352]{0:T(1024)S(1)}, f32[4352]{0:T(1024)S(1)}, u32[]{:S(2)}, u32[]{:S(2)}) collective-permute-start(f32[4352]{0:T(1024)S(1)} %pad_maximum_fusion.14), channel_id=1, source_target_pairs={{0,16},{4,20},{16,0},{20,4},{1,17},{5,21},{17,1},{21,5},{2,18},{6,... | collective-permute-start | bytes 52232 | tf_op jit(solution)/shard_map/ppermute | solution.py:451
  (543 shorter events, 266.2 us)
Async XLA Ops:
  11.8 33.7 %collective-permute-start.1 = (bf16[64,2048]{1,0:T(8,128)(2,1)S(1)}, bf16[64,2048]{1,0:T(8,128)(2,1)S(1)}, u32[]{:S(2)}, u32[]{:S(2)}) collective-permute-start(bf16[64,2048]{1,0:T(8,128)(2,1)S(1)} %constant_dynamic-update-slice_fusion.refs_0_), channel_id=1, source_target_pairs={{0,2},{2,0},{4,6},{6,4},{1,3},{3,1},{5,7},{7,5},{8,10},{10,8},{12,... | collective-permute-start | bytes 786440 | tf_op jit(solution)/shard_map/ppermute | solution.py:455
  64.3 45.3 %all-to-all-start = ((bf16[4,256,768]{2,1,0:T(8,128)(2,1)}), bf16[4,256,768]{2,1,0:T(8,128)(2,1)}, u32[]{:S(2)}, u32[]{:S(2)}) async-start(bf16[4,256,768]{2,1,0:T(8,128)(2,1)} %pad_maximum_fusion), calls=%async_computation | async-start | bytes 3145728 | tf_op jit(solution)/shard_map/all_to_all | solution.py:510
  72.1 39.7 %collective-permute-start.15 = (bf16[128,2048]{1,0:T(8,128)(2,1)S(1)}, bf16[128,2048]{1,0:T(8,128)(2,1)}, u32[]{:S(2)}, u32[]{:S(2)}) collective-permute-start(bf16[128,2048]{1,0:T(8,128)(2,1)S(1)} %pad_maximum_fusion.9.refs_8_), channel_id=1, source_target_pairs={{0,2},{2,0},{4,6},{6,4},{1,3},{3,1},{5,7},{7,5},{8,10},{10,8},{12,... | collective-permute-start | bytes 1572872 | tf_op jit(solution)/shard_map/ppermute | solution.py:455
  109.7 59.7 %collective-permute-start.30 = (bf16[1024,768]{1,0:T(8,128)(2,1)}, bf16[1024,768]{1,0:T(8,128)(2,1)}, u32[]{:S(2)}, u32[]{:S(2)}) collective-permute-start(bf16[1024,768]{1,0:T(8,128)(2,1)} %bitcast.31.refs_12_), channel_id=1, source_target_pairs={{0,8},{8,0},{1,9},{9,1},{2,10},{10,2},{3,11},{11,3},{4,12},{12,4},... | collective-permute-start | bytes 4718600 | tf_op jit(solution)/shard_map/ppermute | solution.py:447
  111.8 29.4 %collective-permute-start.17 = (bf16[128,2048]{1,0:T(8,128)(2,1)S(1)}, bf16[128,2048]{1,0:T(8,128)(2,1)}, u32[]{:S(2)}, u32[]{:S(2)}) collective-permute-start(bf16[128,2048]{1,0:T(8,128)(2,1)S(1)} %pad_maximum_fusion.9.refs_8_), channel_id=1, source_target_pairs={{0,6},{2,4},{4,2},{6,0},{1,7},{3,5},{5,3},{7,1},{8,14},{10,12},{12... | collective-permute-start | bytes 1572872 | tf_op jit(solution)/shard_map/ppermute | solution.py:455
  115.7 53.6 %all-to-all-start.1 = ((bf16[4,256,384]{2,1,0:T(8,128)(2,1)}), bf16[4,256,384]{2,1,0:T(8,128)(2,1)}, u32[]{:S(2)}, u32[]{:S(2)}) async-start(bf16[4,256,384]{2,1,0:T(8,128)(2,1)} %pad_maximum_fusion.8), calls=%async_computation.1 | async-start | bytes 1572864 | tf_op jit(solution)/shard_map/all_to_all | solution.py:510
  170.4 61.3 %collective-permute-start.40 = (bf16[1024,768]{1,0:T(8,128)(2,1)}, bf16[1024,768]{1,0:T(8,128)(2,1)S(1)}, u32[]{:S(2)}, u32[]{:S(2)}) collective-permute-start(bf16[1024,768]{1,0:T(8,128)(2,1)} %collective-permute-done.30.refs_13_), channel_id=1, source_target_pairs={{0,1},{1,0},{2,3},{3,2},{4,5},{5,4},{6,7},{7,6},{8,9},{9,8},{10,11... | collective-permute-start | bytes 4718600 | tf_op jit(solution)/shard_map/ppermute | solution.py:447
  170.9 48.0 %collective-permute-start.42 = (bf16[1024,384]{1,0:T(8,128)(2,1)}, bf16[1024,384]{1,0:T(8,128)(2,1)S(1)}, u32[]{:S(2)}, u32[]{:S(2)}) collective-permute-start(bf16[1024,384]{1,0:T(8,128)(2,1)} %bitcast.36.refs_16_.refs_2_), channel_id=1, source_target_pairs={{0,1},{1,0},{2,3},{3,2},{4,5},{5,4},{6,7},{7,6},{8,9},{9,8},{10,11... | collective-permute-start | bytes 2359304 | tf_op jit(solution)/shard_map/ppermute | solution.py:447
  174.5 28.1 %collective-permute-start.41 = (bf16[1024,384]{1,0:T(8,128)(2,1)}, bf16[1024,384]{1,0:T(8,128)(2,1)S(1)}, u32[]{:S(2)}, u32[]{:S(2)}) collective-permute-start(bf16[1024,384]{1,0:T(8,128)(2,1)} %bitcast.36.refs_16_.refs_2_), channel_id=1, source_target_pairs={{0,8},{8,0},{1,9},{9,1},{2,10},{10,2},{3,11},{11,3},{4,12},{12,4},... | collective-permute-start | bytes 2359304 | tf_op jit(solution)/shard_map/ppermute | solution.py:447
  202.6 29.1 %collective-permute-start.43 = (bf16[1024,384]{1,0:T(8,128)(2,1)S(1)}, bf16[1024,384]{1,0:T(8,128)(2,1)S(1)}, u32[]{:S(2)}, u32[]{:S(2)}) collective-permute-start(bf16[1024,384]{1,0:T(8,128)(2,1)S(1)} %collective-permute-done.41.refs_17_.refs_3_), channel_id=1, source_target_pairs={{0,1},{1,0},{2,3},{3,2},{4,5},{5,4},{6,7},{7,6},{8,9},{9,8},{10,11... | collective-permute-start | bytes 2359304 | tf_op jit(solution)/shard_map/ppermute | solution.py:447
  256.3 27.8 %collective-permute-start.52 = (bf16[2048,768]{1,0:T(8,128)(2,1)S(1)}, bf16[2048,768]{1,0:T(8,128)(2,1)S(1)}, u32[]{:S(2)}, u32[]{:S(2)}) collective-permute-start(bf16[2048,768]{1,0:T(8,128)(2,1)S(1)} %convolution_convert_fusion), channel_id=1, source_target_pairs={{0,1},{1,0},{2,3},{3,2},{4,5},{5,4},{6,7},{7,6},{8,9},{9,8},{10,11... | collective-permute-start | bytes 9437192 | tf_op jit(solution)/shard_map/ppermute | solution.py:447
  310.2 37.0 %collective-permute-start.53 = (bf16[1024,768]{1,0:T(8,128)(2,1)S(1)}, bf16[1024,768]{1,0:T(8,128)(2,1)}, u32[]{:S(2)}, u32[]{:S(2)}) collective-permute-start(bf16[1024,768]{1,0:T(8,128)(2,1)S(1)} %slice.418), channel_id=1, source_target_pairs={{0,8},{8,0},{1,9},{9,1},{2,10},{10,2},{3,11},{11,3},{4,12},{12,4},... | collective-permute-start | bytes 4718600 | tf_op jit(solution)/shard_map/ppermute | solution.py:447
  340.5 27.0 %collective-permute-start.63 = (bf16[128,2048]{1,0:T(8,128)(2,1)}, bf16[128,2048]{1,0:T(8,128)(2,1)}, u32[]{:S(2)}, u32[]{:S(2)}) collective-permute-start(bf16[128,2048]{1,0:T(8,128)(2,1)} %get-tuple-element.244), channel_id=1, source_target_pairs={{0,6},{2,4},{4,2},{6,0},{1,7},{3,5},{5,3},{7,1},{8,14},{10,12},{12... | collective-permute-start | bytes 1572872 | tf_op jit(solution)/shard_map/ppermute | solution.py:455
  350.2 51.2 %all-to-all-start.2 = ((bf16[4,256,768]{2,1,0:T(8,128)(2,1)}), bf16[4,256,768]{2,1,0:T(8,128)(2,1)}, u32[]{:S(2)}, u32[]{:S(2)}) async-start(bf16[4,256,768]{2,1,0:T(8,128)(2,1)} %bitcast.211), calls=%async_computation.2 | async-start | bytes 3145728 | tf_op jit(solution)/shard_map/all_to_all | solution.py:563
  386.9 31.3 %collective-permute-start.71 = (bf16[1024,384]{1,0:T(8,128)(2,1)}, bf16[1024,384]{1,0:T(8,128)(2,1)}, u32[]{:S(2)}, u32[]{:S(2)}) collective-permute-start(bf16[1024,384]{1,0:T(8,128)(2,1)} %slice.423), channel_id=1, source_target_pairs={{0,8},{8,0},{1,9},{9,1},{2,10},{10,2},{3,11},{11,3},{4,12},{12,4},... | collective-permute-start | bytes 2359304 | tf_op jit(solution)/shard_map/ppermute | solution.py:447
  394.9 41.9 %collective-permute-start.76 = (bf16[64,2048]{1,0:T(8,128)(2,1)}, bf16[64,2048]{1,0:T(8,128)(2,1)S(1)}, u32[]{:S(2)}, u32[]{:S(2)}) collective-permute-start(bf16[64,2048]{1,0:T(8,128)(2,1)} %get-tuple-element.272), channel_id=1, source_target_pairs={{0,2},{2,0},{4,6},{6,4},{1,3},{3,1},{5,7},{7,5},{8,10},{10,8},{12,... | collective-permute-start | bytes 786440 | tf_op jit(solution)/shard_map/ppermute | solution.py:455
  395.7 41.2 %collective-permute-start.77 = (bf16[64,2048]{1,0:T(8,128)(2,1)}, bf16[64,2048]{1,0:T(8,128)(2,1)}, u32[]{:S(2)}, u32[]{:S(2)}) collective-permute-start(bf16[64,2048]{1,0:T(8,128)(2,1)} %get-tuple-element.273), channel_id=1, source_target_pairs={{0,4},{2,6},{4,0},{6,2},{1,5},{3,7},{5,1},{7,3},{8,12},{10,14},{12... | collective-permute-start | bytes 786440 | tf_op jit(solution)/shard_map/ppermute | solution.py:455
  397.1 39.8 %collective-permute-start.78 = (bf16[64,2048]{1,0:T(8,128)(2,1)}, bf16[64,2048]{1,0:T(8,128)(2,1)}, u32[]{:S(2)}, u32[]{:S(2)}) collective-permute-start(bf16[64,2048]{1,0:T(8,128)(2,1)} %get-tuple-element.274), channel_id=1, source_target_pairs={{0,6},{2,4},{4,2},{6,0},{1,7},{3,5},{5,3},{7,1},{8,14},{10,12},{12... | collective-permute-start | bytes 786440 | tf_op jit(solution)/shard_map/ppermute | solution.py:455
  444.0 63.3 %all-to-all-start.3 = ((bf16[4,256,384]{2,1,0:T(8,128)(2,1)}), bf16[4,256,384]{2,1,0:T(8,128)(2,1)S(1)}, u32[]{:S(2)}, u32[]{:S(2)}) async-start(bf16[4,256,384]{2,1,0:T(8,128)(2,1)} %bitcast.85), calls=%async_computation.3 | async-start | bytes 1572864 | tf_op jit(solution)/shard_map/all_to_all | solution.py:563
  456.4 28.9 %collective-permute-start.85 = (bf16[256,512]{1,0:T(8,128)(2,1)}, bf16[256,512]{1,0:T(8,128)(2,1)S(1)}, u32[]{:S(2)}, u32[]{:S(2)}) collective-permute-start(bf16[256,512]{1,0:T(8,128)(2,1)} %get-tuple-element.329), channel_id=1, source_target_pairs={{4,0},{20,1},{0,4},{16,5},{5,16},{21,17},{1,20},{17,21},{6,2},{22,... | collective-permute-start | bytes 786440 | tf_op jit(solution)/shard_map/ppermute | solution.py:544
  457.8 31.9 %collective-permute-start.86 = (bf16[256,512]{1,0:T(8,128)(2,1)}, bf16[256,512]{1,0:T(8,128)(2,1)S(1)}, u32[]{:S(2)}, u32[]{:S(2)}) collective-permute-start(bf16[256,512]{1,0:T(8,128)(2,1)} %get-tuple-element.328), channel_id=1, source_target_pairs={{5,0},{21,1},{1,4},{17,5},{4,16},{20,17},{0,20},{16,21},{7,2},{23,... | collective-permute-start | bytes 786440 | tf_op jit(solution)/shard_map/ppermute | solution.py:544
  460.0 31.9 %collective-permute-start.74 = (bf16[64,2048]{1,0:T(8,128)(2,1)S(1)}, bf16[64,2048]{1,0:T(8,128)(2,1)S(1)}, u32[]{:S(2)}, u32[]{:S(2)}) collective-permute-start(bf16[64,2048]{1,0:T(8,128)(2,1)S(1)} %copy-done.52), channel_id=1, source_target_pairs={{0,2},{2,0},{1,3},{3,1},{4,6},{6,4},{5,7},{7,5},{8,10},{10,8},{9,1... | collective-permute-start | bytes 786440 | tf_op jit(solution)/shard_map/ppermute | solution.py:447
  462.9 31.1 %collective-permute-start.87 = (f32[4352]{0:T(1024)S(1)}, f32[4352]{0:T(1024)S(1)}, u32[]{:S(2)}, u32[]{:S(2)}) collective-permute-start(f32[4352]{0:T(1024)S(1)} %pad_maximum_fusion.14), channel_id=1, source_target_pairs={{0,4},{4,0},{16,20},{20,16},{1,5},{5,1},{17,21},{21,17},{2,6},{6,2... | collective-permute-start | bytes 52232 | tf_op jit(solution)/shard_map/ppermute | solution.py:451
  464.5 29.5 %collective-permute-start.88 = (f32[4352]{0:T(1024)S(1)}, f32[4352]{0:T(1024)S(1)}, u32[]{:S(2)}, u32[]{:S(2)}) collective-permute-start(f32[4352]{0:T(1024)S(1)} %pad_maximum_fusion.14), channel_id=1, source_target_pairs={{0,16},{4,20},{16,0},{20,4},{1,17},{5,21},{17,1},{21,5},{2,18},{6,... | collective-permute-start | bytes 52232 | tf_op jit(solution)/shard_map/ppermute | solution.py:451
  (170 other events, 2027.3 us)

commit v6 on v5

--- a/solution.py
+++ b/solution.py
@@ -1124,7 +1124,7 @@
             for i in range(2)
         )
     )
-    key_pre, gate_up_rows, down_pieces = after((key_pre, gate_up_rows, down_pieces))
+    key_pre, gate_up_rows = after((key_pre, gate_up_rows))
     og_got = pair_swap(after(og_both, pair_got)[half:], "near")
     outs = kernel_call(
         input_kernel,

time: 519 us -> 517 us (level)
  starting transfers between devices: 145 us -> 135 us
  waiting for transfers between devices: 202 us -> 212 us
    ppermute x40, starting transfers between devices: 35.4 us -> 22.7 us  [pair_swap(): return lax.ppermute(values, axis, [(0, 1), (1, 0)])]
    ppermute x40, waiting for transfers between devices: 102 us -> 112 us  [pair_swap(): return lax.ppermute(values, axis, [(0, 1), (1, 0)])]
    unnamed x216 -> x222, local copies, waits for them, and re-layouts: 16.2 us -> 16.3 us
  transfers between devices with their start and end apart: 97 -> 97, of which waited for: 39 -> 39; matrix products, arithmetic and copies ran while one was open for 14% -> 13% of each run, Pallas kernels for 10% -> 10%
where the time goes in v6:
time: 517 us; the launch traced here: 507 us
  waiting for transfers between devices  212 us (41%)
  starting transfers between devices  135 us (26%)
  Pallas kernels  66.8 us (13%)
  other arithmetic  40 us (8%)
  local copies, waits for them, and re-layouts  35.3 us (7%)
  matrix products  14.7 us (3%)
    ppermute x40, waiting for transfers between devices, pair_swap(): return lax.ppermute(values, axis, [(0, 1), (1, 0)])  112 us
    ppermute x42, waiting for transfers between devices, side_swap(): return lax.ppermute(values, ('x', 'y'), [(i, i ^ step) for i in range(4)])  89.8 us
    pallas_call x7, Pallas kernels, kernel_call(): pl.pallas_call(body, out_shape=outs, in_specs=specs, out_specs=[pl.BlockS...  64.8 us
    ppermute x42, starting transfers between devices, side_swap(): return lax.ppermute(values, ('x', 'y'), [(i, i ^ step) for i in range(4)])  54 us
    ppermute x3, starting transfers between devices, plane_swap(): return lax.ppermute(values, PLANE, [(i, i ^ step) for i in range(PLANES)])  25.1 us
    ppermute x40, starting transfers between devices, pair_swap(): return lax.ppermute(values, axis, [(0, 1), (1, 0)])  22.7 us
    unnamed x222, local copies, waits for them, and re-layouts  16.3 us
    dot_general x10, matrix products, contract_first(): lax.dot_general(left, right, (((0,), (0,)), ((), ())), preferred_element_...  14.7 us
  transfers between devices with their start and end apart: 97, of which 39 were waited for; matrix products, arithmetic and copies ran while one was open for 13% of the time, Pallas kernels for 10%

profile of v6, /device:TPU:0, one launch (start us, length us, event | category | flops | bytes accessed | tf_op | source)
XLA Modules:
  0.0 507.4 jit_solution(12357515897872720029)
XLA Ops:
  15.9 12.1 %collective-permute-done.refs_1_ = bf16[64,2048]{1,0:T(8,128)(2,1)S(1)} collective-permute-done((bf16[64,2048]{1,0:T(8,128)(2,1)S(1)}, bf16[64,2048]{1,0:T(8,128)(2,1)S(1)}, u32[]{:S(2)}, u32[]{:S(2)}) %collective-permute-start) | collective-permute-done | bytes 262176 | tf_op jit(solution)/shard_map/ppermute | solution.py:447
  32.5 6.8 %collective-permute-done.10 = bf16[256,512]{1,0:T(8,128)(2,1)S(1)} collective-permute-done((bf16[256,512]{1,0:T(8,128)(2,1)}, bf16[256,512]{1,0:T(8,128)(2,1)S(1)}, u32[]{:S(2)}, u32[]{:S(2)}) %collective-permute-start.10) | collective-permute-done | bytes 262176 | tf_op jit(solution)/shard_map/ppermute | solution.py:530
  52.4 8.3 %collective-permute-done.7 = bf16[64,2048]{1,0:T(8,128)(2,1)S(1)} collective-permute-done((bf16[64,2048]{1,0:T(8,128)(2,1)S(1)}, bf16[64,2048]{1,0:T(8,128)(2,1)S(1)}, u32[]{:S(2)}, u32[]{:S(2)}) %collective-permute-start.7) | collective-permute-done | bytes 262176 | tf_op jit(solution)/shard_map/ppermute | solution.py:447
  64.4 5.2 %all-to-all-start = ((bf16[4,256,768]{2,1,0:T(8,128)(2,1)}), bf16[4,256,768]{2,1,0:T(8,128)(2,1)}, u32[]{:S(2)}, u32[]{:S(2)}) async-start(bf16[4,256,768]{2,1,0:T(8,128)(2,1)} %pad_maximum_fusion), calls=%async_computation | async-start | bytes 3145728 | tf_op jit(solution)/shard_map/all_to_all | solution.py:510
  80.1 5.7 %shard_map.255 = (bf16[512,2048]{1,0:T(8,128)(2,1)}, bf16[512,256]{1,0:T(8,128)(2,1)}, bf16[2,512,128]{2,1,0:T(8,128)(2,1)}, f32[2,512,128]{2,1,0:T(8,128)}, f32[512,128]{1,0:T(8,128)}) custom-call(s32[1]{0:T(128)} %bitcast.flag, bf16[64,2048]{1,0:T(8,128)(2,1)} %copy-done.9, bf16[64,2048]{1,0:T(8,128)(2,1)} %copy-done.37, bf16[64,2048]{1,0:T(8,128)(2,1)} %copy-done.38, ...), custom_call_target="tpu_custom_call" | custom-call | flops 1073741824 | bytes 8135684 | tf_op jit(solution)/shard_map/pallas_call | solution.py:578
  86.7 12.3 %collective-permute-done.21.mine_near.refs_1_.refs_9_.refs_14_ = bf16[1024,256]{1,0:T(8,128)(2,1)S(1)} collective-permute-done((bf16[1024,256]{1,0:T(8,128)(2,1)S(1)}, bf16[1024,256]{1,0:T(8,128)(2,1)S(1)}, u32[]{:S(2)}, u32[]{:S(2)}) %collective-permute-start.21) | collective-permute-done | bytes 524320 | tf_op jit(solution)/shard_map/ppermute | solution.py:447
  99.5 10.1 %collective-permute-done.18.second.refs_13_ = bf16[512,256]{1,0:T(8,128)(2,1)S(1)} collective-permute-done((bf16[512,256]{1,0:T(8,128)(2,1)}, bf16[512,256]{1,0:T(8,128)(2,1)S(1)}, u32[]{:S(2)}, u32[]{:S(2)}) %collective-permute-start.18) | collective-permute-done | bytes 262176 | tf_op jit(solution)/shard_map/ppermute | solution.py:447
  115.6 5.8 %all-to-all-start.1 = ((bf16[4,256,384]{2,1,0:T(8,128)(2,1)}), bf16[4,256,384]{2,1,0:T(8,128)(2,1)}, u32[]{:S(2)}, u32[]{:S(2)}) async-start(bf16[4,256,384]{2,1,0:T(8,128)(2,1)} %pad_maximum_fusion.8), calls=%async_computation.1 | async-start | bytes 1572864 | tf_op jit(solution)/shard_map/all_to_all | solution.py:510
  126.7 14.4 %collective-permute-done.17.refs_11_ = bf16[128,2048]{1,0:T(8,128)(2,1)} collective-permute-done((bf16[128,2048]{1,0:T(8,128)(2,1)S(1)}, bf16[128,2048]{1,0:T(8,128)(2,1)}, u32[]{:S(2)}, u32[]{:S(2)}) %collective-permute-start.17) | collective-permute-done | bytes 524320 | tf_op jit(solution)/shard_map/ppermute | solution.py:455
  141.9 9.7 %shard_map.257 = (bf16[2,512,128]{2,1,0:T(8,128)(2,1)}, f32[2,512,128]{2,1,0:T(8,128)}, f32[2,512,128]{2,1,0:T(8,128)}, bf16[64,2048]{1,0:T(8,128)(2,1)}, bf16[6...) custom-call(bf16[2,512,128]{2,1,0:T(8,128)(2,1)} %get-tuple-element., ...), custom_call_target="tpu_custom_call" | custom-call | flops 1073741824 | bytes 7610368 | tf_op jit(solution)/shard_map/pallas_call | solution.py:578
  155.7 6.3 %collective-permute-done.27 = bf16[64,2048]{1,0:T(8,128)(2,1)S(1)} collective-permute-done((bf16[64,2048]{1,0:T(8,128)(2,1)}, bf16[64,2048]{1,0:T(8,128)(2,1)S(1)}, u32[]{:S(2)}, u32[]{:S(2)}) %collective-permute-start.27) | collective-permute-done | bytes 262176 | tf_op jit(solution)/shard_map/ppermute | solution.py:455
  175.8 9.0 %collective-permute-done.31 = bf16[64,2048]{1,0:T(8,128)(2,1)S(1)} collective-permute-done((bf16[64,2048]{1,0:T(8,128)(2,1)S(1)}, bf16[64,2048]{1,0:T(8,128)(2,1)S(1)}, u32[]{:S(2)}, u32[]{:S(2)}) %collective-permute-start.31) | collective-permute-done | bytes 262176 | tf_op jit(solution)/shard_map/ppermute | solution.py:447
  186.8 15.7 %collective-permute-done.41.refs_17_.refs_3_ = bf16[1024,384]{1,0:T(8,128)(2,1)S(1)} collective-permute-done((bf16[1024,384]{1,0:T(8,128)(2,1)}, bf16[1024,384]{1,0:T(8,128)(2,1)S(1)}, u32[]{:S(2)}, u32[]{:S(2)}) %collective-permute-start.41) | collective-permute-done | bytes 786464 | tf_op jit(solution)/shard_map/ppermute | solution.py:447
  204.6 7.1 %collective-permute-done.35.refs_4_ = bf16[64,2048]{1,0:T(8,128)(2,1)S(1)} collective-permute-done((bf16[64,2048]{1,0:T(8,128)(2,1)S(1)}, bf16[64,2048]{1,0:T(8,128)(2,1)S(1)}, u32[]{:S(2)}, u32[]{:S(2)}) %collective-permute-start.35) | collective-permute-done | bytes 262176 | tf_op jit(solution)/shard_map/ppermute | solution.py:455
  226.4 5.3 %collective-permute-done.38.refs_7_ = bf16[64,2048]{1,0:T(8,128)(2,1)S(1)} collective-permute-done((bf16[64,2048]{1,0:T(8,128)(2,1)S(1)}, bf16[64,2048]{1,0:T(8,128)(2,1)S(1)}, u32[]{:S(2)}, u32[]{:S(2)}) %collective-permute-start.38) | collective-permute-done | bytes 262176 | tf_op jit(solution)/shard_map/ppermute | solution.py:455
  233.8 16.2 %shard_map.258 = (bf16[512,384]{1,0:T(8,128)(2,1)}, bf16[512,384]{1,0:T(8,128)(2,1)}, bf16[512,768]{1,0:T(8,128)(2,1)}, bf16[512,768]{1,0:T(8,128)(2,1)}, bf16[6...) custom-call(bf16[64,2048]{1,0:T(8,128)(2,1)} %copy-done.28, ...), custom_call_target="tpu_custom_call" | custom-call | flops 8053063680 | bytes 18087936 | tf_op jit(solution)/shard_map/pallas_call | solution.py:578
  296.8 9.3 %collective-permute-done.53.refs_1_ = bf16[64,2048]{1,0:T(8,128)(2,1)S(1)} collective-permute-done((bf16[64,2048]{1,0:T(8,128)(2,1)S(1)}, bf16[64,2048]{1,0:T(8,128)(2,1)S(1)}, u32[]{:S(2)}, u32[]{:S(2)}) %collective-permute-start.53) | collective-permute-done | bytes 262176 | tf_op jit(solution)/shard_map/ppermute | solution.py:447
  310.6 5.7 %shard_map.259 = (bf16[128,2048]{1,0:T(8,128)(2,1)}, bf16[128,2048]{1,0:T(8,128)(2,1)}, bf16[128,2048]{1,0:T(8,128)(2,1)}, bf16[128,2048]{1,0:T(8,128)(2,1)}) custom-call(bf16[512,384]{1,0:T(8,128)(2,1)} %get-tuple-element.198.refs_0_, bf16[512,384]{1,0:T(8,128)(2,1)} %get-tuple-element.199.refs_1_, bf16[1024,384]{1,0:T(8,128)(2,1)} %bitcast.36.refs_16_.refs_2_, ...), custom_call_target="tpu_custom_call" | custom-call | flops 1610612736 | bytes 6029312 | tf_op jit(solution)/shard_map/pallas_call | solution.py:578
  321.3 15.5 %shard_map.260 = (bf16[512,2048]{1,0:T(8,128)(2,1)}, bf16[2,512,128]{2,1,0:T(8,128)(2,1)}, bf16[2,512,128]{2,1,0:T(8,128)(2,1)}, bf16[2048,256]{1,0:T(8,128)(2,1)}, f32[1,128]{1,0:T(1,128)}) custom-call(bf16[64,2048]{1,0:T(8,128)(2,1)} %copy-done.46, bf16[64,2048]{1,0:T(8,128)(2,1)} %copy-done.87, bf16[64,2048]{1,0:T(8,128)(2,1)} %copy-done.89, ...), custom_call_target="tpu_custom_call" | custom-call | flops 2684354560 | bytes 12067840 | tf_op jit(solution)/shard_map/pallas_call | solution.py:578
  355.5 7.9 %shard_map.261 = (bf16[512,256]{1,0:T(8,128)(2,1)}, bf16[512,256]{1,0:T(8,128)(2,1)}, bf16[64,2048]{1,0:T(8,128)(2,1)}, bf16[64,2048]{1,0:T(8,128)(2,1)}, bf16[6...) custom-call(s32[1]{0:T(128)} %bitcast.flag, ...), custom_call_target="tpu_custom_call" | custom-call | flops 1610612736 | bytes 10757124 | tf_op jit(solution)/shard_map/pallas_call | solution.py:578
  376.7 8.7 %collective-permute-done.67 = bf16[64,2048]{1,0:T(8,128)(2,1)S(1)} collective-permute-done((bf16[64,2048]{1,0:T(8,128)(2,1)S(1)}, bf16[64,2048]{1,0:T(8,128)(2,1)S(1)}, u32[]{:S(2)}, u32[]{:S(2)}) %collective-permute-start.67) | collective-permute-done | bytes 262176 | tf_op jit(solution)/shard_map/ppermute | solution.py:455
  403.5 14.4 %collective-permute-done.71 = bf16[1024,384]{1,0:T(8,128)(2,1)} collective-permute-done((bf16[1024,384]{1,0:T(8,128)(2,1)}, bf16[1024,384]{1,0:T(8,128)(2,1)}, u32[]{:S(2)}, u32[]{:S(2)}) %collective-permute-start.71) | collective-permute-done | bytes 786464 | tf_op jit(solution)/shard_map/ppermute | solution.py:447
  427.9 10.3 %collective-permute-done.73 = bf16[1024,256]{1,0:T(8,128)(2,1)S(1)} collective-permute-done((bf16[1024,256]{1,0:T(8,128)(2,1)S(1)}, bf16[1024,256]{1,0:T(8,128)(2,1)S(1)}, u32[]{:S(2)}, u32[]{:S(2)}) %collective-permute-start.73) | collective-permute-done | bytes 524320 | tf_op jit(solution)/shard_map/ppermute | solution.py:447
  464.7 19.6 %collective-permute-start.88 = (f32[4352]{0:T(1024)S(1)}, f32[4352]{0:T(1024)S(1)}, u32[]{:S(2)}, u32[]{:S(2)}) collective-permute-start(f32[4352]{0:T(1024)S(1)} %pad_maximum_fusion.14), channel_id=1, source_target_pairs={{0,16},{4,20},{16,0},{20,4},{1,17},{5,21},{17,1},{21,5},{2,18},{6,... | collective-permute-start | bytes 52232 | tf_op jit(solution)/shard_map/ppermute | solution.py:451
  (549 shorter events, 263.0 us)
Async XLA Ops:
  11.8 33.7 %collective-permute-start.1 = (bf16[64,2048]{1,0:T(8,128)(2,1)S(1)}, bf16[64,2048]{1,0:T(8,128)(2,1)S(1)}, u32[]{:S(2)}, u32[]{:S(2)}) collective-permute-start(bf16[64,2048]{1,0:T(8,128)(2,1)S(1)} %constant_dynamic-update-slice_fusion.refs_0_), channel_id=1, source_target_pairs={{0,2},{2,0},{4,6},{6,4},{1,3},{3,1},{5,7},{7,5},{8,10},{10,8},{12,... | collective-permute-start | bytes 786440 | tf_op jit(solution)/shard_map/ppermute | solution.py:455
  64.4 45.2 %all-to-all-start = ((bf16[4,256,768]{2,1,0:T(8,128)(2,1)}), bf16[4,256,768]{2,1,0:T(8,128)(2,1)}, u32[]{:S(2)}, u32[]{:S(2)}) async-start(bf16[4,256,768]{2,1,0:T(8,128)(2,1)} %pad_maximum_fusion), calls=%async_computation | async-start | bytes 3145728 | tf_op jit(solution)/shard_map/all_to_all | solution.py:510
  72.0 39.7 %collective-permute-start.15 = (bf16[128,2048]{1,0:T(8,128)(2,1)S(1)}, bf16[128,2048]{1,0:T(8,128)(2,1)}, u32[]{:S(2)}, u32[]{:S(2)}) collective-permute-start(bf16[128,2048]{1,0:T(8,128)(2,1)S(1)} %pad_maximum_fusion.9.refs_8_), channel_id=1, source_target_pairs={{0,2},{2,0},{4,6},{6,4},{1,3},{3,1},{5,7},{7,5},{8,10},{10,8},{12,... | collective-permute-start | bytes 1572872 | tf_op jit(solution)/shard_map/ppermute | solution.py:455
  109.6 59.8 %collective-permute-start.30 = (bf16[1024,768]{1,0:T(8,128)(2,1)}, bf16[1024,768]{1,0:T(8,128)(2,1)}, u32[]{:S(2)}, u32[]{:S(2)}) collective-permute-start(bf16[1024,768]{1,0:T(8,128)(2,1)} %bitcast.31.refs_12_), channel_id=1, source_target_pairs={{0,8},{8,0},{1,9},{9,1},{2,10},{10,2},{3,11},{11,3},{4,12},{12,4},... | collective-permute-start | bytes 4718600 | tf_op jit(solution)/shard_map/ppermute | solution.py:447
  111.7 29.4 %collective-permute-start.17 = (bf16[128,2048]{1,0:T(8,128)(2,1)S(1)}, bf16[128,2048]{1,0:T(8,128)(2,1)}, u32[]{:S(2)}, u32[]{:S(2)}) collective-permute-start(bf16[128,2048]{1,0:T(8,128)(2,1)S(1)} %pad_maximum_fusion.9.refs_8_), channel_id=1, source_target_pairs={{0,6},{2,4},{4,2},{6,0},{1,7},{3,5},{5,3},{7,1},{8,14},{10,12},{12... | collective-permute-start | bytes 1572872 | tf_op jit(solution)/shard_map/ppermute | solution.py:455
  115.6 53.7 %all-to-all-start.1 = ((bf16[4,256,384]{2,1,0:T(8,128)(2,1)}), bf16[4,256,384]{2,1,0:T(8,128)(2,1)}, u32[]{:S(2)}, u32[]{:S(2)}) async-start(bf16[4,256,384]{2,1,0:T(8,128)(2,1)} %pad_maximum_fusion.8), calls=%async_computation.1 | async-start | bytes 1572864 | tf_op jit(solution)/shard_map/all_to_all | solution.py:510
  170.4 61.3 %collective-permute-start.40 = (bf16[1024,768]{1,0:T(8,128)(2,1)}, bf16[1024,768]{1,0:T(8,128)(2,1)S(1)}, u32[]{:S(2)}, u32[]{:S(2)}) collective-permute-start(bf16[1024,768]{1,0:T(8,128)(2,1)} %collective-permute-done.30.refs_13_), channel_id=1, source_target_pairs={{0,1},{1,0},{2,3},{3,2},{4,5},{5,4},{6,7},{7,6},{8,9},{9,8},{10,11... | collective-permute-start | bytes 4718600 | tf_op jit(solution)/shard_map/ppermute | solution.py:447
  170.9 48.1 %collective-permute-start.42 = (bf16[1024,384]{1,0:T(8,128)(2,1)}, bf16[1024,384]{1,0:T(8,128)(2,1)S(1)}, u32[]{:S(2)}, u32[]{:S(2)}) collective-permute-start(bf16[1024,384]{1,0:T(8,128)(2,1)} %bitcast.36.refs_16_.refs_2_), channel_id=1, source_target_pairs={{0,1},{1,0},{2,3},{3,2},{4,5},{5,4},{6,7},{7,6},{8,9},{9,8},{10,11... | collective-permute-start | bytes 2359304 | tf_op jit(solution)/shard_map/ppermute | solution.py:447
  174.5 28.1 %collective-permute-start.41 = (bf16[1024,384]{1,0:T(8,128)(2,1)}, bf16[1024,384]{1,0:T(8,128)(2,1)S(1)}, u32[]{:S(2)}, u32[]{:S(2)}) collective-permute-start(bf16[1024,384]{1,0:T(8,128)(2,1)} %bitcast.36.refs_16_.refs_2_), channel_id=1, source_target_pairs={{0,8},{8,0},{1,9},{9,1},{2,10},{10,2},{3,11},{11,3},{4,12},{12,4},... | collective-permute-start | bytes 2359304 | tf_op jit(solution)/shard_map/ppermute | solution.py:447
  202.6 29.1 %collective-permute-start.43 = (bf16[1024,384]{1,0:T(8,128)(2,1)S(1)}, bf16[1024,384]{1,0:T(8,128)(2,1)S(1)}, u32[]{:S(2)}, u32[]{:S(2)}) collective-permute-start(bf16[1024,384]{1,0:T(8,128)(2,1)S(1)} %collective-permute-done.41.refs_17_.refs_3_), channel_id=1, source_target_pairs={{0,1},{1,0},{2,3},{3,2},{4,5},{5,4},{6,7},{7,6},{8,9},{9,8},{10,11... | collective-permute-start | bytes 2359304 | tf_op jit(solution)/shard_map/ppermute | solution.py:447
  256.1 27.9 %collective-permute-start.52 = (bf16[2048,768]{1,0:T(8,128)(2,1)S(1)}, bf16[2048,768]{1,0:T(8,128)(2,1)S(1)}, u32[]{:S(2)}, u32[]{:S(2)}) collective-permute-start(bf16[2048,768]{1,0:T(8,128)(2,1)S(1)} %convolution_convert_fusion), channel_id=1, source_target_pairs={{0,1},{1,0},{2,3},{3,2},{4,5},{5,4},{6,7},{7,6},{8,9},{9,8},{10,11... | collective-permute-start | bytes 9437192 | tf_op jit(solution)/shard_map/ppermute | solution.py:447
  309.9 35.6 %collective-permute-start.65 = (bf16[1024,768]{1,0:T(8,128)(2,1)S(1)}, bf16[1024,768]{1,0:T(8,128)(2,1)}, u32[]{:S(2)}, u32[]{:S(2)}) collective-permute-start(bf16[1024,768]{1,0:T(8,128)(2,1)S(1)} %slice.422), channel_id=1, source_target_pairs={{0,8},{8,0},{1,9},{9,1},{2,10},{10,2},{3,11},{11,3},{4,12},{12,4},... | collective-permute-start | bytes 4718600 | tf_op jit(solution)/shard_map/ppermute | solution.py:447
  348.5 47.8 %all-to-all-start.2 = ((bf16[4,256,768]{2,1,0:T(8,128)(2,1)}), bf16[4,256,768]{2,1,0:T(8,128)(2,1)}, u32[]{:S(2)}, u32[]{:S(2)}) async-start(bf16[4,256,768]{2,1,0:T(8,128)(2,1)} %bitcast.211), calls=%async_computation.2 | async-start | bytes 3145728 | tf_op jit(solution)/shard_map/all_to_all | solution.py:563
  364.6 29.6 %collective-permute-start.81 = (bf16[2048,256]{1,0:T(8,128)(2,1)S(1)}, bf16[2048,256]{1,0:T(8,128)(2,1)S(1)}, u32[]{:S(2)}, u32[]{:S(2)}) collective-permute-start(bf16[2048,256]{1,0:T(8,128)(2,1)S(1)} %pad_maximum_fusion.5), channel_id=1, source_target_pairs={{0,1},{1,0},{2,3},{3,2},{4,5},{5,4},{6,7},{7,6},{8,9},{9,8},{10,11... | collective-permute-start | bytes 3145736 | tf_op jit(solution)/shard_map/ppermute | solution.py:447
  366.1 30.2 %collective-permute-start.69 = (bf16[2048,256]{1,0:T(8,128)(2,1)S(1)}, bf16[2048,256]{1,0:T(8,128)(2,1)}, u32[]{:S(2)}, u32[]{:S(2)}) collective-permute-start(bf16[2048,256]{1,0:T(8,128)(2,1)S(1)} %convolution_convert_fusion.5), channel_id=1, source_target_pairs={{0,1},{1,0},{2,3},{3,2},{4,5},{5,4},{6,7},{7,6},{8,9},{9,8},{10,11... | collective-permute-start | bytes 3145736 | tf_op jit(solution)/shard_map/ppermute | solution.py:447
  374.9 43.8 %collective-permute-start.60 = (bf16[128,2048]{1,0:T(8,128)(2,1)}, bf16[128,2048]{1,0:T(8,128)(2,1)}, u32[]{:S(2)}, u32[]{:S(2)}) collective-permute-start(bf16[128,2048]{1,0:T(8,128)(2,1)} %get-tuple-element.231), channel_id=1, source_target_pairs={{0,2},{2,0},{4,6},{6,4},{1,3},{3,1},{5,7},{7,5},{8,10},{10,8},{12,... | collective-permute-start | bytes 1572872 | tf_op jit(solution)/shard_map/ppermute | solution.py:455
  385.4 35.9 %collective-permute-start.61 = (bf16[128,2048]{1,0:T(8,128)(2,1)}, bf16[128,2048]{1,0:T(8,128)(2,1)}, u32[]{:S(2)}, u32[]{:S(2)}) collective-permute-start(bf16[128,2048]{1,0:T(8,128)(2,1)} %get-tuple-element.232), channel_id=1, source_target_pairs={{0,4},{2,6},{4,0},{6,2},{1,5},{3,7},{5,1},{7,3},{8,12},{10,14},{12... | collective-permute-start | bytes 1572872 | tf_op jit(solution)/shard_map/ppermute | solution.py:455
  390.6 30.8 %collective-permute-start.62 = (bf16[128,2048]{1,0:T(8,128)(2,1)}, bf16[128,2048]{1,0:T(8,128)(2,1)}, u32[]{:S(2)}, u32[]{:S(2)}) collective-permute-start(bf16[128,2048]{1,0:T(8,128)(2,1)} %get-tuple-element.233), channel_id=1, source_target_pairs={{0,6},{2,4},{4,2},{6,0},{1,7},{3,5},{5,3},{7,1},{8,14},{10,12},{12... | collective-permute-start | bytes 1572872 | tf_op jit(solution)/shard_map/ppermute | solution.py:455
  444.4 61.4 %all-to-all-start.3 = ((bf16[4,256,384]{2,1,0:T(8,128)(2,1)}), bf16[4,256,384]{2,1,0:T(8,128)(2,1)S(1)}, u32[]{:S(2)}, u32[]{:S(2)}) async-start(bf16[4,256,384]{2,1,0:T(8,128)(2,1)} %bitcast.85), calls=%async_computation.3 | async-start | bytes 1572864 | tf_op jit(solution)/shard_map/all_to_all | solution.py:563
  457.8 26.6 %collective-permute-start.85 = (bf16[256,512]{1,0:T(8,128)(2,1)}, bf16[256,512]{1,0:T(8,128)(2,1)S(1)}, u32[]{:S(2)}, u32[]{:S(2)}) collective-permute-start(bf16[256,512]{1,0:T(8,128)(2,1)} %get-tuple-element.321), channel_id=1, source_target_pairs={{4,0},{20,1},{0,4},{16,5},{5,16},{21,17},{1,20},{17,21},{6,2},{22,... | collective-permute-start | bytes 786440 | tf_op jit(solution)/shard_map/ppermute | solution.py:544
  459.2 29.1 %collective-permute-start.86 = (bf16[256,512]{1,0:T(8,128)(2,1)}, bf16[256,512]{1,0:T(8,128)(2,1)S(1)}, u32[]{:S(2)}, u32[]{:S(2)}) collective-permute-start(bf16[256,512]{1,0:T(8,128)(2,1)} %get-tuple-element.320), channel_id=1, source_target_pairs={{5,0},{21,1},{1,4},{17,5},{4,16},{20,17},{0,20},{16,21},{7,2},{23,... | collective-permute-start | bytes 786440 | tf_op jit(solution)/shard_map/ppermute | solution.py:544
  461.6 28.8 %collective-permute-start.74 = (bf16[64,2048]{1,0:T(8,128)(2,1)S(1)}, bf16[64,2048]{1,0:T(8,128)(2,1)S(1)}, u32[]{:S(2)}, u32[]{:S(2)}) collective-permute-start(bf16[64,2048]{1,0:T(8,128)(2,1)S(1)} %copy-done.52), channel_id=1, source_target_pairs={{0,2},{2,0},{1,3},{3,1},{4,6},{6,4},{5,7},{7,5},{8,10},{10,8},{9,1... | collective-permute-start | bytes 786440 | tf_op jit(solution)/shard_map/ppermute | solution.py:447
  463.2 29.4 %collective-permute-start.87 = (f32[4352]{0:T(1024)S(1)}, f32[4352]{0:T(1024)S(1)}, u32[]{:S(2)}, u32[]{:S(2)}) collective-permute-start(f32[4352]{0:T(1024)S(1)} %pad_maximum_fusion.14), channel_id=1, source_target_pairs={{0,4},{4,0},{16,20},{20,16},{1,5},{5,1},{17,21},{21,17},{2,6},{6,2... | collective-permute-start | bytes 52232 | tf_op jit(solution)/shard_map/ppermute | solution.py:451
  464.7 27.8 %collective-permute-start.88 = (f32[4352]{0:T(1024)S(1)}, f32[4352]{0:T(1024)S(1)}, u32[]{:S(2)}, u32[]{:S(2)}) collective-permute-start(f32[4352]{0:T(1024)S(1)} %pad_maximum_fusion.14), channel_id=1, source_target_pairs={{0,16},{4,20},{16,0},{20,4},{1,17},{5,21},{17,1},{21,5},{2,18},{6,... | collective-permute-start | bytes 52232 | tf_op jit(solution)/shard_map/ppermute | solution.py:451
  (173 other events, 2096.6 us)
